TPU v7x, 32 devices: a whole 2x2x4 slice. The times are simulated.
32 devices in a mesh: row: 4 (over z), col: 8 (over y, x, core).
Axes of the slice: x: 2, y: 2, z: 4, core: 2. Of those that a mesh axis runs over, the one named last changes fastest.
Arguments:
- hidden_in: bfloat16 [8192, 2048], P('row', 'col'), may hold values from -6 to 6
- seg_ids: int32 [8192], P('row'), may hold values from 0 to 15, never falling along the last dimension, each value on 1 to 2000 neighbouring positions
- cotangent: bfloat16 [8192, 2048], P('row', 'col'), may hold values from -6 to 6
- norm_mixer: float32 [2048], P('col'), may hold values from 0.5 to 1.5
- w_query: bfloat16 [2048, 2048], P('row', 'col'), may hold values from -0.125 to 0.125
- w_key: bfloat16 [2048, 2048], P('row', 'col'), may hold values from -0.125 to 0.125
- w_value: bfloat16 [2048, 4096], P('row', 'col'), may hold values from -0.125 to 0.125
- w_gate: bfloat16 [2048, 4096], P('row', 'col'), may hold values from -0.125 to 0.125
- w_beta: bfloat16 [2048, 16], P('row', 'col'), may hold values from -0.125 to 0.125
- w_decay: bfloat16 [2048, 16], P('row', 'col'), may hold values from -0.125 to 0.125
- decay_log: float32 [16], P('col'), may hold values from -6.5 to -3
- conv_query: float32 [4, 2048], P(None, 'col'), may hold values from -3 to 3
- conv_key: float32 [4, 2048], P(None, 'col'), may hold values from -3 to 3
- conv_value: float32 [4, 4096], P(None, 'col'), may hold values from -3 to 3
- norm_gated: float32 [4096], P('col'), may hold values from 0.5 to 1.5
- w_out: bfloat16 [4096, 2048], P('col', 'row'), may hold values from -0.1875 to 0.1875
- norm_ffn: float32 [2048], P('col'), may hold values from 0.5 to 1.5
- w_ffn_gate: bfloat16 [2048, 5632], P('row', 'col'), may hold values from -0.125 to 0.125
- w_ffn_up: bfloat16 [2048, 5632], P('row', 'col'), may hold values from -0.125 to 0.125
- w_ffn_down: bfloat16 [5632, 2048], P('col', 'row'), may hold values from -0.078125 to 0.078125
Outputs:
- block_out: bfloat16 [8192, 2048], P('row', 'col')
- grad_input: float32 [8192, 2048], P('row', 'col')
- grad_norm_mixer: float32 [2048], P('col')
- grad_w_query: float32 [2048, 2048], P('row', 'col')
- grad_w_key: float32 [2048, 2048], P('row', 'col')
- grad_w_value: float32 [2048, 4096], P('row', 'col')
- grad_w_gate: float32 [2048, 4096], P('row', 'col')
- grad_w_beta: float32 [2048, 16], P('row', 'col')
- grad_w_decay: float32 [2048, 16], P('row', 'col')
- grad_decay_log: float32 [16], P('col')
- grad_conv_query: float32 [4, 2048], P(None, 'col')
- grad_conv_key: float32 [4, 2048], P(None, 'col')
- grad_conv_value: float32 [4, 4096], P(None, 'col')
- grad_norm_gated: float32 [4096], P('col')
- grad_w_out: float32 [4096, 2048], P('col', 'row')
- grad_norm_ffn: float32 [2048], P('col')
- grad_w_ffn_gate: float32 [2048, 5632], P('row', 'col')
- grad_w_ffn_up: float32 [2048, 5632], P('row', 'col')
- grad_w_ffn_down: float32 [5632, 2048], P('col', 'row')
Inputs may be any that keep to these rules, and one draw needn't show every extreme that they name: `seg_ids`: document ids of the tokens, never falling; a document holds 1 to 2000 tokens and one holds exactly 2000.
All inputs are finite; a program needn't handle non-finite values.
Results may differ from a plain program's by a relative error of at most 0.02.
Values may be sent and summed in bfloat16 or wider, within the bound.
A program may use at most 384 MiB of HBM per device.

v0:
```python
import jax
import jax.numpy as jnp
from jax import lax
from jax.sharding import PartitionSpec as P

D = 2048
DK = 128
DV = 256
CONV = 4
BLOCK = 64
SEQ = 1024


EPSILON = 1e-06
TOP_PRECISION = lax.Precision.HIGHEST


def low_value(values):
    return lax.optimization_barrier(values.astype(jnp.bfloat16)).astype(jnp.float32)


def shifted(values, offset):
    if offset == 0:
        return values
    filler = jnp.zeros((offset,) + values.shape[1:], values.dtype)
    return jnp.concatenate([filler, values[: values.shape[0] - offset]], axis=0)


def tap_masks(seg_ids):
    position = jnp.arange(seg_ids.shape[0], dtype=jnp.int32) % SEQ
    return [
        ((seg_ids == shifted(seg_ids, offset)) & (position >= offset)).astype(jnp.float32)
        for offset in range(CONV)
    ]


def short_conv(values, tap_weights, taps_valid):
    summed = jnp.zeros_like(values)
    for offset in range(CONV):
        summed = (
            summed + tap_weights[offset] * shifted(values, offset) * taps_valid[offset][:, None]
        )
    return jax.nn.silu(summed)


def unit_heads(values):
    shaped = values.reshape(values.shape[0], -1, DK)
    shaped = shaped * lax.rsqrt(jnp.sum(shaped * shaped, axis=-1, keepdims=True) + EPSILON)
    return shaped.reshape(values.shape)


def rows_product(first_op, second_op):
    return lax.dot_general(
        first_op, second_op, (((0,), (0,)), ((), ())), preferred_element_type=jnp.float32
    )


def cols_product(first_op, second_op):
    return lax.dot_general(
        first_op, second_op, (((1,), (1,)), ((), ())), preferred_element_type=jnp.float32
    )


def shard_norm(values, gains):
    squares = lax.psum(jnp.sum(values * values, axis=1), "col")
    scales = lax.rsqrt(squares / D + EPSILON)
    return (scales, values * scales[:, None] * gains)


def shard_norm_back(values, gains, scales, grad_out):
    weighted = grad_out * gains
    totals = lax.psum(jnp.sum(weighted * values, axis=1), "col")
    grad_values = (
        scales[:, None] * weighted - values * (scales * scales * scales * totals / D)[:, None]
    )
    grad_gains = jnp.sum(grad_out * values * scales[:, None], axis=0)
    return (grad_values, grad_gains)


def full_rows(values):
    return lax.all_gather(values, "col", axis=1, tiled=True)


def full_grads(values):
    return lax.all_gather(values, "col", axis=1, tiled=True)


def sum_columns(term):
    return lax.psum_scatter(
        term.astype(jnp.bfloat16), "col", scatter_dimension=1, tiled=True
    ).astype(jnp.float32)


def sum_grad_columns(term):
    return lax.psum_scatter(
        term.astype(jnp.bfloat16), "col", scatter_dimension=1, tiled=True
    ).astype(jnp.float32)


def block_delta(queries, key_rows, values, strength, log_decay, resets):
    row_count = queries.shape[0]
    head_count = strength.shape[1]
    block_count = row_count // BLOCK
    query_blk = queries.reshape(block_count, BLOCK, head_count, DK)
    key_blk = key_rows.reshape(block_count, BLOCK, head_count, DK)
    value_blk = values.reshape(block_count, BLOCK, head_count, DV)
    beta_blk = strength.reshape(block_count, BLOCK, head_count)
    decay_sum = jnp.cumsum(log_decay.reshape(block_count, BLOCK, head_count), axis=1)
    breaks = jnp.cumsum(resets.reshape(block_count, BLOCK), axis=1)
    lower_mask = jnp.tril(jnp.ones((BLOCK, BLOCK), jnp.float32))
    strict_mask = lower_mask - jnp.eye(BLOCK, dtype=jnp.float32)
    same_part = (breaks[:, :, None] == breaks[:, None, :]).astype(jnp.float32)
    spread = jnp.minimum(decay_sum[:, :, None, :] - decay_sum[:, None, :, :], 0.0)
    between = jnp.exp(spread) * (same_part * lower_mask)[:, :, :, None]
    from_start = jnp.exp(decay_sum) * (breaks == 0).astype(jnp.float32)[:, :, None]
    key_key = jnp.einsum("nchk,nshk->ncsh", key_blk, key_blk, precision=TOP_PRECISION)
    coupling = beta_blk[:, :, None, :] * between * key_key * strict_mask[None, :, :, None]
    system = jnp.eye(BLOCK, dtype=jnp.float32) + jnp.transpose(coupling, (0, 3, 1, 2))
    right_side = jnp.concatenate(
        [(beta_blk * from_start)[..., None] * key_blk, beta_blk[..., None] * value_blk], axis=-1
    )
    solved = jax.scipy.linalg.solve_triangular(
        system, jnp.transpose(right_side, (0, 2, 1, 3)), lower=True, unit_diagonal=True
    )
    weight_part = solved[..., :DK]
    update_part = solved[..., DK:]
    scores = jnp.einsum(
        "nchk,nshk->nhcs", query_blk, key_blk, precision=TOP_PRECISION
    ) * jnp.transpose(between, (0, 3, 1, 2))
    query_start = jnp.transpose(from_start[..., None] * query_blk, (0, 2, 1, 3))
    key_end = jnp.transpose(between[:, BLOCK - 1][..., None] * key_blk, (0, 2, 1, 3))
    end_decay = from_start[:, BLOCK - 1]

    def advance(carried_state, block_in):
        current_weight, current_update, score_now, current_query, current_key, decay_now = block_in
        prediction_error = current_update - jnp.einsum(
            "mwn,mny->mwy", current_weight, carried_state, precision=TOP_PRECISION
        )
        output_rows = jnp.einsum(
            "mwn,mny->mwy", current_query, carried_state, precision=TOP_PRECISION
        ) + jnp.einsum("hcs,hsv->hcv", score_now, prediction_error, precision=TOP_PRECISION)
        carried_state = decay_now[:, None, None] * carried_state + jnp.einsum(
            "dyc,dya->dca", current_key, prediction_error, precision=TOP_PRECISION
        )
        return (carried_state, output_rows)

    initial = jnp.zeros((head_count, DK, DV), jnp.float32)
    _, output_rows = lax.scan(
        jax.checkpoint(advance),
        initial,
        (weight_part, update_part, scores, query_start, key_end, end_decay),
    )
    return (jnp.transpose(output_rows, (0, 2, 1, 3)) * DK ** (-0.5)).reshape(
        row_count, head_count * DV
    )


def gated_norm(mixed_out, gains, proj_gate):
    row_count = mixed_out.shape[0]
    head_count = gains.shape[0] // DV
    shaped = mixed_out.reshape(row_count, head_count, DV)
    shaped = shaped * lax.rsqrt(jnp.mean(shaped * shaped, axis=-1, keepdims=True) + EPSILON)
    shaped = (
        shaped
        * gains.reshape(head_count, DV)
        * jax.nn.silu(proj_gate).reshape(row_count, head_count, DV)
    )
    return shaped.reshape(row_count, head_count * DV)


def on_device(
    hidden_in,
    seg_ids,
    cotangent,
    norm_mixer,
    w_query,
    w_key,
    w_value,
    w_gate,
    w_beta,
    w_decay,
    decay_log,
    conv_query,
    conv_key,
    conv_value,
    norm_gated,
    w_out,
    norm_ffn,
    w_ffn_gate,
    w_ffn_up,
    w_ffn_down,
):
    taps_valid = tap_masks(seg_ids)
    resets = 1.0 - taps_valid[1]

    def conv_part(proj_query, proj_key, proj_value, taps_query, taps_key, taps_value):
        return (
            unit_heads(short_conv(proj_query, taps_query, taps_valid)),
            unit_heads(short_conv(proj_key, taps_key, taps_valid)),
            short_conv(proj_value, taps_value, taps_valid),
        )

    def mixer_part(queries, key_rows, values, proj_gate, proj_beta, proj_decay, rates, gains):
        strength = jax.nn.sigmoid(proj_beta)
        log_decay = -jnp.exp(rates) * jax.nn.softplus(proj_decay)
        mixed_out = block_delta(queries, key_rows, values, strength, log_decay, resets)
        return gated_norm(mixed_out, gains, proj_gate)

    in_full = (
        lax.all_gather(w_query, "row", axis=0, tiled=True),
        lax.all_gather(w_key, "row", axis=0, tiled=True),
        lax.all_gather(w_value, "row", axis=0, tiled=True),
        lax.all_gather(w_gate, "row", axis=0, tiled=True),
        lax.all_gather(w_beta, "row", axis=0, tiled=True),
        lax.all_gather(w_decay, "row", axis=0, tiled=True),
        lax.all_gather(w_ffn_gate, "row", axis=0, tiled=True),
        lax.all_gather(w_ffn_up, "row", axis=0, tiled=True),
    )
    out_full = (
        lax.all_gather(w_out, "row", axis=1, tiled=True),
        lax.all_gather(w_ffn_down, "row", axis=1, tiled=True),
    )
    hidden = hidden_in.astype(jnp.float32)
    scale_mixer, normed_shard = shard_norm(hidden, norm_mixer)
    normed = full_rows(normed_shard.astype(jnp.bfloat16))
    projected = [
        jnp.dot(normed, weight, preferred_element_type=jnp.float32) for weight in in_full[:6]
    ]
    conv_outs, conv_pull = jax.vjp(
        conv_part, projected[0], projected[1], projected[2], conv_query, conv_key, conv_value
    )
    gated_f32, mixer_pull = jax.vjp(
        mixer_part,
        low_value(conv_outs[0]),
        low_value(conv_outs[1]),
        low_value(conv_outs[2]),
        projected[3],
        projected[4],
        projected[5],
        decay_log,
        norm_gated,
    )
    gated = gated_f32.astype(jnp.bfloat16)
    mixer_term = jnp.dot(gated, out_full[0], preferred_element_type=jnp.float32)
    middle = hidden + sum_columns(mixer_term)
    scale_ffn, normed_mid = shard_norm(middle, norm_ffn)
    normed_ffn = full_rows(normed_mid.astype(jnp.bfloat16))
    gate_pre = jnp.dot(normed_ffn, in_full[6], preferred_element_type=jnp.float32)
    up_pre = jnp.dot(normed_ffn, in_full[7], preferred_element_type=jnp.float32)
    inner_act = (jax.nn.silu(gate_pre) * up_pre).astype(jnp.bfloat16)
    block_out = (
        middle + sum_columns(jnp.dot(inner_act, out_full[1], preferred_element_type=jnp.float32))
    ).astype(jnp.bfloat16)
    back_in = (
        lax.all_gather(w_query, "row", axis=0, tiled=True),
        lax.all_gather(w_key, "row", axis=0, tiled=True),
        lax.all_gather(w_value, "row", axis=0, tiled=True),
        lax.all_gather(w_gate, "row", axis=0, tiled=True),
        lax.all_gather(w_beta, "row", axis=0, tiled=True),
        lax.all_gather(w_decay, "row", axis=0, tiled=True),
        lax.all_gather(w_ffn_gate, "row", axis=0, tiled=True),
        lax.all_gather(w_ffn_up, "row", axis=0, tiled=True),
    )
    back_out = (
        lax.all_gather(w_out, "row", axis=1, tiled=True),
        lax.all_gather(w_ffn_down, "row", axis=1, tiled=True),
    )
    grad_top = full_grads(cotangent)
    grad_inner = cols_product(grad_top, back_out[1])
    sig_gate = jax.nn.sigmoid(gate_pre)
    grad_gate = (grad_inner * up_pre * sig_gate * (1.0 + gate_pre * (1.0 - sig_gate))).astype(
        jnp.bfloat16
    )
    grad_up = (grad_inner * gate_pre * sig_gate).astype(jnp.bfloat16)
    grad_normed_ffn = sum_grad_columns(
        cols_product(grad_gate, back_in[6]) + cols_product(grad_up, back_in[7])
    )
    grad_from_ffn, grad_norm_ffn_part = shard_norm_back(
        middle, norm_ffn, scale_ffn, grad_normed_ffn
    )
    grad_middle = cotangent.astype(jnp.float32) + grad_from_ffn
    grad_mid_full = full_grads(grad_middle.astype(jnp.bfloat16))
    grad_gated = cols_product(grad_mid_full, back_out[0])
    mixer_grads = mixer_pull(grad_gated)
    conv_grads = conv_pull((mixer_grads[0], mixer_grads[1], mixer_grads[2]))
    grad_proj = [
        member.astype(jnp.bfloat16)
        for member in (
            conv_grads[0],
            conv_grads[1],
            conv_grads[2],
            mixer_grads[3],
            mixer_grads[4],
            mixer_grads[5],
        )
    ]
    grad_normed_term = cols_product(grad_proj[0], back_in[0])
    for position in range(1, 6):
        grad_normed_term = grad_normed_term + cols_product(grad_proj[position], back_in[position])
    grad_normed = sum_grad_columns(grad_normed_term)
    grad_from_mixer, grad_norm_mixer_part = shard_norm_back(
        hidden, norm_mixer, scale_mixer, grad_normed
    )
    grad_input = grad_middle + grad_from_mixer
    in_grads = (
        lax.psum_scatter(
            rows_product(normed, grad_proj[0]).astype(jnp.bfloat16),
            "row",
            scatter_dimension=0,
            tiled=True,
        ).astype(jnp.float32),
        lax.psum_scatter(
            rows_product(normed, grad_proj[1]).astype(jnp.bfloat16),
            "row",
            scatter_dimension=0,
            tiled=True,
        ).astype(jnp.float32),
        lax.psum_scatter(
            rows_product(normed, grad_proj[2]).astype(jnp.bfloat16),
            "row",
            scatter_dimension=0,
            tiled=True,
        ).astype(jnp.float32),
        lax.psum_scatter(
            rows_product(normed, grad_proj[3]).astype(jnp.bfloat16),
            "row",
            scatter_dimension=0,
            tiled=True,
        ).astype(jnp.float32),
        lax.psum_scatter(
            rows_product(normed, grad_proj[4]).astype(jnp.bfloat16),
            "row",
            scatter_dimension=0,
            tiled=True,
        ).astype(jnp.float32),
        lax.psum_scatter(
            rows_product(normed, grad_proj[5]).astype(jnp.bfloat16),
            "row",
            scatter_dimension=0,
            tiled=True,
        ).astype(jnp.float32),
        lax.psum_scatter(
            rows_product(normed_ffn, grad_gate).astype(jnp.bfloat16),
            "row",
            scatter_dimension=0,
            tiled=True,
        ).astype(jnp.float32),
        lax.psum_scatter(
            rows_product(normed_ffn, grad_up).astype(jnp.bfloat16),
            "row",
            scatter_dimension=0,
            tiled=True,
        ).astype(jnp.float32),
    )
    out_grads = (
        lax.psum_scatter(
            rows_product(gated, grad_mid_full).astype(jnp.bfloat16),
            "row",
            scatter_dimension=1,
            tiled=True,
        ).astype(jnp.float32),
        lax.psum_scatter(
            rows_product(inner_act, grad_top).astype(jnp.bfloat16),
            "row",
            scatter_dimension=1,
            tiled=True,
        ).astype(jnp.float32),
    )
    small = lax.psum(
        (
            grad_norm_mixer_part,
            grad_norm_ffn_part,
            mixer_grads[6],
            conv_grads[3],
            conv_grads[4],
            conv_grads[5],
            mixer_grads[7],
        ),
        "row",
    )
    return (
        block_out,
        grad_input,
        small[0],
        in_grads[0],
        in_grads[1],
        in_grads[2],
        in_grads[3],
        in_grads[4],
        in_grads[5],
        small[2],
        small[3],
        small[4],
        small[5],
        small[6],
        out_grads[0],
        small[1],
        in_grads[6],
        in_grads[7],
        out_grads[1],
    )


def solution(mesh):
    placed = (
        P("row", "col"),
        P("row"),
        P("row", "col"),
        P("col"),
        P("row", "col"),
        P("row", "col"),
        P("row", "col"),
        P("row", "col"),
        P("row", "col"),
        P("row", "col"),
        P("col"),
        P(None, "col"),
        P(None, "col"),
        P(None, "col"),
        P("col"),
        P("col", "row"),
        P("col"),
        P("row", "col"),
        P("row", "col"),
        P("col", "row"),
    )
    return jax.shard_map(
        on_device,
        mesh=mesh,
        in_specs=placed,
        out_specs=(
            P("row", "col"),
            P("row", "col"),
            P("col"),
            P("row", "col"),
            P("row", "col"),
            P("row", "col"),
            P("row", "col"),
            P("row", "col"),
            P("row", "col"),
            P("col"),
            P(None, "col"),
            P(None, "col"),
            P(None, "col"),
            P("col"),
            P("col", "row"),
            P("col"),
            P("row", "col"),
            P("row", "col"),
            P("col", "row"),
        ),
        check_vma=False,
    )
```

profile of v0, /device:TPU:0, one launch (start us, length us, event | category | flops | bytes accessed | tf_op | source)
XLA Modules:
  0.0 2170.2 jit_solution(10188422451352466657)
XLA Ops:
  8.8 15.5 psum.77
  34.4 12.1 all_gather.55
  46.5 11.9 all_gather.53
  62.5 20.5 all-gather.13.cloned.1.call-done
  168.9 8.5 fusion.60
  177.5 134.0 %custom-call.10 = f32[32,2,1,64,64]{0,3,4,2,1:T(8,128)} custom-call(f32[32,2,1,64,64]{0,4,3,2,1:T(8,128)} %get-tuple-element.753), custom_call_target="InvertDiagBlocksLowerTriangular" | custom-call | tf_op jit(solution)/shard_map/jvp(jit(_solve_triangular))/vmap(vmap())/triangular_solve | solution.py:122
  316.0 8.3 fusion.157
  359.7 190.9 %while.42 = (s32[]{:T(128)}, f32[2,128,256]{2,1,0:T(8,128)S(1)}, f32[32,2,64,256]{3,2,1,0:T(8,128)}, f32[32,2,128,256]{3,2,1,0:T(8,128)}, f32[32,2]{1,0:T(8,128)...) while((s32[]{:T(128)}, f32[2,128,256]{2,1,0:T(8,128)S(1)}, ...), condition=%wide.region_7.8_spmd.clone, body=%wide.region_6.7_spmd.clone.sunk | while | flops 176619520 | bytes 2755249 | solution.py:148
  565.3 14.1 multiply_convert_fusion.3
  579.4 9.0 convolution_convert_fusion.1
  589.3 70.1 %reduce-scatter.19.cloned.1.call-done = bf16[2048,256]{1,0:T(8,128)(2,1)} async-done(((bf16[2048,2048]{1,0:T(8,128)(2,1)}), bf16[2048,256]{1,0:T(8,128)(2,1)}) %reduce-scatter.19.cloned.1.call-update) | async-done | bytes 1048592 | tf_op jit(solution)/shard_map/reduce_scatter | solution.py:89
  661.1 13.0 psum.78
  677.5 42.7 %all-gather.29.cloned.1.call-done = bf16[2048,704]{0,1:T(8,128)(2,1)} async-done(((bf16[512,704]{0,1:T(8,128)(2,1)}), bf16[2048,704]{0,1:T(8,128)(2,1)}) %all-gather.29.cloned.1.call-update) | async-done | bytes 2883600 | tf_op jit(solution)/shard_map/all_gather | solution.py:217
  720.2 57.3 %all-gather.25.cloned.1.call-done = bf16[2048,2048]{1,0:T(8,128)(2,1)} async-done(((bf16[2048,256]{1,0:T(8,128)(2,1)}), bf16[2048,2048]{1,0:T(8,128)(2,1)}) %all-gather.25.cloned.1.call-update) | async-done | bytes 8388624 | tf_op jit(solution)/shard_map/all_gather | solution.py:81
  777.5 11.0 fusion.161
  788.5 49.7 %all-gather.27.cloned.1.call-done = bf16[2048,704]{0,1:T(8,128)(2,1)} async-done(((bf16[512,704]{0,1:T(8,128)(2,1)}), bf16[2048,704]{0,1:T(8,128)(2,1)}) %all-gather.27.cloned.1.call-update) | async-done | bytes 2883600 | tf_op jit(solution)/shard_map/all_gather | solution.py:216
  838.2 11.0 fusion.160
  849.2 48.6 %all-gather.31.cloned.1.call-done = bf16[704,2048]{1,0:T(8,128)(2,1)} async-done(((bf16[704,512]{1,0:T(8,128)(2,1)}), bf16[704,2048]{1,0:T(8,128)(2,1)}) %all-gather.31.cloned.1.call-update) | async-done | bytes 2883600 | tf_op jit(solution)/shard_map/all_gather | solution.py:221
  897.7 56.6 %all-gather.33.cloned.1.call-done = bf16[2048,2048]{1,0:T(8,128)(2,1)} async-done(((bf16[2048,256]{1,0:T(8,128)(2,1)}), bf16[2048,2048]{1,0:T(8,128)(2,1)}) %all-gather.33.cloned.1.call-update) | async-done | bytes 8388624 | tf_op jit(solution)/shard_map/all_gather | solution.py:85
  954.3 15.2 multiply_convert_fusion
  969.6 10.5 fusion.162
  980.1 12.6 add_convert_fusion.1
  992.8 71.4 %reduce-scatter.23.cloned.1.call-done = bf16[2048,256]{1,0:T(8,128)(2,1)} async-done(((bf16[2048,2048]{1,0:T(8,128)(2,1)}), bf16[2048,256]{1,0:T(8,128)(2,1)}) %reduce-scatter.23.cloned.1.call-update) | async-done | bytes 1048592 | tf_op jit(solution)/shard_map/reduce_scatter | solution.py:95
  1067.0 12.9 psum.79
  1082.8 10.6 convolution_convert_fusion.4
  1095.2 11.0 convolution_convert_fusion.2
  1123.0 11.0 convolution_convert_fusion.3
  1138.8 14.8 fusion.42
  1178.0 431.2 %while.43 = (s32[]{:T(128)}, f32[2,128,256]{2,1,0:T(8,128)S(1)}, f32[32,2,64,128]{3,2,1,0:T(8,128)}, f32[32,2,64,256]{3,2,1,0:T(8,128)}, f32[32,2,64,64]{3,2,1,0...) while((s32[]{:T(128)}, f32[2,128,256]{2,1,0:T(8,128)S(1)}, ...), condition=%wide.region_19.20_spmd.clone, body=%wide.region_17.19_spmd.clone.sunk | while | flops 403177472 | bytes 7307623 | solution.py:148
  1616.5 10.7 fusion.34
  1645.4 8.3 fusion.61
  1662.6 9.6 multiply_reduce_fusion.5
  1677.7 8.4 fusion.50
  1726.3 6.9 fusion.154
  1776.9 7.7 multiply_reduce_fusion.9
  1785.6 6.9 convolution_convert_fusion.9
  1848.0 8.1 fusion.168
  1856.2 8.3 fusion.139
  1870.3 12.9 fusion.167
  1883.2 8.4 fusion.166
  1891.6 8.3 fusion.163
  1899.9 31.4 %add_convert_fusion = bf16[2048,2048]{1,0:T(8,128)(2,1)} fusion(f32[2048,2048]{1,0:T(8,128)} %fusion.139, f32[2048,2048]{1,0:T(8,128)} %fusion.168, f32[2048,2048]{1,0:T(8,128)} %fusion.167, f32[2048,2048]{1,0:T(8,128)} %fusion.166, f32[2048,2048]{1,0:T(8,128)} %fusion.163, bf16[2048,256]{0,1:T(8,128)(2,1)S(1)} %get-tuple-element.755, ...), kind=kOutput, calls=%fused_computation.55 | convolution fusion | flops 2172649472 | bytes 94371840 | tf_op jit(solution)/shard_map/dot_general | solution.py:59
  1933.2 10.9 convolution_convert_fusion
  1965.3 43.8 %reduce-scatter.31.cloned.1.call-done = bf16[512,512]{1,0:T(8,128)(2,1)} async-done(((bf16[2048,512]{1,0:T(8,128)(2,1)}), bf16[512,512]{1,0:T(8,128)(2,1)}) %reduce-scatter.31.cloned.1.call-update) | async-done | bytes 524304 | tf_op jit(solution)/shard_map/reduce_scatter | solution.py:318
  2011.2 72.4 %reduce-scatter.25.cloned.1.call-done = bf16[2048,256]{1,0:T(8,128)(2,1)} async-done(((bf16[2048,2048]{1,0:T(8,128)(2,1)}), bf16[2048,256]{1,0:T(8,128)(2,1)}) %reduce-scatter.25.cloned.1.call-update) | async-done | bytes 1048592 | tf_op jit(solution)/shard_map/reduce_scatter | solution.py:95
  2085.8 19.5 all-reduce.36
  2105.4 12.3 psum.80
  2117.7 40.5 %reduce-scatter.21.cloned.1.call-done = bf16[2048,256]{1,0:T(8,128)(2,1)} async-done(((bf16[2048,2048]{1,0:T(8,128)(2,1)}), bf16[2048,256]{1,0:T(8,128)(2,1)}) %reduce-scatter.21.cloned.1.call-update) | async-done | bytes 1048592 | tf_op jit(solution)/shard_map/reduce_scatter | solution.py:89
  (1449 shorter events, 1051.0 us)
Async XLA Ops:
  7.2 75.8 %all-gather.13.cloned.1.call-start = ((), (), s32[]{:S(2)}) async-start(), calls=%async_computation.14 | async-start | bytes 9437184 | tf_op jit(solution)/shard_map/all_gather | solution.py:81
  27.5 30.9 %copy-start.143 = (f32[4,512]{1,0:T(4,128)S(1)}, f32[4,512]{1,0:T(4,128)}, u32[]{:S(2)}) copy-start(f32[4,512]{1,0:T(4,128)} %param.37) | copy-start | bytes 24580
  27.5 85.0 %all-gather.15.cloned.1.call-start = ((), (), s32[]{:S(2)}) async-start(), calls=%async_computation.15 | async-start | bytes 1310720 | tf_op jit(solution)/shard_map/all_gather | solution.py:211
  28.3 113.3 %all-gather.19.cloned.1.call-start = ((), (), s32[]{:S(2)}) async-start(), calls=%async_computation.17 | async-start | bytes 1310720 | tf_op jit(solution)/shard_map/all_gather | solution.py:210
  29.0 287.0 %all-gather.17.cloned.1.call-start = ((), (), s32[]{:S(2)}) async-start(), calls=%async_computation.16 | async-start | bytes 2621440 | tf_op jit(solution)/shard_map/all_gather | solution.py:212
  29.6 535.7 %all-gather.21.cloned.1.call-start = ((), (), s32[]{:S(2)}) async-start(), calls=%async_computation.18 | async-start | bytes 2621440 | tf_op jit(solution)/shard_map/all_gather | solution.py:213
  30.2 549.3 %all-gather.23.cloned.1.call-start = ((), (), s32[]{:S(2)}) async-start(), calls=%async_computation.19 | async-start | bytes 2621440 | tf_op jit(solution)/shard_map/all_gather | solution.py:220
  30.7 628.6 %reduce-scatter.19.cloned.1.call-start = ((), (), s32[]{:S(2)}) async-start(), calls=%async_computation.20 | async-start | bytes 9437184 | tf_op jit(solution)/shard_map/reduce_scatter | solution.py:89
  30.9 293.4 %copy-start.60 = (f32[2048]{0:T(1024)}, f32[2048]{0:T(1024)S(1)}, u32[]{:S(2)}) copy-start(f32[2048]{0:T(1024)S(1)} %get-tuple-element.730) | copy-start | bytes 24580
  33.2 49.8 %copy-start.113 = (f32[2]{0:T(128)}, f32[2]{0:T(128)S(1)}, u32[]{:S(2)}) copy-start(f32[2]{0:T(128)S(1)} %exponential_negate_fusion) | copy-start | bytes 28
  60.4 263.9 %copy-start.62 = (f32[2048]{0:T(1024)}, f32[2048]{0:T(1024)S(1)}, u32[]{:S(2)}) copy-start(f32[2048]{0:T(1024)S(1)} %get-tuple-element.784) | copy-start | bytes 24580
  62.5 106.4 %copy-start.13 = (f32[32,64,64]{0,2,1:T(8,128)}, f32[32,64,64]{0,2,1:T(8,128)S(1)}, u32[]{:S(2)}) copy-start(f32[32,64,64]{0,2,1:T(8,128)S(1)} %get-tuple-element.767) | copy-start | bytes 1572868
  105.2 63.7 %copy-start.49 = (f32[32,2,64]{0,2,1:T(8,128)}, f32[32,2,64]{0,2,1:T(8,128)S(1)}, u32[]{:S(2)}) copy-start(f32[32,2,64]{0,2,1:T(8,128)S(1)} %copy.340) | copy-start | bytes 49156
  130.0 205.7 %copy-start.7 = (bf16[32,64,2,128]{3,1,2,0:T(8,128)(2,1)}, bf16[32,64,2,128]{3,1,2,0:T(8,128)(2,1)S(1)}, u32[]{:S(2)}) copy-start(bf16[32,64,2,128]{3,1,2,0:T(8,128)(2,1)S(1)} %copy.338) | copy-start | bytes 3145732
  588.4 71.0 %copy-start.10 = (bf16[2048,256]{1,0:T(8,128)(2,1)S(1)}, bf16[2048,256]{1,0:T(8,128)(2,1)}, u32[]{:S(2)}) copy-start(bf16[2048,256]{1,0:T(8,128)(2,1)} %param.24) | copy-start | bytes 3145732
  588.4 85.7 %copy-start.123 = (f32[256]{0:T(256)S(1)}, f32[256]{0:T(256)}, u32[]{:S(2)}) copy-start(f32[256]{0:T(256)} %param.40) | copy-start | bytes 3076
  588.5 131.7 %all-gather.29.cloned.1.call-start = ((), (), s32[]{:S(2)}) async-start(), calls=%async_computation.23 | async-start | bytes 3604480 | tf_op jit(solution)/shard_map/all_gather | solution.py:217
  589.2 188.3 %all-gather.25.cloned.1.call-start = ((), (), s32[]{:S(2)}) async-start(), calls=%async_computation.21 | async-start | bytes 9437184 | tf_op jit(solution)/shard_map/all_gather | solution.py:81
  674.1 405.8 %copy-start.85 = (f32[2048]{0:T(1024)}, f32[2048]{0:T(1024)S(1)}, u32[]{:S(2)}) copy-start(f32[2048]{0:T(1024)S(1)} %add_rsqrt_fusion.2) | copy-start | bytes 24580
  675.5 162.6 %all-gather.27.cloned.1.call-start = ((), (), s32[]{:S(2)}) async-start(), calls=%async_computation.22 | async-start | bytes 3604480 | tf_op jit(solution)/shard_map/all_gather | solution.py:216
  676.1 221.6 %all-gather.31.cloned.1.call-start = ((), (), s32[]{:S(2)}) async-start(), calls=%async_computation.24 | async-start | bytes 3604480 | tf_op jit(solution)/shard_map/all_gather | solution.py:221
  676.9 277.5 %all-gather.33.cloned.1.call-start = ((), (), s32[]{:S(2)}) async-start(), calls=%async_computation.26 | async-start | bytes 9437184 | tf_op jit(solution)/shard_map/all_gather | solution.py:85
  677.4 386.7 %reduce-scatter.23.cloned.1.call-start = ((), (), s32[]{:S(2)}) async-start(), calls=%async_computation.27 | async-start | bytes 9437184 | tf_op jit(solution)/shard_map/reduce_scatter | solution.py:95
  992.7 87.2 %copy-start.42 = (bf16[2048,256]{1,0:T(8,128)(2,1)S(1)}, bf16[2048,256]{1,0:T(8,128)(2,1)}, u32[]{:S(2)}) copy-start(bf16[2048,256]{1,0:T(8,128)(2,1)} %param.26) | copy-start | bytes 3145732
  992.7 146.0 %all-gather.35.cloned.1.call-start = ((), (), s32[]{:S(2)}) async-start(), calls=%async_computation.28 | async-start | bytes 9437184 | tf_op jit(solution)/shard_map/all_gather | solution.py:85
  1082.7 861.4 %reduce-scatter.41.cloned.1.call-start = ((), (), s32[]{:S(2)}) async-start(), calls=%async_computation.37 | async-start | bytes 3604480 | tf_op jit(solution)/shard_map/reduce_scatter | solution.py:362
  1093.4 853.3 %reduce-scatter.39.cloned.1.call-start = ((), (), s32[]{:S(2)}) async-start(), calls=%async_computation.36 | async-start | bytes 3604480 | tf_op jit(solution)/shard_map/reduce_scatter | solution.py:348
  1106.2 842.8 %reduce-scatter.37.cloned.1.call-start = ((), (), s32[]{:S(2)}) async-start(), calls=%async_computation.35 | async-start | bytes 3604480 | tf_op jit(solution)/shard_map/reduce_scatter | solution.py:342
  1134.0 817.7 %reduce-scatter.43.cloned.1.call-start = ((), (), s32[]{:S(2)}) async-start(), calls=%async_computation.38 | async-start | bytes 655360
  1178.0 431.2 %copy-start.34 = (f32[32,2,64,64]{3,2,1,0:T(8,128)S(1)}, f32[32,2,64,64]{3,2,1,0:T(8,128)}, u32[]{:S(2)}) copy-start(f32[32,2,64,64]{3,2,1,0:T(8,128)} %fusion.159) | copy-start | bytes 3145732
  1771.0 182.4 %reduce-scatter.45.cloned.1.call-start = ((), (), s32[]{:S(2)}) async-start(), calls=%async_computation.39 | async-start | bytes 655360
  1776.8 178.2 %reduce-scatter.27.cloned.1.call-start = ((), (), s32[]{:S(2)}) async-start(), calls=%async_computation.30 | async-start | bytes 1310720 | tf_op jit(solution)/shard_map/reduce_scatter | solution.py:306
  1792.5 164.2 %reduce-scatter.29.cloned.1.call-start = ((), (), s32[]{:S(2)}) async-start(), calls=%async_computation.31 | async-start | bytes 1310720 | tf_op jit(solution)/shard_map/reduce_scatter | solution.py:312
  1799.5 159.1 %reduce-scatter.35.cloned.1.call-start = ((), (), s32[]{:S(2)}) async-start(), calls=%async_computation.34 | async-start | bytes 2621440 | tf_op jit(solution)/shard_map/reduce_scatter | solution.py:356
  1815.4 147.7 %reduce-scatter.33.cloned.1.call-start = ((), (), s32[]{:S(2)}) async-start(), calls=%async_computation.33 | async-start | bytes 2621440 | tf_op jit(solution)/shard_map/reduce_scatter | solution.py:324
  1838.0 171.1 %reduce-scatter.31.cloned.1.call-start = ((), (), s32[]{:S(2)}) async-start(), calls=%async_computation.32 | async-start | bytes 2621440 | tf_op jit(solution)/shard_map/reduce_scatter | solution.py:318
  1870.2 213.4 %reduce-scatter.25.cloned.1.call-start = ((), (), s32[]{:S(2)}) async-start(), calls=%async_computation.29 | async-start | bytes 9437184 | tf_op jit(solution)/shard_map/reduce_scatter | solution.py:95
  1931.3 226.8 %reduce-scatter.21.cloned.1.call-start = ((), (), s32[]{:S(2)}) async-start(), calls=%async_computation.25 | async-start | bytes 9437184 | tf_op jit(solution)/shard_map/reduce_scatter | solution.py:89
  1958.6 125.0 %copy-start.11 = (bf16[2048,256]{1,0:T(8,128)(2,1)S(1)}, bf16[2048,256]{1,0:T(8,128)(2,1)}, u32[]{:S(2)}) copy-start(bf16[2048,256]{1,0:T(8,128)(2,1)} %param.24) | copy-start | bytes 3145732
  1958.6 125.0 %copy-start.99 = (f32[2048]{0:T(1024)S(1)}, f32[2048]{0:T(1024)}, u32[]{:S(2)}) copy-start(f32[2048]{0:T(1024)} %copy-done.98) | copy-start | bytes 24580
  1958.6 125.0 %copy-start.142 = (f32[256]{0:T(256)S(1)}, f32[256]{0:T(256)}, u32[]{:S(2)}) copy-start(f32[256]{0:T(256)} %param.27) | copy-start | bytes 3076
  1965.3 120.6 %copy-start.151 = (f32[256]{0:T(256)S(1)}, f32[256]{0:T(256)}, u32[]{:S(2)}) copy-start(f32[256]{0:T(256)} %get-tuple-element.633) | copy-start | bytes 3076
  1965.3 152.4 %copy-start.105 = (f32[2048]{0:T(1024)S(1)}, f32[2048]{0:T(1024)}, u32[]{:S(2)}) copy-start(f32[2048]{0:T(1024)} %copy-done.104) | copy-start | bytes 24580
  1965.3 192.9 %copy-start.29 = (bf16[2048,256]{1,0:T(8,128)(2,1)S(1)}, bf16[2048,256]{1,0:T(8,128)(2,1)}, u32[]{:S(2)}) copy-start(bf16[2048,256]{1,0:T(8,128)(2,1)} %reduce-scatter.19.cloned.1.call-done) | copy-start | bytes 3145732
  1965.3 192.9 %copy-start.43 = (bf16[2048,256]{1,0:T(8,128)(2,1)S(1)}, bf16[2048,256]{1,0:T(8,128)(2,1)}, u32[]{:S(2)}) copy-start(bf16[2048,256]{1,0:T(8,128)(2,1)} %param.26) | copy-start | bytes 3145732
  1965.3 192.9 %copy-start.86 = (f32[2048]{0:T(1024)S(1)}, f32[2048]{0:T(1024)}, u32[]{:S(2)}) copy-start(f32[2048]{0:T(1024)} %copy-done.85) | copy-start | bytes 24580
  1965.3 192.9 %copy-start.107 = (f32[2048]{0:T(1024)S(1)}, f32[2048]{0:T(1024)}, u32[]{:S(2)}) copy-start(f32[2048]{0:T(1024)} %copy-done.106) | copy-start | bytes 24580
  1965.3 192.9 %copy-start.124 = (f32[256]{0:T(256)S(1)}, f32[256]{0:T(256)}, u32[]{:S(2)}) copy-start(f32[256]{0:T(256)} %param.40) | copy-start | bytes 3076
  (188 other events, 1025.6 us)
Sparse Core Ops, SparseCore 0:
  27.6 55.3 all-gather.12
  84.6 27.9 all-gather.14
  114.1 27.4 all-gather.18
  143.0 45.4 all-gather.16
  189.8 44.6 all-gather.20
  236.0 44.6 all-gather.22
  588.6 70.7 reduce-scatter.18
  661.0 59.1 all-gather.28
  722.8 54.6 all-gather.24
  779.0 59.1 all-gather.26
  839.8 57.8 all-gather.30
  899.6 54.6 all-gather.32
  992.8 71.2 reduce-scatter.22
  1082.8 55.8 all-gather.34
  1140.9 56.1 reduce-scatter.40
  1199.3 56.0 reduce-scatter.38
  1257.5 56.0 reduce-scatter.36
  1771.1 21.6 reduce-scatter.42
  1795.7 19.9 reduce-scatter.44
  1818.3 25.4 reduce-scatter.26
  1846.8 25.7 reduce-scatter.28
  1874.9 42.5 reduce-scatter.34
  1919.9 43.1 reduce-scatter.32
  1965.8 43.1 reduce-scatter.30
  2012.9 70.6 reduce-scatter.24
  2086.9 71.2 reduce-scatter.20
where the time goes:
time: 2190 us; the launch traced here: 2170 us
  matrix products  678 us (31%)
  waiting for transfers between devices  595 us (27%)
  local copies, waits for them, and re-layouts  432 us (20%)
  other arithmetic  347 us (16%)
  blocking collectives  97.2 us (4%)
    squeeze x192, local copies, waits for them, and re-layouts, block_delta(): lax.scan(jax.checkpoint(advance), initial, (weight_part, update_part, sco...  184 us
    reduce_scatter x2, waiting for transfers between devices, sum_grad_columns(): lax.psum_scatter(term.astype(jnp.bfloat16), 'col', scatter_dimension=1, t...  144 us
    another operation x4, other arithmetic, block_delta(): jax.scipy.linalg.solve_triangular(system, jnp.transpose(right_side, (0, 2...  135 us
    dot_general x10, matrix products, cols_product(): lax.dot_general(first_op, second_op, (((1,), (1,)), ((), ())), preferred_...  131 us
    dot_general x96, matrix products, advance(): jnp.einsum('hcs,hsv->hcv', score_now, prediction_error, precision=TOP_PRE...  113 us
    reduce_scatter x2, waiting for transfers between devices, sum_columns(): lax.psum_scatter(term.astype(jnp.bfloat16), 'col', scatter_dimension=1, t...  111 us
    dot_general x128, matrix products, advance(): jnp.einsum('mwn,mny->mwy', current_weight, carried_state, precision=TOP_P...  93.9 us
    dot_general x96, matrix products, advance(): jnp.einsum('dyc,dya->dca', current_key, prediction_error, precision=TOP_P...  81.5 us
  transfers between devices with their start and end apart: 26, of which 15 were waited for; matrix products, arithmetic and copies ran while one was open for 63% of the time, Pallas kernels for 0%

commit v1 on v0

v1 whole, which is shorter than its diff:
```python
import functools

import jax
import jax.numpy as jnp
from jax import lax
from jax.experimental import pallas as pl
from jax.experimental.pallas import tpu as pltpu
from jax.sharding import PartitionSpec as P

D = 2048
DK = 128
DV = 256
CONV = 4
SEQ = 1024
CHUNK = 128
EPSILON = 1e-06
SCALE = DK ** (-0.5)
f32 = jnp.float32
bf16 = jnp.bfloat16


def mm(a, b, dims=((1,), (0,))):
    return lax.dot_general(a, b, (dims, ((), ())), preferred_element_type=f32)


def split(a):
    hi = a.astype(bf16)
    return hi, (a - hi.astype(f32)).astype(bf16)


def mm3(a, b):
    ah, al = split(a)
    bh, bl = split(b)
    return mm(ah, bh) + (mm(ah, bl) + mm(al, bh))


def sigmoid(u):
    return 1.0 / (1.0 + jnp.exp(-u))


def iotas(n):
    return (
        lax.broadcasted_iota(jnp.int32, (n, n), 0),
        lax.broadcasted_iota(jnp.int32, (n, n), 1),
    )


def unit_lower_inverse(a, row, col):
    n = a.shape[0]
    eye = (row == col).astype(f32)
    base = 8
    d = jnp.where(row // base == col // base, a, 0.0)
    d2 = mm3(d, d)
    x = eye - d
    x = x + mm3(x, d2)
    d4 = mm3(d2, d2)
    x = x + mm3(x, d4)
    size = base
    while size < n:
        off = jnp.where((row // (2 * size) == col // (2 * size)) & (row // size != col // size), a, 0.0)
        xh = x.astype(bf16)
        x = x - mm(xh, mm(off.astype(bf16), xh).astype(bf16))
        size *= 2
    return x


def conv_taps(buf, s, width, weights, masks):
    pre = weights[0:1] * buf[s, 8 : 8 + CHUNK, :]
    for j in range(1, CONV):
        pre = pre + weights[j : j + 1] * buf[s, 8 - j : 8 - j + CHUNK, :] * masks[j - 1]
    return pre


def forward_kernel(heads, seqs, pq, pk, pv, pg, cols, rows, wq, wk, wv, gain,
                   gated, inv_out, upd_out, state_out, state, bq, bk, bv):
    step = pl.program_id(0)

    @pl.when(step == 0)
    def _():
        state[...] = jnp.zeros_like(state)
        for buf in (bq, bk, bv):
            buf[:, 0:8, :] = jnp.zeros_like(buf[:, 0:8, :])

    row, col = iotas(CHUNK)
    lower = row >= col
    tril = lower.astype(bf16)
    for s in range(seqs):
        cc = cols[s]
        rr = rows[s]
        masks = [cc[:, j : j + 1] for j in range(CONV - 1)]
        ch, cl = split(cc)
        csum = mm(tril, ch) + mm(tril, cl)
        rh, rl = split(rr)
        rsum = mm(rh, tril, ((1,), (1,))) + mm(rl, tril, ((1,), (1,)))
        same = (cc[:, 6:7] == rr[6:7, :]) & lower
        for src, buf in ((pq, bq), (pk, bk), (pv, bv)):
            buf[s, 8 : 8 + CHUNK, :] = src[s]
        cq = conv_taps(bq, s, heads * DK, wq, masks)
        ck = conv_taps(bk, s, heads * DK, wk, masks)
        cv = conv_taps(bv, s, heads * DV, wv, masks)
        for buf in (bq, bk, bv):
            buf[s, 0:8, :] = buf[s, CHUNK : CHUNK + 8, :]
        aq = cq * sigmoid(cq)
        ak = ck * sigmoid(ck)
        av = cv * sigmoid(cv)
        for h in range(heads):
            keys = slice(h * DK, (h + 1) * DK)
            vals = slice(h * DV, (h + 1) * DV)
            q = aq[:, keys]
            q = (q * lax.rsqrt(jnp.sum(q * q, axis=1, keepdims=True) + EPSILON)).astype(bf16)
            k = ak[:, keys]
            k = (k * lax.rsqrt(jnp.sum(k * k, axis=1, keepdims=True) + EPSILON)).astype(bf16)
            v = av[:, vals].astype(bf16).astype(f32)
            beta = cc[:, 8 + h : 9 + h]
            at = 8 + heads + h
            gcol = csum[:, at : at + 1]
            grow = rsum[at : at + 1, :]
            decay = jnp.where(same, jnp.exp(jnp.minimum(gcol - grow, 0.0)), 0.0)
            start = jnp.exp(gcol) * cc[:, 7:8]
            end = jnp.exp(jnp.minimum(gcol[CHUNK - 1 :, :] - gcol, 0.0)) * jnp.where(
                cc[:, 6:7] == cc[CHUNK - 1 :, 6:7], 1.0, 0.0
            )
            kk = mm(k, k, ((1,), (1,)))
            qk = mm(q, k, ((1,), (1,)))
            coupling = jnp.where(row > col, beta * decay * kk, 0.0)
            inv = unit_lower_inverse(coupling, row, col).astype(bf16)
            inv_out[s, h] = inv
            begin = state[s, h]
            state_out[0, s, h] = begin
            low = begin.astype(bf16)
            right = beta * (v - start * mm(k, low))
            upd = mm(inv, right.astype(bf16)).astype(bf16)
            upd_out[s, :, vals] = upd
            mixed = (start * mm(q, low) + mm((decay * qk).astype(bf16), upd)) * SCALE
            kend = (end * k.astype(f32)).astype(bf16)
            state[s, h] = start[CHUNK - 1 :, :] * begin + mm(kend, upd, ((0,), (0,)))
            gate = pg[s, :, vals]
            scaled = mixed * lax.rsqrt(jnp.mean(mixed * mixed, axis=1, keepdims=True) + EPSILON)
            gated[s, :, vals] = (scaled * gain[:, vals] * (gate * sigmoid(gate))).astype(bf16)


def backward_kernel(heads, seqs, dgated, pq, pk, pv, pg, hq, hk, hv, cols, rows, inv_in, upd_in, state_in,
                    wq, wk, wv, gain,
                    dpq, dpk, dpv, dpg, dcols, dwq, dwk, dwv, dgain,
                    dstate, bq, bk, bv, tq, tk, tv):
    step = pl.program_id(0)

    @pl.when(step == 0)
    def _():
        dstate[...] = jnp.zeros_like(dstate)
        for buf in (tq, tk, tv):
            buf[:, CHUNK : CHUNK + 8, :] = jnp.zeros_like(buf[:, CHUNK : CHUNK + 8, :])
        for out in (dwq, dwk, dwv, dgain):
            out[...] = jnp.zeros_like(out)

    row, col = iotas(CHUNK)
    lower = row >= col
    tril = lower.astype(bf16)
    lane = lax.broadcasted_iota(jnp.int32, (CHUNK, 2 * heads), 1)
    last = lax.broadcasted_iota(jnp.int32, (CHUNK, 1), 0) == CHUNK - 1
    for s in range(seqs):
        cc = cols[s]
        rr = rows[s]
        masks = [cc[:, j : j + 1] for j in range(CONV - 1)]
        ahead = [cc[:, 3 + j : 4 + j] for j in range(CONV - 1)]
        ch, cl = split(cc)
        csum = mm(tril, ch) + mm(tril, cl)
        rh, rl = split(rr)
        rsum = mm(rh, tril, ((1,), (1,))) + mm(rl, tril, ((1,), (1,)))
        same = (cc[:, 6:7] == rr[6:7, :]) & lower
        pres = []
        for src, halo, buf, weights in ((pq, hq, bq, wq), (pk, hk, bk, wk), (pv, hv, bv, wv)):
            buf[s, 0:8, :] = halo[s]
            buf[s, 8 : 8 + CHUNK, :] = src[s]
            pres.append(conv_taps(buf, s, None, weights, masks))
        sigs = [sigmoid(pre) for pre in pres]
        acts = [pre * sig for pre, sig in zip(pres, sigs)]
        dcol = jnp.zeros((CHUNK, 2 * heads), f32)
        for h in range(heads):
            keys = slice(h * DK, (h + 1) * DK)
            vals = slice(h * DV, (h + 1) * DV)
            q = acts[0][:, keys]
            rq = lax.rsqrt(jnp.sum(q * q, axis=1, keepdims=True) + EPSILON)
            qn = q * rq
            q = qn.astype(bf16)
            k = acts[1][:, keys]
            rk = lax.rsqrt(jnp.sum(k * k, axis=1, keepdims=True) + EPSILON)
            kn = k * rk
            k = kn.astype(bf16)
            v = acts[2][:, vals].astype(bf16).astype(f32)
            beta = cc[:, 8 + h : 9 + h]
            at = 8 + heads + h
            gcol = csum[:, at : at + 1]
            grow = rsum[at : at + 1, :]
            decay = jnp.where(same, jnp.exp(jnp.minimum(gcol - grow, 0.0)), 0.0)
            start = jnp.exp(gcol) * cc[:, 7:8]
            end = jnp.exp(jnp.minimum(gcol[CHUNK - 1 :, :] - gcol, 0.0)) * jnp.where(
                cc[:, 6:7] == cc[CHUNK - 1 :, 6:7], 1.0, 0.0
            )
            kk = mm(k, k, ((1,), (1,)))
            qk = mm(q, k, ((1,), (1,)))
            plain = jnp.where(row > col, decay * kk, 0.0)
            scores = decay * qk
            scores_low = scores.astype(bf16)
            inv = inv_in[s, h]
            upd = upd_in[s, :, vals]
            begin = state_in[0, s, h]
            low = begin.astype(bf16)
            ks = mm(k, low)
            qs = mm(q, low)
            mixed = (start * qs + mm(scores_low, upd)) * SCALE
            gate = pg[s, :, vals]
            sg = sigmoid(gate)
            silu = gate * sg
            rm = lax.rsqrt(jnp.mean(mixed * mixed, axis=1, keepdims=True) + EPSILON)
            scaled = mixed * rm
            dy = dgated[s, :, vals]
            dyn = dy * scaled
            gains = gain[:, vals]
            dgain[:, vals] += jnp.sum(dyn * silu, axis=0, keepdims=True)
            dpg[s, :, vals] = (dyn * gains * (sg * (1.0 + gate * (1.0 - sg)))).astype(bf16)
            dscaled = dy * gains * silu
            dmixed = rm * (dscaled - scaled * jnp.mean(dscaled * scaled, axis=1, keepdims=True))
            dout = (dmixed * SCALE)
            dlow = dout.astype(bf16)
            ds = dstate[s, h]
            dsl = ds.astype(bf16)
            kf = k.astype(f32)
            kend = (end * kf).astype(bf16)
            dupd = mm(scores_low, dlow, ((0,), (0,))) + mm(kend, dsl)
            dright = mm(inv, dupd.astype(bf16), ((0,), (0,)))
            drl = dright.astype(bf16)
            dscore = mm(dlow, upd, ((1,), (1,)))
            dcoup = -mm(drl, upd, ((1,), (1,)))
            uds = mm(upd, dsl, ((1,), (1,)))
            w = beta * dright
            wa = (start * w).astype(bf16)
            dsc = (dscore * decay).astype(bf16)
            dqn = start * mm(dlow, low, ((1,), (1,))) + mm(dsc, k)
            g = jnp.where(row > col, beta * dcoup * decay, 0.0)
            dkn = (
                end * uds
                - mm(wa, low, ((1,), (1,)))
                + mm(dsc, q, ((0,), (0,)))
                + mm((g + g.T).astype(bf16), k)
            )
            dbeta = jnp.sum(dright * (v - start * ks), axis=1, keepdims=True) + jnp.sum(
                dcoup * plain, axis=1, keepdims=True
            )
            dstart = jnp.sum(dout * qs - w * ks, axis=1, keepdims=True)
            dend = jnp.sum(kf * uds, axis=1, keepdims=True) * end
            z = dscore * scores + dcoup * (beta * plain)
            final = start[CHUNK - 1 :, :]
            carried = jnp.sum(jnp.sum(ds * begin, axis=1, keepdims=True), axis=0, keepdims=True) * final
            carried = carried + jnp.sum(dend, axis=0, keepdims=True)
            dg = jnp.sum(z - z.T, axis=1, keepdims=True) + dstart * start - dend
            dg = dg + jnp.where(last, carried, 0.0)
            dcol = dcol + jnp.where(lane == h, dbeta, 0.0) + jnp.where(lane == heads + h, dg, 0.0)
            dstate[s, h] = (
                mm((start * q.astype(f32)).astype(bf16), dlow, ((0,), (0,)))
                + final * ds
                - mm(k, wa, ((0,), (0,)))
            )
            dq = rq * (dqn - qn * jnp.sum(dqn * qn, axis=1, keepdims=True))
            dk = rk * (dkn - kn * jnp.sum(dkn * kn, axis=1, keepdims=True))
            for grad, n, buf, part in ((dq, 0, tq, keys), (dk, 1, tk, keys), (w, 2, tv, vals)):
                sig = sigs[n][:, part]
                buf[s, 0:CHUNK, part] = grad * (sig * (1.0 + pres[n][:, part] * (1.0 - sig)))
        dh, dl = split(dcol)
        dl2 = (dcol - dh.astype(f32) - dl.astype(f32)).astype(bf16)
        tail = ((0,), (0,))
        rev = mm(tril, dh, tail) + (mm(tril, dl, tail) + mm(tril, dl2, tail))
        dcols[s] = jnp.where(lane < heads, dcol, rev)
        for buf, src, out, weights, dw in ((tq, bq, dpq, wq, dwq), (tk, bk, dpk, wk, dwk), (tv, bv, dpv, wv, dwv)):
            pre = buf[s, 0:CHUNK, :]
            total = weights[0:1] * pre
            dw[0:1, :] += jnp.sum(pre * src[s, 8 : 8 + CHUNK, :], axis=0, keepdims=True)
            for j in range(1, CONV):
                total = total + weights[j : j + 1] * buf[s, j : j + CHUNK, :] * ahead[j - 1]
                dw[j : j + 1, :] += jnp.sum(
                    pre * masks[j - 1] * src[s, 8 - j : 8 - j + CHUNK, :], axis=0, keepdims=True
                )
            out[s] = total.astype(bf16)
            buf[s, CHUNK : CHUNK + 8, :] = buf[s, 0:8, :]


def whole(shape):
    return pl.BlockSpec(shape, lambda c: (0,) * len(shape))


def mixer_forward(pq, pk, pv, pg, cols, rows, wq, wk, wv, gain):
    seqs = pq.shape[0]
    heads = pq.shape[2] // DK
    steps = SEQ // CHUNK
    kw, vw = heads * DK, heads * DV

    def tok(width):
        return pl.BlockSpec((seqs, CHUNK, width), lambda c: (0, c, 0))

    return pl.pallas_call(
        functools.partial(forward_kernel, heads, seqs),
        grid=(steps,),
        in_specs=[tok(kw), tok(kw), tok(vw), tok(vw), tok(cols.shape[2]),
                  pl.BlockSpec((seqs, rows.shape[1], CHUNK), lambda c: (0, 0, c)),
                  whole((CONV, kw)), whole((CONV, kw)), whole((CONV, vw)), whole((1, vw))],
        out_specs=[tok(vw),
                   pl.BlockSpec((seqs, heads, CHUNK, CHUNK), lambda c: (0, 0, c, 0)),
                   tok(vw),
                   pl.BlockSpec((1, seqs, heads, DK, DV), lambda c: (c, 0, 0, 0, 0))],
        out_shape=[jax.ShapeDtypeStruct((seqs, SEQ, vw), bf16),
                   jax.ShapeDtypeStruct((seqs, heads, SEQ, CHUNK), bf16),
                   jax.ShapeDtypeStruct((seqs, SEQ, vw), bf16),
                   jax.ShapeDtypeStruct((steps, seqs, heads, DK, DV), f32)],
        scratch_shapes=[pltpu.VMEM((seqs, heads, DK, DV), f32),
                        pltpu.VMEM((seqs, 8 + CHUNK, kw), f32),
                        pltpu.VMEM((seqs, 8 + CHUNK, kw), f32),
                        pltpu.VMEM((seqs, 8 + CHUNK, vw), f32)],
        compiler_params=pltpu.CompilerParams(dimension_semantics=("arbitrary",), vmem_limit_bytes=48 << 20),
        name="mixer_forward",
    )(pq, pk, pv, pg, cols, rows, wq, wk, wv, gain)


def mixer_backward(dgated, pq, pk, pv, pg, cols, rows, inv, upd, states, wq, wk, wv, gain):
    seqs = pq.shape[0]
    heads = pq.shape[2] // DK
    steps = SEQ // CHUNK
    kw, vw = heads * DK, heads * DV

    def tok(width):
        return pl.BlockSpec((seqs, CHUNK, width), lambda c: (0, steps - 1 - c, 0))

    def halo(width):
        return pl.BlockSpec(
            (seqs, 8, width),
            lambda c: (0, jnp.maximum((steps - 1 - c) * (CHUNK // 8) - 1, 0), 0),
        )

    return pl.pallas_call(
        functools.partial(backward_kernel, heads, seqs),
        grid=(steps,),
        in_specs=[tok(vw), tok(kw), tok(kw), tok(vw), tok(vw), halo(kw), halo(kw), halo(vw), tok(cols.shape[2]),
                  pl.BlockSpec((seqs, rows.shape[1], CHUNK), lambda c: (0, 0, steps - 1 - c)),
                  pl.BlockSpec((seqs, heads, CHUNK, CHUNK), lambda c: (0, 0, steps - 1 - c, 0)),
                  tok(vw),
                  pl.BlockSpec((1, seqs, heads, DK, DV), lambda c: (steps - 1 - c, 0, 0, 0, 0)),
                  whole((CONV, kw)), whole((CONV, kw)), whole((CONV, vw)), whole((1, vw))],
        out_specs=[tok(kw), tok(kw), tok(vw), tok(vw), tok(2 * heads),
                   whole((CONV, kw)), whole((CONV, kw)), whole((CONV, vw)), whole((1, vw))],
        out_shape=[jax.ShapeDtypeStruct((seqs, SEQ, kw), bf16),
                   jax.ShapeDtypeStruct((seqs, SEQ, kw), bf16),
                   jax.ShapeDtypeStruct((seqs, SEQ, vw), bf16),
                   jax.ShapeDtypeStruct((seqs, SEQ, vw), bf16),
                   jax.ShapeDtypeStruct((seqs, SEQ, 2 * heads), f32),
                   jax.ShapeDtypeStruct((CONV, kw), f32),
                   jax.ShapeDtypeStruct((CONV, kw), f32),
                   jax.ShapeDtypeStruct((CONV, vw), f32),
                   jax.ShapeDtypeStruct((1, vw), f32)],
        scratch_shapes=[pltpu.VMEM((seqs, heads, DK, DV), f32)]
        + [pltpu.VMEM((seqs, 8 + CHUNK, width), f32) for width in (kw, kw, vw)] * 2,
        compiler_params=pltpu.CompilerParams(dimension_semantics=("arbitrary",), vmem_limit_bytes=56 << 20),
        name="mixer_backward",
    )(dgated, pq, pk, pv, pg, pq, pk, pv, cols, rows, inv, upd, states, wq, wk, wv, gain)


def token_tables(seg_ids, strength, log_decay):
    seqs = seg_ids.shape[0] // SEQ
    seg = seg_ids.reshape(seqs, 1, SEQ)
    position = lax.broadcasted_iota(jnp.int32, (1, 1, SEQ), 2)
    back, ahead = [], []
    for j in range(1, CONV):
        same = seg[:, :, j:] == seg[:, :, : SEQ - j]
        none = jnp.zeros((seqs, 1, j), jnp.bool_)
        back.append(jnp.concatenate([none, same], axis=2))
        ahead.append(jnp.concatenate([same, none], axis=2))
    before = jnp.concatenate([jnp.full((seqs, 1, 1), -1, jnp.int32), seg[:, :, CHUNK - 1 : SEQ - 1 : CHUNK]], axis=2)
    carry = seg == jnp.repeat(before, CHUNK, axis=2)
    heads = strength.shape[0]
    tables = [m.astype(f32) for m in back + ahead] + [seg.astype(f32), carry.astype(f32)]
    tables += [
        jnp.swapaxes(strength.reshape(heads, seqs, SEQ), 0, 1),
        jnp.swapaxes(log_decay.reshape(heads, seqs, SEQ), 0, 1),
    ]
    pad = 16 - 8 - 2 * heads
    if pad:
        tables.append(jnp.zeros((seqs, pad, SEQ), f32))
    rows = jnp.concatenate(tables, axis=1)
    return rows, jnp.swapaxes(rows, 1, 2)


def rows_product(first_op, second_op):
    return lax.dot_general(
        first_op, second_op, (((0,), (0,)), ((), ())), preferred_element_type=f32
    )


def cols_product(first_op, second_op):
    return lax.dot_general(
        first_op, second_op, (((1,), (1,)), ((), ())), preferred_element_type=f32
    )


def shard_norm(values, gains):
    squares = lax.psum(jnp.sum(values * values, axis=1), "col")
    scales = lax.rsqrt(squares / D + EPSILON)
    return (scales, values * scales[:, None] * gains)


def shard_norm_back(values, gains, scales, grad_out):
    weighted = grad_out * gains
    totals = lax.psum(jnp.sum(weighted * values, axis=1), "col")
    grad_values = (
        scales[:, None] * weighted - values * (scales * scales * scales * totals / D)[:, None]
    )
    grad_gains = jnp.sum(grad_out * values * scales[:, None], axis=0)
    return (grad_values, grad_gains)


def gather_cols(values):
    return lax.all_gather(values, "col", axis=1, tiled=True)


def gather_rows(values, axis):
    return lax.all_gather(values, "row", axis=axis, tiled=True)


def sum_columns(term):
    return lax.psum_scatter(
        term.astype(bf16), "col", scatter_dimension=1, tiled=True
    ).astype(f32)


def sum_rows(term, axis):
    return lax.psum_scatter(
        term.astype(bf16), "row", scatter_dimension=axis, tiled=True
    ).astype(f32)


def on_device(
    hidden_in,
    seg_ids,
    cotangent,
    norm_mixer,
    w_query,
    w_key,
    w_value,
    w_gate,
    w_beta,
    w_decay,
    decay_log,
    conv_query,
    conv_key,
    conv_value,
    norm_gated,
    w_out,
    norm_ffn,
    w_ffn_gate,
    w_ffn_up,
    w_ffn_down,
):
    tokens = seg_ids.shape[0]
    seqs = tokens // SEQ
    heads = decay_log.shape[0]

    def by_seq(values):
        return values.reshape(seqs, SEQ, values.shape[1])

    def flat(values):
        return values.reshape(tokens, values.shape[2])

    small_in = gather_rows(jnp.concatenate([w_beta, w_decay], axis=1).T, 1)
    full = [gather_rows(w, 0) for w in (w_query, w_key, w_value, w_gate)]
    full_out = gather_rows(w_out, 1)
    full_gate = gather_rows(w_ffn_gate, 0)
    full_up = gather_rows(w_ffn_up, 0)
    full_down = gather_rows(w_ffn_down, 1)

    hidden = hidden_in.astype(f32)
    scale_mixer, normed_shard = shard_norm(hidden, norm_mixer)
    normed = gather_cols(normed_shard.astype(bf16))
    projected = [by_seq(jnp.dot(normed, w, preferred_element_type=f32)) for w in full]
    proj_small = cols_product(small_in, normed)
    proj_beta, proj_decay = proj_small[:heads], proj_small[heads:]
    strength = jax.nn.sigmoid(proj_beta)
    rate = -jnp.exp(decay_log)[:, None]
    log_decay = rate * jax.nn.softplus(proj_decay)
    rows, cols = token_tables(seg_ids, strength, log_decay)
    gains = norm_gated[None]
    gated, inv, upd, states = mixer_forward(
        *projected, cols, rows, conv_query, conv_key, conv_value, gains
    )
    gated = flat(gated)
    middle = hidden + sum_columns(jnp.dot(gated, full_out, preferred_element_type=f32))
    scale_ffn, normed_mid = shard_norm(middle, norm_ffn)
    normed_ffn = gather_cols(normed_mid.astype(bf16))
    gate_pre = jnp.dot(normed_ffn, full_gate, preferred_element_type=f32)
    up_pre = jnp.dot(normed_ffn, full_up, preferred_element_type=f32)
    sig_gate = jax.nn.sigmoid(gate_pre)
    inner_act = (gate_pre * sig_gate * up_pre).astype(bf16)
    block_out = (
        middle + sum_columns(jnp.dot(inner_act, full_down, preferred_element_type=f32))
    ).astype(bf16)

    grad_top = gather_cols(cotangent)
    grad_inner = cols_product(grad_top, full_down)
    grad_gate = (grad_inner * up_pre * sig_gate * (1.0 + gate_pre * (1.0 - sig_gate))).astype(bf16)
    grad_up = (grad_inner * gate_pre * sig_gate).astype(bf16)
    grad_normed_ffn = sum_columns(
        cols_product(grad_gate, full_gate) + cols_product(grad_up, full_up)
    )
    grad_from_ffn, grad_norm_ffn = shard_norm_back(middle, norm_ffn, scale_ffn, grad_normed_ffn)
    grad_middle = cotangent.astype(f32) + grad_from_ffn
    grad_mid_full = gather_cols(grad_middle.astype(bf16))
    grad_gated = cols_product(grad_mid_full, full_out)
    dpq, dpk, dpv, dpg, dcols, dwq, dwk, dwv, dgain = mixer_backward(
        by_seq(grad_gated), *projected, cols, rows, inv, upd, states,
        conv_query, conv_key, conv_value, gains,
    )
    grad_proj = [flat(g) for g in (dpq, dpk, dpv, dpg)]
    dsmall = flat(dcols).T
    dstrength, dlog = dsmall[:heads], dsmall[heads:]
    grad_small = jnp.concatenate(
        [dstrength * strength * (1.0 - strength), dlog * rate * jax.nn.sigmoid(proj_decay)], axis=0
    ).astype(bf16)
    grad_decay_log = jnp.sum(dlog * log_decay, axis=1)
    term = rows_product(grad_small, small_in)
    for g, w in zip(grad_proj, full):
        term = term + cols_product(g, w)
    grad_normed = sum_columns(term)
    grad_from_mixer, grad_norm_mixer = shard_norm_back(hidden, norm_mixer, scale_mixer, grad_normed)
    grad_input = grad_middle + grad_from_mixer

    in_grads = [sum_rows(rows_product(normed, g), 0) for g in grad_proj]
    small_grads = sum_rows(jnp.dot(grad_small, normed, preferred_element_type=f32), 1).T
    gate_grad = sum_rows(rows_product(normed_ffn, grad_gate), 0)
    up_grad = sum_rows(rows_product(normed_ffn, grad_up), 0)
    out_grad = sum_rows(rows_product(gated, grad_mid_full), 1)
    down_grad = sum_rows(rows_product(inner_act, grad_top), 1)
    small = lax.psum(
        (grad_norm_mixer, grad_norm_ffn, grad_decay_log, dwq, dwk, dwv, dgain[0]), "row"
    )
    return (
        block_out,
        grad_input,
        small[0],
        in_grads[0],
        in_grads[1],
        in_grads[2],
        in_grads[3],
        small_grads[:, :heads],
        small_grads[:, heads:],
        small[2],
        small[3],
        small[4],
        small[5],
        small[6],
        out_grad,
        small[1],
        gate_grad,
        up_grad,
        down_grad,
    )


def solution(mesh):
    placed = (
        P("row", "col"),
        P("row"),
        P("row", "col"),
        P("col"),
        P("row", "col"),
        P("row", "col"),
        P("row", "col"),
        P("row", "col"),
        P("row", "col"),
        P("row", "col"),
        P("col"),
        P(None, "col"),
        P(None, "col"),
        P(None, "col"),
        P("col"),
        P("col", "row"),
        P("col"),
        P("row", "col"),
        P("row", "col"),
        P("col", "row"),
    )
    return jax.shard_map(
        on_device,
        mesh=mesh,
        in_specs=placed,
        out_specs=(
            P("row", "col"),
            P("row", "col"),
            P("col"),
            P("row", "col"),
            P("row", "col"),
            P("row", "col"),
            P("row", "col"),
            P("row", "col"),
            P("row", "col"),
            P("col"),
            P(None, "col"),
            P(None, "col"),
            P(None, "col"),
            P("col"),
            P("col", "row"),
            P("col"),
            P("row", "col"),
            P("row", "col"),
            P("col", "row"),
        ),
        check_vma=False,
    )
```

time: 2190 us -> 1440 us (0.66)
  local copies, waits for them, and re-layouts: 432 us -> 12.8 us
  matrix products: 678 us -> 276 us
  other arithmetic: 347 us -> 39.2 us
  waiting for transfers between devices: 595 us -> 872 us
  Pallas kernels: 0 us -> 126 us
    dot_general x433 -> x9, matrix products: 460 us -> 82.7 us  [the longest x4 36 us: on_device(): jnp.dot(normed, w, preferred_element_type=f32)]
    squeeze x192 -> x0, local copies, waits for them, and re-layouts: 184 us -> none  [block_delta(): lax.scan(jax.checkpoint(advance), initial, (weight_part, update_part, sco...]
    another operation x39 -> x0, other arithmetic: 145 us -> none  [the longest x4 135 us: block_delta(): jax.scipy.linalg.solve_triangular(system, jnp.transpose(right_side, (0, 2...]
    all_gather x12, waiting for transfers between devices: 288 us -> 430 us  [the longest x8 259 us: gather_rows(): return lax.all_gather(values, 'row', axis=axis, tiled=True)]
    reduce_scatter x12, waiting for transfers between devices: 300 us -> 437 us  [the longest x4 254 us: sum_columns(): lax.psum_scatter(term.astype(bf16), 'col', scatter_dimension=1, tiled=True)]
    pallas_call x0 -> x2, Pallas kernels: none -> 126 us  [the longest x1 70.5 us: mixer_forward(): pl.pallas_call(functools.partial(forward_kernel, heads, seqs), grid=(step...]
    reduce_sum x50 -> x1, other arithmetic: 70.6 us -> 0.15 us  [on_device(): grad_decay_log = jnp.sum(dlog * log_decay, axis=1)]
    mul x50 -> x0, local copies, waits for them, and re-layouts: 58.3 us -> none  [the longest x32 22 us: advance(): decay_now[:, None, None] * carried_state]
  transfers between devices with their start and end apart: 26 -> 25, of which waited for: 15 -> 20; matrix products, arithmetic and copies ran while one was open for 63% -> 18% of each run, Pallas kernels for 0% -> 9%
where the time goes in v1:
time: 1440 us; the launch traced here: 1430 us
  waiting for transfers between devices  872 us (61%)
  matrix products  276 us (19%)
  Pallas kernels  126 us (9%)
  blocking collectives  86.5 us (6%)
  other arithmetic  39.2 us (3%)
  between operations  15.2 us (1%)
    all_gather x8, waiting for transfers between devices, gather_rows(): return lax.all_gather(values, 'row', axis=axis, tiled=True)  259 us
    reduce_scatter x4, waiting for transfers between devices, sum_columns(): lax.psum_scatter(term.astype(bf16), 'col', scatter_dimension=1, tiled=True)  254 us
    reduce_scatter x8, waiting for transfers between devices, sum_rows(): lax.psum_scatter(term.astype(bf16), 'row', scatter_dimension=axis, tiled=...  183 us
    all_gather x4, waiting for transfers between devices, gather_cols(): return lax.all_gather(values, 'col', axis=1, tiled=True)  171 us
    dot_general x9, matrix products, cols_product(): lax.dot_general(first_op, second_op, (((1,), (1,)), ((), ())), preferred_...  109 us
    dot_general x9, matrix products, rows_product(): lax.dot_general(first_op, second_op, (((0,), (0,)), ((), ())), preferred_...  84.4 us
    pallas_call x1, Pallas kernels, mixer_forward(): pl.pallas_call(functools.partial(forward_kernel, heads, seqs), grid=(step...  70.5 us
    pallas_call x1, Pallas kernels, mixer_backward(): pl.pallas_call(functools.partial(backward_kernel, heads, seqs), grid=(ste...  55.6 us
  transfers between devices with their start and end apart: 25, of which 20 were waited for; matrix products, arithmetic and copies ran while one was open for 18% of the time, Pallas kernels for 9%

profile of v1, /device:TPU:0, one launch (start us, length us, event | category | flops | bytes accessed | tf_op | source)
XLA Modules:
  0.0 1429.9 jit_solution(1765814166853773237)
XLA Ops:
  8.9 15.5 %psum.77 = f32[2048]{0:T(1024)S(1)} all-reduce(f32[2048]{0:T(1024)S(1)} %fusion.10), channel_id=1, replica_groups=mesh['row'=4,'col'=8] {'col'}, use_global_device_ids=true, to_apply=%region_1.0 | all-reduce | flops 2048 | bytes 16384 | tf_op jit(solution)/shard_map/psum | solution.py:403
  31.5 13.4 all_gather.44
  45.0 38.0 %all-gather.13.cloned.1.call-done = bf16[2048,2048]{1,0:T(8,128)(2,1)} async-done(((bf16[2048,256]{1,0:T(8,128)(2,1)}), bf16[2048,2048]{1,0:T(8,128)(2,1)}) %all-gather.13.cloned.1.call-update) | async-done | bytes 8388624 | tf_op jit(solution)/shard_map/all_gather | solution.py:419
  88.6 23.9 %all-gather.17.cloned.1.call-done = bf16[2048,256]{1,0:T(8,128)(2,1)} async-done(((bf16[512,256]{1,0:T(8,128)(2,1)}), bf16[2048,256]{1,0:T(8,128)(2,1)}) %all-gather.17.cloned.1.call-update) | async-done | bytes 1048592 | tf_op jit(solution)/shard_map/all_gather | solution.py:423
  121.0 20.6 %all-gather.15.cloned.1.call-done = bf16[2048,256]{1,0:T(8,128)(2,1)} async-done(((bf16[512,256]{1,0:T(8,128)(2,1)}), bf16[2048,256]{1,0:T(8,128)(2,1)}) %all-gather.15.cloned.1.call-update) | async-done | bytes 1048592 | tf_op jit(solution)/shard_map/all_gather | solution.py:423
  148.9 39.6 %all-gather.21.cloned.1.call-done = bf16[2048,512]{1,0:T(8,128)(2,1)} async-done(((bf16[512,512]{1,0:T(8,128)(2,1)}), bf16[2048,512]{1,0:T(8,128)(2,1)}) %all-gather.21.cloned.1.call-update) | async-done | bytes 2097168 | tf_op jit(solution)/shard_map/all_gather | solution.py:423
  188.4 10.5 fusion.35
  198.9 35.6 %all-gather.19.cloned.1.call-done = bf16[2048,512]{1,0:T(8,128)(2,1)} async-done(((bf16[512,512]{1,0:T(8,128)(2,1)}), bf16[2048,512]{1,0:T(8,128)(2,1)}) %all-gather.19.cloned.1.call-update) | async-done | bytes 2097168 | tf_op jit(solution)/shard_map/all_gather | solution.py:423
  234.6 10.8 fusion.34
  245.4 70.5 %mixer_forward.1 = (bf16[2,1024,512]{2,1,0:T(8,128)(2,1)S(1)}, bf16[2,2,1024,128]{3,2,1,0:T(8,128)(2,1)S(1)}, bf16[2,1024,512]{2,1,0:T(8,128)(2,1)}, f32[8,2,2,128,256]{4,3,2,1,0:T(8,128)}) custom-call(f32[2,1024,256]{2,1,0:T(8,128)} %bitcast.93, f32[2,1024,256]{2,1,0:T(8,128)} %bitcast.90, f32[2,1024,512]{2,1,0:T(8,128)} %bitcast.87, ...), custom_call_target="tpu_custom_call" | custom-call | tf_op jit(solution)/shard_map/mixer_forward/pallas_call | solution.py:300
  316.8 9.1 convolution_convert_fusion.1
  326.7 69.4 %reduce-scatter.16.cloned.1.call-done = bf16[2048,256]{1,0:T(8,128)(2,1)} async-done(((bf16[2048,2048]{1,0:T(8,128)(2,1)}), bf16[2048,256]{1,0:T(8,128)(2,1)}) %reduce-scatter.16.cloned.1.call-update) | async-done | bytes 1048592 | tf_op jit(solution)/shard_map/reduce_scatter | solution.py:427
  397.8 13.0 psum.78
  415.8 41.2 %all-gather.29.cloned.1.call-done = bf16[2048,704]{0,1:T(8,128)(2,1)} async-done(((bf16[512,704]{0,1:T(8,128)(2,1)}), bf16[2048,704]{0,1:T(8,128)(2,1)}) %all-gather.29.cloned.1.call-update) | async-done | bytes 2883600 | tf_op jit(solution)/shard_map/all_gather | solution.py:423
  457.0 57.3 %all-gather.25.cloned.1.call-done = bf16[2048,2048]{1,0:T(8,128)(2,1)} async-done(((bf16[2048,256]{1,0:T(8,128)(2,1)}), bf16[2048,2048]{1,0:T(8,128)(2,1)}) %all-gather.25.cloned.1.call-update) | async-done | bytes 8388624 | tf_op jit(solution)/shard_map/all_gather | solution.py:419
  514.3 11.0 fusion.38
  525.3 49.7 %all-gather.27.cloned.1.call-done = bf16[2048,704]{0,1:T(8,128)(2,1)} async-done(((bf16[512,704]{0,1:T(8,128)(2,1)}), bf16[2048,704]{0,1:T(8,128)(2,1)}) %all-gather.27.cloned.1.call-update) | async-done | bytes 2883600 | tf_op jit(solution)/shard_map/all_gather | solution.py:423
  575.0 11.0 fusion.37
  586.0 48.5 %all-gather.31.cloned.1.call-done = bf16[704,2048]{1,0:T(8,128)(2,1)} async-done(((bf16[704,512]{1,0:T(8,128)(2,1)}), bf16[704,2048]{1,0:T(8,128)(2,1)}) %all-gather.31.cloned.1.call-update) | async-done | bytes 2883600 | tf_op jit(solution)/shard_map/all_gather | solution.py:423
  634.5 56.6 %all-gather.33.cloned.1.call-done = bf16[2048,2048]{1,0:T(8,128)(2,1)} async-done(((bf16[2048,256]{1,0:T(8,128)(2,1)}), bf16[2048,2048]{1,0:T(8,128)(2,1)}) %all-gather.33.cloned.1.call-update) | async-done | bytes 8388624 | tf_op jit(solution)/shard_map/all_gather | solution.py:419
  691.2 15.3 %multiply_convert_fusion = (bf16[2048,704]{0,1:T(8,128)(2,1)S(1)}, bf16[2048,704]{0,1:T(8,128)(2,1)S(1)}, bf16[2048,704]{0,1:T(8,128)(2,1)}) fusion(f32[2048,704]{0,1:T(8,128)} %fusion.37, f32[2048,704]{0,1:T(8,128)} %fusion.38, bf16[2048,2048]{1,0:T(8,128)(2,1)} %all-gather.33.cloned.1.call-done, bf16[704,2048]{1,0:T(8,128)(2,1)} %all-gather.31.cloned.1.call-done), kind=kOutput, calls=%fused_computation.4 | convolution fusion | flops 5928648704 | bytes 31457280 | tf_op jit(solution)/shard_map/dot_general | solution.py:397
  706.5 10.5 fusion.39
  717.0 12.5 add_convert_fusion.1
  729.6 71.4 %reduce-scatter.20.cloned.1.call-done = bf16[2048,256]{1,0:T(8,128)(2,1)} async-done(((bf16[2048,2048]{1,0:T(8,128)(2,1)}), bf16[2048,256]{1,0:T(8,128)(2,1)}) %reduce-scatter.20.cloned.1.call-update) | async-done | bytes 1048592 | tf_op jit(solution)/shard_map/reduce_scatter | solution.py:427
  803.8 12.9 psum.79
  820.2 10.5 convolution_convert_fusion.4
  832.6 11.2 convolution_convert_fusion.2
  845.6 11.6 convolution_convert_fusion.3
  857.3 18.9 %all-gather.35.cloned.1.call-done = bf16[2048,2048]{1,0:T(8,128)(2,1)} async-done(((bf16[2048,256]{1,0:T(8,128)(2,1)}), bf16[2048,2048]{1,0:T(8,128)(2,1)}) %all-gather.35.cloned.1.call-update) | async-done | bytes 8388624 | tf_op jit(solution)/shard_map/all_gather | solution.py:419
  876.2 9.5 fusion.40
  885.7 55.6 %mixer_backward.1 = (bf16[2,1024,256]{2,1,0:T(8,128)(2,1)}, bf16[2,1024,256]{2,1,0:T(8,128)(2,1)}, bf16[2,1024,512]{2,1,0:T(8,128)(2,1)}, bf16[2,1024,512]{2,1,0...) custom-call(f32[2,1024,512]{2,1,0:T(8,128)} %bitcast.98, ...), custom_call_target="tpu_custom_call" | custom-call | tf_op jit(solution)/shard_map/mixer_backward/pallas_call | solution.py:338
  963.4 9.2 convolution_convert_fusion.5
  972.7 10.1 convolution_convert_fusion.7
  982.8 9.5 convolution_convert_fusion.6
  992.6 13.0 fusion.43
  1005.7 8.2 fusion.41
  1022.0 8.3 fusion.42
  1030.3 25.6 %add_convert_fusion = bf16[2048,2048]{1,0:T(8,128)(2,1)} fusion(f32[2048,2048]{1,0:T(8,128)} %fusion.43, f32[2048,2048]{1,0:T(8,128)} %fusion.42, f32[2048,2048]{1,0:T(8,128)} %fusion.27, f32[2048,2048]{1,0:T(8,128)} %fusion.41, bf16[2048,256]{1,0:T(8,128)(2,1)S(1)} %bitcast.101, bf16[2048,256]{1,0:T(8,128)(2,1)S(1)} %copy-done.15), kind=kOutput, calls=%fused_computation | convolution fusion | flops 2168455168 | bytes 77594624 | tf_op jit(solution)/shard_map/dot_general | solution.py:397
  1057.7 10.9 convolution_convert_fusion
  1077.5 25.9 %reduce-scatter.24.cloned.1.call-done = bf16[512,256]{1,0:T(8,128)(2,1)} async-done(((bf16[2048,256]{1,0:T(8,128)(2,1)}), bf16[512,256]{1,0:T(8,128)(2,1)}) %reduce-scatter.24.cloned.1.call-update) | async-done | bytes 262160 | tf_op jit(solution)/shard_map/reduce_scatter | solution.py:433
  1105.3 26.9 %reduce-scatter.26.cloned.1.call-done = bf16[512,256]{1,0:T(8,128)(2,1)} async-done(((bf16[2048,256]{1,0:T(8,128)(2,1)}), bf16[512,256]{1,0:T(8,128)(2,1)}) %reduce-scatter.26.cloned.1.call-update) | async-done | bytes 262160 | tf_op jit(solution)/shard_map/reduce_scatter | solution.py:433
  1133.9 43.1 %reduce-scatter.32.cloned.1.call-done = bf16[512,512]{1,0:T(8,128)(2,1)} async-done(((bf16[512,2048]{1,0:T(8,128)(2,1)}), bf16[512,512]{1,0:T(8,128)(2,1)}) %reduce-scatter.32.cloned.1.call-update) | async-done | bytes 524304 | tf_op jit(solution)/shard_map/reduce_scatter | solution.py:433
  1179.2 43.9 %reduce-scatter.28.cloned.1.call-done = bf16[512,512]{1,0:T(8,128)(2,1)} async-done(((bf16[2048,512]{1,0:T(8,128)(2,1)}), bf16[512,512]{1,0:T(8,128)(2,1)}) %reduce-scatter.28.cloned.1.call-update) | async-done | bytes 524304 | tf_op jit(solution)/shard_map/reduce_scatter | solution.py:433
  1225.3 43.4 %reduce-scatter.30.cloned.1.call-done = bf16[512,512]{1,0:T(8,128)(2,1)} async-done(((bf16[2048,512]{1,0:T(8,128)(2,1)}), bf16[512,512]{1,0:T(8,128)(2,1)}) %reduce-scatter.30.cloned.1.call-update) | async-done | bytes 524304 | tf_op jit(solution)/shard_map/reduce_scatter | solution.py:433
  1270.8 72.2 %reduce-scatter.22.cloned.1.call-done = bf16[2048,256]{1,0:T(8,128)(2,1)} async-done(((bf16[2048,2048]{1,0:T(8,128)(2,1)}), bf16[2048,256]{1,0:T(8,128)(2,1)}) %reduce-scatter.22.cloned.1.call-update) | async-done | bytes 1048592 | tf_op jit(solution)/shard_map/reduce_scatter | solution.py:427
  1345.4 19.6 %all-reduce.7 = (f32[256]{0:T(256)}, f32[2]{0:T(128)}, f32[4,256]{1,0:T(4,128)}, f32[4,256]{1,0:T(4,128)}, f32[4,512]{1,0:T(4,128)}, /*index=5*/f32[512]{0:T(512)}, f32[256]{0:T(256)}) all-reduce(f32[256]{0:T(256)S(1)} %get-tuple-element.47, f32[2]{0:T(128)S(1)} %get-tuple-element.61, ...), channel_id=1, replica_groups=mesh['row'=4,'col'=8] {'row'}, use_global_device_ids=true, to_apply=%region_13.14 | all-reduce | flops 5122 | bytes 40976 | tf_op jit(solution)/shard_map/psum | solution.py:538
  1364.9 12.3 psum.80
  1377.2 40.6 %reduce-scatter.18.cloned.1.call-done = bf16[2048,256]{1,0:T(8,128)(2,1)} async-done(((bf16[2048,2048]{1,0:T(8,128)(2,1)}), bf16[2048,256]{1,0:T(8,128)(2,1)}) %reduce-scatter.18.cloned.1.call-update) | async-done | bytes 1048592 | tf_op jit(solution)/shard_map/reduce_scatter | solution.py:427
  (226 shorter events, 107.0 us)
Async XLA Ops:
  7.2 75.8 %all-gather.13.cloned.1.call-start = ((), (), s32[]{:S(2)}) async-start(), calls=%async_computation.13 | async-start | bytes 9437184 | tf_op jit(solution)/shard_map/all_gather | solution.py:419
  27.5 85.0 %all-gather.17.cloned.1.call-start = ((), (), s32[]{:S(2)}) async-start(), calls=%async_computation.15 | async-start | bytes 1310720 | tf_op jit(solution)/shard_map/all_gather | solution.py:423
  28.3 113.3 %all-gather.15.cloned.1.call-start = ((), (), s32[]{:S(2)}) async-start(), calls=%async_computation.14 | async-start | bytes 1310720 | tf_op jit(solution)/shard_map/all_gather | solution.py:423
  29.0 159.5 %all-gather.21.cloned.1.call-start = ((), (), s32[]{:S(2)}) async-start(), calls=%async_computation.17 | async-start | bytes 2621440 | tf_op jit(solution)/shard_map/all_gather | solution.py:423
  29.6 205.0 %all-gather.19.cloned.1.call-start = ((), (), s32[]{:S(2)}) async-start(), calls=%async_computation.16 | async-start | bytes 2621440 | tf_op jit(solution)/shard_map/all_gather | solution.py:423
  30.2 286.6 %all-gather.23.cloned.1.call-start = ((), (), s32[]{:S(2)}) async-start(), calls=%async_computation.18 | async-start | bytes 2621440 | tf_op jit(solution)/shard_map/all_gather | solution.py:423
  30.7 365.4 %reduce-scatter.16.cloned.1.call-start = ((), (), s32[]{:S(2)}) async-start(), calls=%async_computation.19 | async-start | bytes 9437184 | tf_op jit(solution)/shard_map/reduce_scatter | solution.py:427
  31.2 88.7 %copy-start.44 = (f32[2]{0:T(128)}, f32[2]{0:T(128)S(1)}, u32[]{:S(2)}) copy-start(f32[2]{0:T(128)S(1)} %exponential_negate_fusion) | copy-start | bytes 28
  120.6 124.7 %copy-start.1 = (f32[2,16,1024]{2,1,0:T(8,128)}, f32[2,16,1024]{2,1,0:T(8,128)S(1)}, u32[]{:S(2)}) copy-start(f32[2,16,1024]{2,1,0:T(8,128)S(1)} %concatenate.42.rows) | copy-start | bytes 393220
  120.9 124.4 %copy-start = (f32[2,1024,16]{2,1,0:T(8,128)}, f32[2,1024,16]{2,1,0:T(8,128)S(1)}, u32[]{:S(2)}) copy-start(f32[2,1024,16]{2,1,0:T(8,128)S(1)} %copy.42.cols) | copy-start | bytes 393220
  325.9 70.3 %copy-start.9 = (bf16[2048,256]{1,0:T(8,128)(2,1)S(1)}, bf16[2048,256]{1,0:T(8,128)(2,1)}, u32[]{:S(2)}) copy-start(bf16[2048,256]{1,0:T(8,128)(2,1)} %param.20) | copy-start | bytes 3145732
  325.9 84.9 %copy-start.37 = (f32[256]{0:T(256)S(1)}, f32[256]{0:T(256)}, u32[]{:S(2)}) copy-start(f32[256]{0:T(256)} %param.36) | copy-start | bytes 3076
  325.9 131.1 %all-gather.29.cloned.1.call-start = ((), (), s32[]{:S(2)}) async-start(), calls=%async_computation.22 | async-start | bytes 3604480 | tf_op jit(solution)/shard_map/all_gather | solution.py:423
  326.7 187.6 %all-gather.25.cloned.1.call-start = ((), (), s32[]{:S(2)}) async-start(), calls=%async_computation.20 | async-start | bytes 9437184 | tf_op jit(solution)/shard_map/all_gather | solution.py:419
  410.8 405.9 %copy-start.23 = (f32[2048]{0:T(1024)}, f32[2048]{0:T(1024)S(1)}, u32[]{:S(2)}) copy-start(f32[2048]{0:T(1024)S(1)} %add_rsqrt_fusion) | copy-start | bytes 24580
  413.5 161.5 %all-gather.27.cloned.1.call-start = ((), (), s32[]{:S(2)}) async-start(), calls=%async_computation.21 | async-start | bytes 3604480 | tf_op jit(solution)/shard_map/all_gather | solution.py:423
  414.0 220.5 %all-gather.31.cloned.1.call-start = ((), (), s32[]{:S(2)}) async-start(), calls=%async_computation.23 | async-start | bytes 3604480 | tf_op jit(solution)/shard_map/all_gather | solution.py:423
  414.8 276.4 %all-gather.33.cloned.1.call-start = ((), (), s32[]{:S(2)}) async-start(), calls=%async_computation.25 | async-start | bytes 9437184 | tf_op jit(solution)/shard_map/all_gather | solution.py:419
  415.4 385.6 %reduce-scatter.20.cloned.1.call-start = ((), (), s32[]{:S(2)}) async-start(), calls=%async_computation.26 | async-start | bytes 9437184 | tf_op jit(solution)/shard_map/reduce_scatter | solution.py:427
  729.5 71.5 %copy-start.11 = (bf16[2048,256]{1,0:T(8,128)(2,1)S(1)}, bf16[2048,256]{1,0:T(8,128)(2,1)}, u32[]{:S(2)}) copy-start(bf16[2048,256]{1,0:T(8,128)(2,1)} %reduce-scatter.16.cloned.1.call-done) | copy-start | bytes 3145732
  729.5 87.8 %copy-start.13 = (bf16[2048,256]{1,0:T(8,128)(2,1)S(1)}, bf16[2048,256]{1,0:T(8,128)(2,1)}, u32[]{:S(2)}) copy-start(bf16[2048,256]{1,0:T(8,128)(2,1)} %param.22) | copy-start | bytes 3145732
  729.5 146.6 %all-gather.35.cloned.1.call-start = ((), (), s32[]{:S(2)}) async-start(), calls=%async_computation.27 | async-start | bytes 9437184 | tf_op jit(solution)/shard_map/all_gather | solution.py:419
  820.1 248.6 %reduce-scatter.38.cloned.1.call-start = ((), (), s32[]{:S(2)}) async-start(), calls=%async_computation.36 | async-start | bytes 3604480 | tf_op jit(solution)/shard_map/reduce_scatter | solution.py:433
  830.7 240.4 %reduce-scatter.36.cloned.1.call-start = ((), (), s32[]{:S(2)}) async-start(), calls=%async_computation.35 | async-start | bytes 3604480 | tf_op jit(solution)/shard_map/reduce_scatter | solution.py:433
  843.8 229.7 %reduce-scatter.34.cloned.1.call-start = ((), (), s32[]{:S(2)}) async-start(), calls=%async_computation.34 | async-start | bytes 3604480 | tf_op jit(solution)/shard_map/reduce_scatter | solution.py:433
  857.2 218.7 %reduce-scatter.40.cloned.1.call-start = ((), (), s32[]{:S(2)}) async-start(), calls=%async_computation.37 | async-start | bytes 655360
  885.7 57.2 %copy-start.45 = (f32[2]{0:T(128)S(1)}, f32[2]{0:T(128)}, u32[]{:S(2)}) copy-start(f32[2]{0:T(128)} %copy-done.44) | copy-start | bytes 28
  948.8 154.7 %reduce-scatter.24.cloned.1.call-start = ((), (), s32[]{:S(2)}) async-start(), calls=%async_computation.29 | async-start | bytes 1310720 | tf_op jit(solution)/shard_map/reduce_scatter | solution.py:433
  956.1 176.0 %reduce-scatter.26.cloned.1.call-start = ((), (), s32[]{:S(2)}) async-start(), calls=%async_computation.30 | async-start | bytes 1310720 | tf_op jit(solution)/shard_map/reduce_scatter | solution.py:433
  963.3 213.7 %reduce-scatter.32.cloned.1.call-start = ((), (), s32[]{:S(2)}) async-start(), calls=%async_computation.33 | async-start | bytes 2621440 | tf_op jit(solution)/shard_map/reduce_scatter | solution.py:433
  972.6 250.6 %reduce-scatter.28.cloned.1.call-start = ((), (), s32[]{:S(2)}) async-start(), calls=%async_computation.31 | async-start | bytes 2621440 | tf_op jit(solution)/shard_map/reduce_scatter | solution.py:433
  982.8 285.9 %reduce-scatter.30.cloned.1.call-start = ((), (), s32[]{:S(2)}) async-start(), calls=%async_computation.32 | async-start | bytes 2621440 | tf_op jit(solution)/shard_map/reduce_scatter | solution.py:433
  992.4 350.7 %reduce-scatter.22.cloned.1.call-start = ((), (), s32[]{:S(2)}) async-start(), calls=%async_computation.28 | async-start | bytes 9437184 | tf_op jit(solution)/shard_map/reduce_scatter | solution.py:427
  1055.9 361.9 %reduce-scatter.18.cloned.1.call-start = ((), (), s32[]{:S(2)}) async-start(), calls=%async_computation.24 | async-start | bytes 9437184 | tf_op jit(solution)/shard_map/reduce_scatter | solution.py:427
  1105.3 237.8 %copy-start.10 = (bf16[2048,256]{1,0:T(8,128)(2,1)S(1)}, bf16[2048,256]{1,0:T(8,128)(2,1)}, u32[]{:S(2)}) copy-start(bf16[2048,256]{1,0:T(8,128)(2,1)} %param.20) | copy-start | bytes 3145732
  1105.3 237.8 %copy-start.32 = (f32[2048]{0:T(1024)S(1)}, f32[2048]{0:T(1024)}, u32[]{:S(2)}) copy-start(f32[2048]{0:T(1024)} %copy-done.31) | copy-start | bytes 24580
  1105.3 237.8 %copy-start.39 = (f32[256]{0:T(256)S(1)}, f32[256]{0:T(256)}, u32[]{:S(2)}) copy-start(f32[256]{0:T(256)} %param.23) | copy-start | bytes 3076
  1179.1 166.2 %copy-start.40 = (f32[4,512]{1,0:T(4,128)S(1)}, f32[4,512]{1,0:T(4,128)}, u32[]{:S(2)}) copy-start(f32[4,512]{1,0:T(4,128)} %get-tuple-element.43) | copy-start | bytes 24580
  1179.1 166.2 %copy-start.41 = (f32[256]{0:T(256)S(1)}, f32[256]{0:T(256)}, u32[]{:S(2)}) copy-start(f32[256]{0:T(256)} %get-tuple-element.45) | copy-start | bytes 3076
  1179.1 166.2 %copy-start.42 = (f32[4,256]{1,0:T(4,128)S(1)}, f32[4,256]{1,0:T(4,128)}, u32[]{:S(2)}) copy-start(f32[4,256]{1,0:T(4,128)} %get-tuple-element.41) | copy-start | bytes 12292
  1179.1 166.2 %copy-start.43 = (f32[4,256]{1,0:T(4,128)S(1)}, f32[4,256]{1,0:T(4,128)}, u32[]{:S(2)}) copy-start(f32[4,256]{1,0:T(4,128)} %get-tuple-element.42) | copy-start | bytes 12292
  1179.1 166.2 %copy-start.48 = (f32[1,512]{1,0:T(1,128)S(1)}, f32[1,512]{1,0:T(1,128)}, u32[]{:S(2)}) copy-start(f32[1,512]{1,0:T(1,128)} %get-tuple-element.44) | copy-start | bytes 6148
  1179.2 198.0 %copy-start.34 = (f32[2048]{0:T(1024)S(1)}, f32[2048]{0:T(1024)}, u32[]{:S(2)}) copy-start(f32[2048]{0:T(1024)} %copy-done.33) | copy-start | bytes 24580
  1179.2 238.7 %copy-start.12 = (bf16[2048,256]{1,0:T(8,128)(2,1)S(1)}, bf16[2048,256]{1,0:T(8,128)(2,1)}, u32[]{:S(2)}) copy-start(bf16[2048,256]{1,0:T(8,128)(2,1)} %reduce-scatter.16.cloned.1.call-done) | copy-start | bytes 3145732
  1179.2 238.7 %copy-start.14 = (bf16[2048,256]{1,0:T(8,128)(2,1)S(1)}, bf16[2048,256]{1,0:T(8,128)(2,1)}, u32[]{:S(2)}) copy-start(bf16[2048,256]{1,0:T(8,128)(2,1)} %param.22) | copy-start | bytes 3145732
  1179.2 238.7 %copy-start.24 = (f32[2048]{0:T(1024)S(1)}, f32[2048]{0:T(1024)}, u32[]{:S(2)}) copy-start(f32[2048]{0:T(1024)} %copy-done.23) | copy-start | bytes 24580
  1179.2 238.7 %copy-start.36 = (f32[2048]{0:T(1024)S(1)}, f32[2048]{0:T(1024)}, u32[]{:S(2)}) copy-start(f32[2048]{0:T(1024)} %copy-done.35) | copy-start | bytes 24580
  1179.2 238.6 %copy-start.38 = (f32[256]{0:T(256)S(1)}, f32[256]{0:T(256)}, u32[]{:S(2)}) copy-start(f32[256]{0:T(256)} %param.36) | copy-start | bytes 3076
  (38 other events, 716.2 us)
Sparse Core Ops, SparseCore 0:
  27.6 55.3 all-gather.12
  84.6 27.9 all-gather.16
  114.1 27.4 all-gather.14
  143.0 45.4 all-gather.20
  189.9 44.6 all-gather.18
  236.0 44.6 all-gather.22
  326.1 70.0 reduce-scatter.15
  397.8 59.1 all-gather.28
  459.6 54.6 all-gather.24
  515.8 59.1 all-gather.26
  576.6 57.8 all-gather.30
  636.4 54.6 all-gather.32
  729.6 71.3 reduce-scatter.19
  820.2 55.8 all-gather.34
  878.3 56.1 reduce-scatter.37
  936.7 56.0 reduce-scatter.35
  994.9 56.0 reduce-scatter.33
  1053.7 21.4 reduce-scatter.39
  1078.1 25.3 reduce-scatter.23
  1106.3 25.7 reduce-scatter.25
  1134.4 42.4 reduce-scatter.31
  1180.0 43.1 reduce-scatter.27
  1225.5 43.1 reduce-scatter.29
  1272.4 70.6 reduce-scatter.21
  1346.5 71.2 reduce-scatter.17

commit v2 on v1

--- a/solution.py
+++ b/solution.py
@@ -156,7 +156,7 @@
     row, col = iotas(CHUNK)
     lower = row >= col
     tril = lower.astype(bf16)
-    lane = lax.broadcasted_iota(jnp.int32, (CHUNK, 2 * heads), 1)
+    lane = lax.broadcasted_iota(jnp.int32, (CHUNK, 2 * heads + 1), 1)
     last = lax.broadcasted_iota(jnp.int32, (CHUNK, 1), 0) == CHUNK - 1
     for s in range(seqs):
         cc = cols[s]
@@ -175,7 +175,8 @@
             pres.append(conv_taps(buf, s, None, weights, masks))
         sigs = [sigmoid(pre) for pre in pres]
         acts = [pre * sig for pre, sig in zip(pres, sigs)]
-        dcol = jnp.zeros((CHUNK, 2 * heads), f32)
+        dcol = jnp.zeros((CHUNK, 2 * heads + 1), f32)
+        weigh = jnp.zeros((CHUNK, 1), f32)
         for h in range(heads):
             keys = slice(h * DK, (h + 1) * DK)
             vals = slice(h * DV, (h + 1) * DV)
@@ -218,7 +219,9 @@
             dyn = dy * scaled
             gains = gain[:, vals]
             dgain[:, vals] += jnp.sum(dyn * silu, axis=0, keepdims=True)
-            dpg[s, :, vals] = (dyn * gains * (sg * (1.0 + gate * (1.0 - sg)))).astype(bf16)
+            dgate = dyn * gains * (sg * (1.0 + gate * (1.0 - sg)))
+            dpg[s, :, vals] = dgate.astype(bf16)
+            weigh = weigh + jnp.sum(dgate * gate, axis=1, keepdims=True)
             dscaled = dy * gains * silu
             dmixed = rm * (dscaled - scaled * jnp.mean(dscaled * scaled, axis=1, keepdims=True))
             dout = (dmixed * SCALE)
@@ -270,7 +273,6 @@
         dl2 = (dcol - dh.astype(f32) - dl.astype(f32)).astype(bf16)
         tail = ((0,), (0,))
         rev = mm(tril, dh, tail) + (mm(tril, dl, tail) + mm(tril, dl2, tail))
-        dcols[s] = jnp.where(lane < heads, dcol, rev)
         for buf, src, out, weights, dw in ((tq, bq, dpq, wq, dwq), (tk, bk, dpk, wk, dwk), (tv, bv, dpv, wv, dwv)):
             pre = buf[s, 0:CHUNK, :]
             total = weights[0:1] * pre
@@ -281,7 +283,9 @@
                     pre * masks[j - 1] * src[s, 8 - j : 8 - j + CHUNK, :], axis=0, keepdims=True
                 )
             out[s] = total.astype(bf16)
+            weigh = weigh + jnp.sum(total * src[s, 8 : 8 + CHUNK, :], axis=1, keepdims=True)
             buf[s, CHUNK : CHUNK + 8, :] = buf[s, 0:8, :]
+        dcols[s] = jnp.where(lane < heads, dcol, jnp.where(lane < 2 * heads, rev, weigh))
 
 
 def whole(shape):
@@ -344,13 +348,13 @@
                   tok(vw),
                   pl.BlockSpec((1, seqs, heads, DK, DV), lambda c: (steps - 1 - c, 0, 0, 0, 0)),
                   whole((CONV, kw)), whole((CONV, kw)), whole((CONV, vw)), whole((1, vw))],
-        out_specs=[tok(kw), tok(kw), tok(vw), tok(vw), tok(2 * heads),
+        out_specs=[tok(kw), tok(kw), tok(vw), tok(vw), tok(2 * heads + 1),
                    whole((CONV, kw)), whole((CONV, kw)), whole((CONV, vw)), whole((1, vw))],
         out_shape=[jax.ShapeDtypeStruct((seqs, SEQ, kw), bf16),
                    jax.ShapeDtypeStruct((seqs, SEQ, kw), bf16),
                    jax.ShapeDtypeStruct((seqs, SEQ, vw), bf16),
                    jax.ShapeDtypeStruct((seqs, SEQ, vw), bf16),
-                   jax.ShapeDtypeStruct((seqs, SEQ, 2 * heads), f32),
+                   jax.ShapeDtypeStruct((seqs, SEQ, 2 * heads + 1), f32),
                    jax.ShapeDtypeStruct((CONV, kw), f32),
                    jax.ShapeDtypeStruct((CONV, kw), f32),
                    jax.ShapeDtypeStruct((CONV, vw), f32),
@@ -386,53 +390,390 @@
     rows = jnp.concatenate(tables, axis=1)
     return rows, jnp.swapaxes(rows, 1, 2)
 
+TILE = 256
+MESH = pl.DeviceIdType.MESH
+
+
+def flip(value, bits):
+    bit = 1
+    while bit <= bits:
+        if bits & bit:
+            value = value + bit - 2 * bit * ((value // bit) % 2)
+        bit *= 2
+    return value
+
+
+class Grid:
+    def __init__(self):
+        self.rows = lax.axis_size("row")
+        self.cols = lax.axis_size("col")
+        self.shard = D // self.rows
+        self.block = D // self.cols
+        self.parts = self.cols // self.rows
+        self.half = self.cols // 2
+        self.me = lax.axis_index("col")
+        self.at = lax.axis_index("row")
+        self.ids = jnp.stack([self.me, self.at]).astype(jnp.int32)
+        self.slots = list(range(0, self.cols, 2)) + list(range(1, self.cols, 2))
+
+    def swap(self, values, axis, bits):
+        count = self.rows if axis == "row" else self.cols
+        return lax.ppermute(values, axis, [(i, i ^ bits) for i in range(count)])
+
+    def total(self, values, axis):
+        bits = 1
+        while bits < (self.rows if axis == "row" else self.cols):
+            values = values + self.swap(values, axis, bits)
+            bits *= 2
+        return values
+
+    def gather_cols(self, values):
+        same = [values] + [self.swap(values, "col", k) for k in range(2, self.cols, 2)]
+        return same + [self.swap(v, "col", 1) for v in same]
+
+    def gather_rows(self, values):
+        return lax.all_gather(values, "row", axis=0, tiled=True)
+
+    def sum_rows(self, term, axis):
+        return lax.psum_scatter(term.astype(bf16), "row", scatter_dimension=axis, tiled=True).astype(f32)
+
+
+def fixed(array):
+    return pl.BlockSpec(array.shape, lambda i, ids: (0,) * array.ndim, pipeline_mode=pl.Buffered(1))
+
+
+def tokens_of(width, tile=TILE):
+    return pl.BlockSpec((tile, width), lambda i, ids: (i, 0))
+
+
+def cost(flops, operands, outs):
+    moved = sum(o.size * o.dtype.itemsize for o in operands)
+    moved += sum(o.size * o.dtype.itemsize for o in outs)
+    return pl.CostEstimate(flops=flops, bytes_accessed=moved, transcendentals=0)
+
+
+def launch(kernel, grid, ids, operands, in_specs, out_specs, out_shape, scratch, name, flops):
+    return pl.pallas_call(
+        kernel,
+        grid_spec=pltpu.PrefetchScalarGridSpec(
+            num_scalar_prefetch=1, grid=grid, in_specs=in_specs, out_specs=out_specs, scratch_shapes=scratch
+        ),
+        out_shape=out_shape,
+        compiler_params=pltpu.CompilerParams(
+            dimension_semantics=("arbitrary",) * len(grid), vmem_limit_bytes=56 << 20
+        ),
+        cost_estimate=cost(flops, operands, out_shape),
+        name=name,
+    )(ids, *operands)
+
+
+def place(g, ids, k):
+    return pl.multiple_of((ids[0] ^ k) * g.block, g.block)
+
+
+def dot_back(g, x, weights):
+    return sum(
+        mm(x[:, s * g.shard : (s + 1) * g.shard], weights[s], ((1,), (1,))) for s in range(g.rows)
+    )
+
+
+def project_kernel(g, widths, ids, *refs):
+    blocks, refs = refs[: g.cols], refs[g.cols :]
+    gain, weight, small_weight, normed, scale, pq, pk, pv, pg, small = refs
+    values = [b[...].astype(f32) for b in blocks]
+    squares = sum(jnp.sum(v * v, axis=1, keepdims=True) for v in values)
+    scales = lax.rsqrt(squares / D + EPSILON)
+    scale[...] = scales
+    for k, v in zip(g.slots, values):
+        at = place(g, ids, k)
+        normed[:, pl.ds(at, g.block)] = (v * scales * gain[:, pl.ds(at, g.block)]).astype(bf16)
+    x = normed[...]
+    at = 0
+    for out, width in zip((pq, pk, pv, pg), widths):
+        out[...] = mm(x, weight[:, at : at + width])
+        at += width
+    small[...] = mm(small_weight[...], x, ((1,), (1,)))
+
+
+def project(g, blocks, gains, weight, small_weight, widths):
+    tokens = blocks[0].shape[0]
+    few = small_weight.shape[0]
+    return launch(
+        functools.partial(project_kernel, g, widths),
+        (tokens // TILE,),
+        g.ids,
+        blocks + [gains, weight, small_weight],
+        [tokens_of(g.block)] * g.cols + [fixed(gains), fixed(weight), fixed(small_weight)],
+        [tokens_of(D), tokens_of(1)] + [tokens_of(w) for w in widths] + [pl.BlockSpec((few, TILE), lambda i, ids: (0, i))],
+        [jax.ShapeDtypeStruct((tokens, D), bf16), jax.ShapeDtypeStruct((tokens, 1), f32)]
+        + [jax.ShapeDtypeStruct((tokens, w), f32) for w in widths]
+        + [jax.ShapeDtypeStruct((few, tokens), f32)],
+        [],
+        "project",
+        2 * tokens * D * (sum(widths) + few),
+    )
+
+
+def ffn_kernel(g, ids, *refs):
+    xs, refs = refs[0], refs[1:]
+    ts, refs = refs[: g.cols], refs[g.cols :]
+    undo, wg, wu, wd, xr, tr, inner, dgate, dup, total, scale = refs
+    squares = 0.0
+    for k, t in zip(g.slots, ts):
+        at = place(g, ids, k)
+        x = xs[k]
+        xr[:, pl.ds(at, g.block)] = x
+        tr[:, pl.ds(at, g.block)] = t[...]
+        v = x.astype(f32)
+        squares = squares + jnp.sum(v * v * undo[:, pl.ds(at, g.block)], axis=1, keepdims=True)
+    scales = lax.rsqrt(squares / D + EPSILON)
+    scale[...] = scales
+    x = xr[...]
+    gate = mm(x, wg[...]) * scales
+    up = mm(x, wu[...]) * scales
+    grad = dot_back(g, tr, wd)
+    sig = sigmoid(gate)
+    silu = gate * sig
+    inner[...] = (silu * up).astype(bf16)
+    dg = grad * up * (sig * (1.0 + gate * (1.0 - sig)))
+    du = grad * silu
+    total[...] = jnp.sum(dg * gate + du * up, axis=1, keepdims=True)
+    dgate[...] = (dg * scales).astype(bf16)
+    dup[...] = (du * scales).astype(bf16)
+
+
+def ffn(g, xs, ts, undo, wg, wu, wd):
+    tokens = xs.shape[1]
+    width = wg.shape[1]
+    return launch(
+        functools.partial(ffn_kernel, g),
+        (tokens // TILE,),
+        g.ids,
+        [xs] + ts + [undo, wg, wu, wd],
+        [pl.BlockSpec((g.cols, TILE, g.block), lambda i, ids: (0, i, 0))]
+        + [tokens_of(g.block)] * g.cols
+        + [fixed(w) for w in (undo, wg, wu, wd)],
+        [tokens_of(D)] * 2 + [tokens_of(width)] * 3 + [tokens_of(1)] * 2,
+        [jax.ShapeDtypeStruct((tokens, D), bf16)] * 2
+        + [jax.ShapeDtypeStruct((tokens, width), bf16)] * 3
+        + [jax.ShapeDtypeStruct((tokens, 1), f32)] * 2,
+        [],
+        "ffn",
+        6 * tokens * D * width,
+    )
+
+
+def back_gate_kernel(g, ids, ms, wo, mr, out):
+    for k in g.slots:
+        mr[:, pl.ds(place(g, ids, k), g.block)] = ms[k]
+    out[...] = dot_back(g, mr, wo)
+
+
+def back_gate(g, ms, wo):
+    tokens = ms.shape[1]
+    width = wo.shape[1]
+    return launch(
+        functools.partial(back_gate_kernel, g),
+        (tokens // TILE,),
+        g.ids,
+        [ms, wo],
+        [pl.BlockSpec((g.cols, TILE, g.block), lambda i, ids: (0, i, 0)), fixed(wo)],
+        [tokens_of(D), tokens_of(width)],
+        [jax.ShapeDtypeStruct((tokens, D), bf16), jax.ShapeDtypeStruct((tokens, width), f32)],
+        [],
+        "back_gate",
+        2 * tokens * D * width,
+    )
+
+
+class Sizes:
+    def __init__(self, cols, block, parts, shard):
+        self.cols, self.block, self.parts, self.shard = cols, block, parts, shard
+        self.half = cols // 2
+
+
+def piece(z, kind, y, weight, owner):
+    if kind == "rows":
+        return mm(y, weight[pl.ds(pl.multiple_of(owner * z.block, z.block), z.block), :], ((1,), (1,)))
+    part = pl.multiple_of((owner % z.parts) * z.block, z.block)
+    return mm(y, weight[owner // z.parts, :, pl.ds(part, z.block)])
+
+
+def exchange_kernel(z, kinds, finish, gathers, extras, outs, steps, tile, *refs):
+    count = len(kinds)
+    ys, refs = refs[:count], refs[count:]
+    ws, refs = refs[:count], refs[count:]
+    extra, refs = refs[:extras], refs[extras:]
+    out, refs = refs[:outs], refs[outs:]
+    if gathers:
+        slots, refs = refs[0], refs[1:]
+    near, far, far_got, pair, pair_got, refs = *refs[:5], refs[5:]
+    far_s, far_r, pair_s, pair_r, refs = *refs[:4], refs[4:]
+    if gathers:
+        block, own_s, same_s, same_r, turn_s, turn_r, part_s, part_r = refs
+    me = lax.axis_index("col")
+    partner = flip(me, 1)
+    peers = [flip(me, 2 * j) for j in range(1, z.half)]
+
+    barrier = pltpu.get_barrier_semaphore()
+    for device in [partner] + peers:
+        pl.semaphore_signal(barrier, inc=1, device_id={"col": device}, device_id_type=MESH)
+    pl.semaphore_wait(barrier, z.half)
+
+    def remote(source, target, send, receive, device):
+        return pltpu.make_async_remote_copy(
+            src_ref=source, dst_ref=target, send_sem=send, recv_sem=receive,
+            device_id={"col": device}, device_id_type=MESH,
+        )
+
+    def rows_at(i):
+        return pl.ds(pl.multiple_of(i * tile, tile), tile)
+
+    def send_far(i):
+        return remote(far.at[i], far_got.at[i], far_s.at[i], far_r.at[i], partner)
+
+    def send_pair(i, j):
+        return remote(pair.at[i, j], pair_got.at[i, j], pair_s.at[i, j], pair_r.at[i, j], peers[j - 1])
+
+    def keep(i):
+        return pltpu.make_async_copy(block.at[i], slots.at[0, rows_at(i), :], own_s.at[i])
+
+    def send_part(i):
+        return remote(block.at[i], slots.at[1, rows_at(i), :], part_s.at[i], part_r.at[i], partner)
+
+    def send_same(i, j):
+        return remote(block.at[i], slots.at[2 * j, rows_at(i), :], same_s.at[i, j], same_r.at[i, j], peers[j - 1])
+
+    def send_turn(i, j):
+        return remote(
+            slots.at[2 * j, rows_at(i), :], slots.at[2 * j + 1, rows_at(i), :],
+            turn_s.at[i, j], turn_r.at[i, j], partner,
+        )
+
+    lag = 4 if gathers else 3
+
+    @pl.loop(0, steps + lag - 1)
+    def _(it):
+        @pl.when(it < steps)
+        def _():
+            tiles = [y[rows_at(it), :] for y in ys]
+            for side, held in ((1, far), (0, near)):
+                for j in range(z.half):
+                    owner = flip(me, 2 * j + side)
+                    total = sum(piece(z, kind, y, w, owner) for kind, y, w in zip(kinds, tiles, ws))
+                    held[it, j] = total.astype(bf16)
+                if side == 1:
+                    send_far(it).start()
+
+        @pl.when((it >= 1) & (it < steps + 1))
+        def _():
+            i = it - 1
+            send_far(i).wait_recv()
+            for j in range(1, z.half):
+                pair[i, j] = (near[i, j].astype(f32) + far_got[i, j].astype(f32)).astype(bf16)
+                send_pair(i, j).start()
+
+        @pl.when((it >= 2) & (it < steps + 2))
+        def _():
+            i = it - 2
+            total = near[i, 0].astype(f32) + far_got[i, 0].astype(f32)
+            for j in range(1, z.half):
+                send_pair(i, j).wait_recv()
+                total = total + pair_got[i, j].astype(f32)
+            result = finish(rows_at(i), i, total, extra, out)
+            if gathers:
+                block[i] = result
+                for j in range(1, z.half):
+                    send_same(i, j).start()
+                send_part(i).start()
+                keep(i).start()
+
+        if gathers:
+            @pl.when(it >= 3)
+            def _():
+                i = it - 3
+                for j in range(1, z.half):
+                    send_same(i, j).wait_recv()
+                    send_turn(i, j).start()
+
+    @pl.loop(0, steps)
+    def _(i):
+        send_far(i).wait_send()
+        for j in range(1, z.half):
+            send_pair(i, j).wait_send()
+        if gathers:
+            keep(i).wait()
+            send_part(i).wait()
+            for j in range(1, z.half):
+                send_same(i, j).wait_send()
+                send_turn(i, j).wait()
+
+
+def finish_middle(rows, i, total, extra, out):
+    hidden, gain = extra
+    middle = hidden[rows, :].astype(f32) + total
+    out[0][rows, :] = middle
+    return (middle * gain[...]).astype(bf16)
+
+
+def finish_gradient(rows, i, total, extra, out):
+    top, middle, gain, weigh = extra
+    before = middle[rows, :]
+    grad = top[rows, :].astype(f32) + gain[...] * total - before * weigh[rows, :]
+    out[0][rows, :] = grad
+    out[1][i] = jnp.sum(total * before, axis=0, keepdims=True)
+    return grad.astype(bf16)
+
+
+def finish_input(rows, i, total, extra, out):
+    above, hidden, gain, scale, weigh = extra
+    before = hidden[rows, :].astype(f32)
+    scaled = scale[rows, :] * total
+    out[0][rows, :] = above[rows, :] + gain[...] * scaled - before * weigh[rows, :]
+    out[1][i] = jnp.sum(scaled * before, axis=0, keepdims=True)
+
+
+def finish_out(rows, i, total, extra, out):
+    (middle,) = extra
+    out[0][rows, :] = (middle[rows, :] + total).astype(bf16)
+
+
+def exchange(z, kinds, ys, ws, finish, extras, outs, gathers, number, tile=TILE):
+    tokens = ys[0].shape[0]
+    steps = tokens // tile
+    half, block = z.half, z.block
+    vmem = pl.BlockSpec(memory_space=pltpu.VMEM)
+    shapes = list(outs)
+    specs = [vmem] * len(outs)
+    wide = (steps, half, tile, block)
+    dma = pltpu.SemaphoreType.DMA
+    scratch = [pltpu.VMEM(wide, bf16)] * 5
+    scratch += [dma((steps,))] * 2 + [dma((steps, half))] * 2
+    if gathers:
+        shapes.append(jax.ShapeDtypeStruct((z.cols, tokens, block), bf16))
+        specs.append(pl.BlockSpec(memory_space=pl.ANY))
+        scratch += [pltpu.VMEM((steps, tile, block), bf16), dma((steps,))]
+        scratch += [dma((steps, half))] * 4 + [dma((steps,))] * 2
+    operands = [*ys, *ws, *extras]
+    depth = sum(y.shape[1] for y in ys)
+    return pl.pallas_call(
+        functools.partial(exchange_kernel, z, kinds, finish, gathers, len(extras), len(outs), steps, tile),
+        in_specs=[vmem] * len(operands),
+        out_specs=specs,
+        out_shape=shapes,
+        scratch_shapes=scratch,
+        compiler_params=pltpu.CompilerParams(
+            collective_id=number, has_side_effects=True, vmem_limit_bytes=58 << 20
+        ),
+        cost_estimate=cost(2 * tokens * z.cols * block * depth + 50 * 10**9, operands, shapes),
+        name="exchange",
+    )(*operands)
+
 
 def rows_product(first_op, second_op):
     return lax.dot_general(
         first_op, second_op, (((0,), (0,)), ((), ())), preferred_element_type=f32
     )
-
-
-def cols_product(first_op, second_op):
-    return lax.dot_general(
-        first_op, second_op, (((1,), (1,)), ((), ())), preferred_element_type=f32
-    )
-
-
-def shard_norm(values, gains):
-    squares = lax.psum(jnp.sum(values * values, axis=1), "col")
-    scales = lax.rsqrt(squares / D + EPSILON)
-    return (scales, values * scales[:, None] * gains)
-
-
-def shard_norm_back(values, gains, scales, grad_out):
-    weighted = grad_out * gains
-    totals = lax.psum(jnp.sum(weighted * values, axis=1), "col")
-    grad_values = (
-        scales[:, None] * weighted - values * (scales * scales * scales * totals / D)[:, None]
-    )
-    grad_gains = jnp.sum(grad_out * values * scales[:, None], axis=0)
-    return (grad_values, grad_gains)
-
-
-def gather_cols(values):
-    return lax.all_gather(values, "col", axis=1, tiled=True)
-
-
-def gather_rows(values, axis):
-    return lax.all_gather(values, "row", axis=axis, tiled=True)
-
-
-def sum_columns(term):
-    return lax.psum_scatter(
-        term.astype(bf16), "col", scatter_dimension=1, tiled=True
-    ).astype(f32)
-
-
-def sum_rows(term, axis):
-    return lax.psum_scatter(
-        term.astype(bf16), "row", scatter_dimension=axis, tiled=True
-    ).astype(f32)
 
 
 def on_device(
@@ -457,9 +798,13 @@
     w_ffn_up,
     w_ffn_down,
 ):
+    g = Grid()
+    z = Sizes(g.cols, g.block, g.parts, g.shard)
     tokens = seg_ids.shape[0]
     seqs = tokens // SEQ
     heads = decay_log.shape[0]
+    local = jax.ShapeDtypeStruct((tokens, g.block), f32)
+    sums = jax.ShapeDtypeStruct((tokens // TILE, 1, g.block), f32)
 
     def by_seq(values):
         return values.reshape(seqs, SEQ, values.shape[1])
@@ -467,94 +812,103 @@
     def flat(values):
         return values.reshape(tokens, values.shape[2])
 
-    small_in = gather_rows(jnp.concatenate([w_beta, w_decay], axis=1).T, 1)
-    full = [gather_rows(w, 0) for w in (w_query, w_key, w_value, w_gate)]
-    full_out = gather_rows(w_out, 1)
-    full_gate = gather_rows(w_ffn_gate, 0)
-    full_up = gather_rows(w_ffn_up, 0)
-    full_down = gather_rows(w_ffn_down, 1)
-
-    hidden = hidden_in.astype(f32)
-    scale_mixer, normed_shard = shard_norm(hidden, norm_mixer)
-    normed = gather_cols(normed_shard.astype(bf16))
-    projected = [by_seq(jnp.dot(normed, w, preferred_element_type=f32)) for w in full]
-    proj_small = cols_product(small_in, normed)
+    ins = (w_query, w_key, w_value, w_gate)
+    widths = [w.shape[1] for w in ins]
+    inw = g.gather_rows(jnp.concatenate(ins, axis=1))
+    ow = g.gather_rows(w_out[None])
+    ew, uw = g.gather_rows(w_ffn_gate), g.gather_rows(w_ffn_up)
+    dw = g.gather_rows(w_ffn_down[None])
+    few = 2 * heads
+    small_own = jnp.concatenate([w_beta, w_decay], axis=1).T
+    small_in = g.total(
+        lax.dynamic_update_slice(jnp.zeros((few, D), bf16), small_own, (0, g.at * g.shard)), "row"
+    )
+    gains = jnp.zeros((2, D), f32)
+    gains = lax.dynamic_update_slice(gains, jnp.stack([norm_mixer, norm_ffn]), (0, g.me * g.block))
+    gains = g.total(gains, "col")
+    blocks = g.gather_cols(hidden_in)
+    tops = g.gather_cols(cotangent)
+
+    normed, scale_mixer, pq, pk, pv, pg, proj_small = project(g, blocks, gains[:1], inw, small_in, widths)
+    projected = [by_seq(p) for p in (pq, pk, pv, pg)]
     proj_beta, proj_decay = proj_small[:heads], proj_small[heads:]
     strength = jax.nn.sigmoid(proj_beta)
     rate = -jnp.exp(decay_log)[:, None]
     log_decay = rate * jax.nn.softplus(proj_decay)
     rows, cols = token_tables(seg_ids, strength, log_decay)
-    gains = norm_gated[None]
+    gain_gated = norm_gated[None]
     gated, inv, upd, states = mixer_forward(
-        *projected, cols, rows, conv_query, conv_key, conv_value, gains
+        *projected, cols, rows, conv_query, conv_key, conv_value, gain_gated
     )
     gated = flat(gated)
-    middle = hidden + sum_columns(jnp.dot(gated, full_out, preferred_element_type=f32))
-    scale_ffn, normed_mid = shard_norm(middle, norm_ffn)
-    normed_ffn = gather_cols(normed_mid.astype(bf16))
-    gate_pre = jnp.dot(normed_ffn, full_gate, preferred_element_type=f32)
-    up_pre = jnp.dot(normed_ffn, full_up, preferred_element_type=f32)
-    sig_gate = jax.nn.sigmoid(gate_pre)
-    inner_act = (gate_pre * sig_gate * up_pre).astype(bf16)
-    block_out = (
-        middle + sum_columns(jnp.dot(inner_act, full_down, preferred_element_type=f32))
-    ).astype(bf16)
-
-    grad_top = gather_cols(cotangent)
-    grad_inner = cols_product(grad_top, full_down)
-    grad_gate = (grad_inner * up_pre * sig_gate * (1.0 + gate_pre * (1.0 - sig_gate))).astype(bf16)
-    grad_up = (grad_inner * gate_pre * sig_gate).astype(bf16)
-    grad_normed_ffn = sum_columns(
-        cols_product(grad_gate, full_gate) + cols_product(grad_up, full_up)
-    )
-    grad_from_ffn, grad_norm_ffn = shard_norm_back(middle, norm_ffn, scale_ffn, grad_normed_ffn)
-    grad_middle = cotangent.astype(f32) + grad_from_ffn
-    grad_mid_full = gather_cols(grad_middle.astype(bf16))
-    grad_gated = cols_product(grad_mid_full, full_out)
+    middle, mids = exchange(
+        z, ("cols",), [gated], [ow], finish_middle, [hidden_in, norm_ffn[None]], [local], True, 0
+    )
+    undo = 1.0 / (gains[1:] * gains[1:])
+    xr, tr, inner, dgate, dup, weigh, scale_ffn = ffn(g, mids, tops, undo, ew, uw, dw)
+    gate_grad = g.sum_rows(rows_product(xr, dgate), 0)
+    up_grad = g.sum_rows(rows_product(xr, dup), 0)
+    down_grad = g.sum_rows(rows_product(inner, tr), 1)
+    weigh = scale_ffn * scale_ffn * g.total(weigh[:, 0], "col")[:, None] / D
+    grad_middle, norm_sums, downs = exchange(
+        z, ("rows", "rows"), [dgate, dup], [ew, uw], finish_gradient,
+        [cotangent, middle, norm_ffn[None], weigh], [local, sums], True, 1,
+    )
+    grad_norm_ffn = jnp.sum(norm_sums, axis=(0, 1))
+    mr, grad_gated = back_gate(g, downs, ow)
+    out_grad = g.sum_rows(rows_product(gated, mr), 1)
     dpq, dpk, dpv, dpg, dcols, dwq, dwk, dwv, dgain = mixer_backward(
         by_seq(grad_gated), *projected, cols, rows, inv, upd, states,
-        conv_query, conv_key, conv_value, gains,
-    )
-    grad_proj = [flat(g) for g in (dpq, dpk, dpv, dpg)]
+        conv_query, conv_key, conv_value, gain_gated,
+    )
+    dproj = jnp.concatenate([flat(d) for d in (dpq, dpk, dpv, dpg)], axis=1)
+    in_grads = g.sum_rows(rows_product(normed, dproj), 0)
     dsmall = flat(dcols).T
-    dstrength, dlog = dsmall[:heads], dsmall[heads:]
+    dstrength, dlog = dsmall[:heads], dsmall[heads:few]
     grad_small = jnp.concatenate(
         [dstrength * strength * (1.0 - strength), dlog * rate * jax.nn.sigmoid(proj_decay)], axis=0
-    ).astype(bf16)
+    )
+    weigh = g.total(dsmall[few] + jnp.sum(grad_small * proj_small, axis=0), "col")[:, None]
+    weigh = scale_mixer * scale_mixer * weigh / D
+    grad_small = grad_small.astype(bf16)
+    small_grads = jnp.dot(grad_small, normed, preferred_element_type=f32)
     grad_decay_log = jnp.sum(dlog * log_decay, axis=1)
-    term = rows_product(grad_small, small_in)
-    for g, w in zip(grad_proj, full):
-        term = term + cols_product(g, w)
-    grad_normed = sum_columns(term)
-    grad_from_mixer, grad_norm_mixer = shard_norm_back(hidden, norm_mixer, scale_mixer, grad_normed)
-    grad_input = grad_middle + grad_from_mixer
-
-    in_grads = [sum_rows(rows_product(normed, g), 0) for g in grad_proj]
-    small_grads = sum_rows(jnp.dot(grad_small, normed, preferred_element_type=f32), 1).T
-    gate_grad = sum_rows(rows_product(normed_ffn, grad_gate), 0)
-    up_grad = sum_rows(rows_product(normed_ffn, grad_up), 0)
-    out_grad = sum_rows(rows_product(gated, grad_mid_full), 1)
-    down_grad = sum_rows(rows_product(inner_act, grad_top), 1)
-    small = lax.psum(
-        (grad_norm_mixer, grad_norm_ffn, grad_decay_log, dwq, dwk, dwv, dgain[0]), "row"
-    )
+    small_rows = small_in.T
+    grad_input, mixer_sums = exchange(
+        z, ("rows", "rows"), [dproj, grad_small.T], [inw, small_rows], finish_input,
+        [grad_middle, hidden_in, norm_mixer[None], scale_mixer, weigh], [local, sums], False, 2,
+    )
+    (block_out,) = exchange(
+        z, ("cols",), [inner], [dw], finish_out, [middle],
+        [jax.ShapeDtypeStruct((tokens, g.block), bf16)], False, 3,
+    )
+    grad_norm_mixer = jnp.sum(mixer_sums, axis=(0, 1))
+    pieces = [dwq, dwk, dwv, dgain, grad_norm_ffn, grad_decay_log, small_grads]
+    joined = g.total(jnp.concatenate([p.reshape(-1) for p in pieces]), "row")
+    summed, at = [], 0
+    for p in pieces:
+        summed.append(joined[at : at + p.size].reshape(p.shape))
+        at += p.size
+    small_grads = lax.dynamic_slice(summed[6], (0, g.at * g.shard), (few, g.shard)).T
+    grad_norm_mixer = g.total(grad_norm_mixer, "row")
+    grads, at = [], 0
+    for w in widths:
+        grads.append(in_grads[:, at : at + w])
+        at += w
     return (
         block_out,
         grad_input,
-        small[0],
-        in_grads[0],
-        in_grads[1],
-        in_grads[2],
-        in_grads[3],
+        grad_norm_mixer,
+        *grads,
         small_grads[:, :heads],
         small_grads[:, heads:],
-        small[2],
-        small[3],
-        small[4],
-        small[5],
-        small[6],
+        summed[5],
+        summed[0],
+        summed[1],
+        summed[2],
+        summed[3][0],
         out_grad,
-        small[1],
+        summed[4],
         gate_grad,
         up_grad,
         down_grad,

time: 1440 us -> 912 us (0.63)
  waiting for transfers between devices: 872 us -> 212 us
  Pallas kernels: 126 us -> 533 us
  matrix products: 276 us -> 65.3 us
  blocking collectives: 86.5 us -> 0 us
  starting transfers between devices: 2.05 us -> 33.9 us
    all_gather x12 -> x5, waiting for transfers between devices: 430 us -> 21 us  [gather_rows(): return lax.all_gather(values, 'row', axis=0, tiled=True)]
    pallas_call x0 -> x7, Pallas kernels: none -> 404 us  [the longest x4 332 us: exchange(): pl.pallas_call(functools.partial(exchange_kernel, z, kinds, finish, gathe...]
    reduce_scatter x4 -> x0, waiting for transfers between devices: 254 us -> none  [sum_columns(): lax.psum_scatter(term.astype(bf16), 'col', scatter_dimension=1, tiled=True)]
    dot_general x18 -> x1, matrix products: 191 us -> 4.72 us  [on_device(): small_grads = jnp.dot(grad_small, normed, preferred_element_type=f32)]
    ppermute x0 -> x29, waiting for transfers between devices: none -> 125 us  [swap(): return lax.ppermute(values, axis, [(i, i ^ bits) for i in range(count)])]
    reduce_scatter x8 -> x5, waiting for transfers between devices: 183 us -> 64.6 us  [sum_rows(): lax.psum_scatter(term.astype(bf16), 'row', scatter_dimension=axis, tiled=...]
    psum x5 -> x0, blocking collectives: 73.2 us -> none  [the longest x2 28.4 us: shard_norm(): squares = lax.psum(jnp.sum(values * values, axis=1), 'col')]
    ppermute x0 -> x29, starting transfers between devices: none -> 33.5 us  [swap(): return lax.ppermute(values, axis, [(i, i ^ bits) for i in range(count)])]
  transfers between devices with their start and end apart: 25 -> 39, of which waited for: 20 -> 12; matrix products, arithmetic and copies ran while one was open for 18% -> 10% of each run, Pallas kernels for 9% -> 42%
where the time goes in v2:
time: 912 us; the launch traced here: 908 us
  Pallas kernels  533 us (58%)
  waiting for transfers between devices  212 us (23%)
  matrix products  65.3 us (7%)
  starting transfers between devices  33.9 us (4%)
  other arithmetic  26.4 us (3%)
  local copies, waits for them, and re-layouts  21.9 us (2%)
  between operations  15.5 us (2%)
    pallas_call x4, Pallas kernels, exchange(): pl.pallas_call(functools.partial(exchange_kernel, z, kinds, finish, gathe...  332 us
    ppermute x29, waiting for transfers between devices, swap(): return lax.ppermute(values, axis, [(i, i ^ bits) for i in range(count)])  125 us
    pallas_call x3, Pallas kernels, launch(): pl.pallas_call(kernel, grid_spec=pltpu.PrefetchScalarGridSpec(num_scalar_...  72.3 us
    pallas_call x1, Pallas kernels, mixer_forward(): pl.pallas_call(functools.partial(forward_kernel, heads, seqs), grid=(step...  70.8 us
    reduce_scatter x5, waiting for transfers between devices, sum_rows(): lax.psum_scatter(term.astype(bf16), 'row', scatter_dimension=axis, tiled=...  64.6 us
    dot_general x5, matrix products, rows_product(): lax.dot_general(first_op, second_op, (((0,), (0,)), ((), ())), preferred_...  60.6 us
    pallas_call x1, Pallas kernels, mixer_backward(): pl.pallas_call(functools.partial(backward_kernel, heads, seqs), grid=(ste...  58 us
    ppermute x29, starting transfers between devices, swap(): return lax.ppermute(values, axis, [(i, i ^ bits) for i in range(count)])  33.5 us
  transfers between devices with their start and end apart: 39, of which 12 were waited for; matrix products, arithmetic and copies ran while one was open for 10% of the time, Pallas kernels for 42%

profile of v2, /device:TPU:0, one launch (start us, length us, event | category | flops | bytes accessed | tf_op | source)
XLA Modules:
  0.0 907.9 jit_solution(1423248009901274965)
XLA Ops:
  7.3 2.7 pad_maximum_fusion.1
  13.8 2.7 collective-permute-start.10
  16.4 1.6 collective-permute-start.8
  18.0 24.6 %collective-permute-done.10 = bf16[4,2048]{0,1:T(8,128)(2,1)S(1)} collective-permute-done((bf16[4,2048]{0,1:T(8,128)(2,1)S(1)}, bf16[4,2048]{0,1:T(8,128)(2,1)S(1)}, u32[]{:S(2)}, u32[]{:S(2)}) %collective-permute-start.10) | collective-permute-done | bytes 16416 | tf_op jit(solution)/shard_map/ppermute | solution.py:421
  42.7 8.1 collective-permute-start.11
  50.8 1.6 collective-permute-start.9
  53.8 1.6 collective-permute-start.13
  55.8 51.5 %collective-permute-done.11 = bf16[4,2048]{0,1:T(8,128)(2,1)S(1)} collective-permute-done((bf16[4,2048]{0,1:T(8,128)(2,1)S(1)}, bf16[4,2048]{0,1:T(8,128)(2,1)S(1)}, u32[]{:S(2)}, u32[]{:S(2)}) %collective-permute-start.11) | collective-permute-done | bytes 16416 | tf_op jit(solution)/shard_map/ppermute | solution.py:421
  107.4 1.5 collective-permute-start.1
  108.9 1.5 collective-permute-start
  112.6 9.4 %collective-permute-done.13.refs_3_ = bf16[2048,256]{1,0:T(8,128)(2,1)} collective-permute-done((bf16[2048,256]{1,0:T(8,128)(2,1)S(1)}, bf16[2048,256]{1,0:T(8,128)(2,1)}, u32[]{:S(2)}, u32[]{:S(2)}) %collective-permute-start.13) | collective-permute-done | bytes 1048608 | tf_op jit(solution)/shard_map/ppermute | solution.py:421
  122.6 21.8 %collective-permute-done.1.refs_2_ = bf16[2048,256]{1,0:T(8,128)(2,1)} collective-permute-done((bf16[2048,256]{1,0:T(8,128)(2,1)}, bf16[2048,256]{1,0:T(8,128)(2,1)}, u32[]{:S(2)}, u32[]{:S(2)}) %collective-permute-start.1) | collective-permute-done | bytes 1048608 | tf_op jit(solution)/shard_map/ppermute | solution.py:421
  147.5 9.1 %collective-permute-done.12.refs_2_ = bf16[2048,256]{1,0:T(8,128)(2,1)} collective-permute-done((bf16[2048,256]{1,0:T(8,128)(2,1)S(1)}, bf16[2048,256]{1,0:T(8,128)(2,1)}, u32[]{:S(2)}, u32[]{:S(2)}) %collective-permute-start.12) | collective-permute-done | bytes 1048608 | tf_op jit(solution)/shard_map/ppermute | solution.py:421
  157.7 26.9 %project.1 = (bf16[2048,2048]{1,0:T(8,128)(2,1)}, f32[2048,1]{1,0:T(8,128)}, f32[2048,256]{1,0:T(8,128)}, f32[2048,256]{1,0:T(8,128)}, f32[2048,512]{1,0:T(8,128...) custom-call(s32[2]{0:T(128)} %pad_add_fusion.ids, bf16[2048,256]{1,0:T(8,128)(2,1)} %refs_5_.1, ...), custom_call_target="tpu_custom_call" | custom-call | flops 12918456320 | bytes 35717120 | tf_op jit(solution)/shard_map/project/pallas_call | solution.py:456
  186.5 70.8 %mixer_forward.1 = (bf16[2,1024,512]{2,1,0:T(8,128)(2,1)S(1)}, bf16[2,2,1024,128]{3,2,1,0:T(8,128)(2,1)S(1)}, bf16[2,1024,512]{2,1,0:T(8,128)(2,1)}, f32[8,2,2,128,256]{4,3,2,1,0:T(8,128)}) custom-call(f32[2,1024,256]{2,1,0:T(8,128)} %bitcast.70, f32[2,1024,256]{2,1,0:T(8,128)} %bitcast.73, f32[2,1024,512]{2,1,0:T(8,128)} %bitcast.67, ...), custom_call_target="tpu_custom_call" | custom-call | tf_op jit(solution)/shard_map/mixer_forward/pallas_call | solution.py:304
  259.6 104.3 %exchange.4 = (f32[2048,256]{1,0:T(8,128)}, bf16[8,2048,256]{2,1,0:T(8,128)(2,1)}) custom-call(bf16[2048,512]{1,0:T(8,128)(2,1)} %bitcast.65, bf16[4,512,512]{2,1,0:T(8,128)(2,1)} %bitcast.121, bf16[2048,256]{1,0:T(8,128)(2,1)} %refs_5_.1, f32[1,256]{1,0:T(1,128)} %bitcast.111), custom_call_target="tpu_custom_call" | custom-call | flops 54294966272 | bytes 15729664 | tf_op jit(solution)/shard_map/exchange/pallas_call | solution.py:759
  364.0 21.0 %all-gather.12.cloned.1.call-done.refs_11_.refs_3_ = bf16[2048,704]{1,0:T(8,128)(2,1)} async-done(((bf16[512,704]{1,0:T(8,128)(2,1)}), bf16[2048,704]{1,0:T(8,128)(2,1)}) %all-gather.12.cloned.1.call-update) | async-done | bytes 2883600 | tf_op jit(solution)/shard_map/all_gather | solution.py:435
  385.0 32.0 %ffn.1 = (bf16[2048,2048]{1,0:T(8,128)(2,1)}, bf16[2048,2048]{1,0:T(8,128)(2,1)}, bf16[2048,704]{1,0:T(8,128)(2,1)}, bf16[2048,704]{1,0:T(8,128)(2,1)}, bf16[204...) custom-call(s32[2]{0:T(128)} %pad_add_fusion.ids, bf16[8,2048,256]{2,1,0:T(8,128)(2,1)} %get-tuple-element.61.refs_0_, ...), custom_call_target="tpu_custom_call" | custom-call | flops 17716740096 | bytes 50880512 | tf_op jit(solution)/shard_map/ffn/pallas_call | solution.py:456
  417.0 1.6 reduce
  419.8 1.4 collective-permute-start.20
  421.3 2.2 collective-permute-done.20
  423.5 1.5 collective-permute-start.21
  425.0 2.2 collective-permute-done.21
  427.5 2.3 multiply_multiply_fusion.1.refs_7_
  429.8 109.3 %exchange.6 = (f32[2048,256]{1,0:T(8,128)}, f32[8,1,256]{2,1,0:T(1,128)}, bf16[8,2048,256]{2,1,0:T(8,128)(2,1)}) custom-call(bf16[2048,704]{1,0:T(8,128)(2,1)} %get-tuple-element.64.refs_0_, bf16[2048,704]{1,0:T(8,128)(2,1)} %get-tuple-element.65.refs_1_, bf16[2048,704]{1,0:T(8,128)(2,1)} %all-gather.10.cloned.1.call-done.refs_10_.refs_2_, ...), custom_call_target="tpu_custom_call" | custom-call | flops 61811159040 | bytes 25183232 | tf_op jit(solution)/shard_map/exchange/pallas_call | solution.py:759
  539.2 13.4 %back_gate.1 = (bf16[2048,2048]{1,0:T(8,128)(2,1)}, f32[2048,512]{1,0:T(8,128)}) custom-call(s32[2]{0:T(128)} %pad_add_fusion.ids, bf16[8,2048,256]{2,1,0:T(8,128)(2,1)} %get-tuple-element.68.ms, bf16[4,512,512]{2,1,0:T(8,128)(2,1)} %bitcast.122), custom_call_target="tpu_custom_call" | custom-call | flops 4294967296 | bytes 23068672 | tf_op jit(solution)/shard_map/back_gate/pallas_call | solution.py:456
  552.5 9.3 %convolution_convert_fusion.4 = bf16[512,2048]{1,0:T(8,128)(2,1)} fusion(bf16[2048,512]{1,0:T(8,128)(2,1)S(1)} %bitcast.66, bf16[2048,2048]{1,0:T(8,128)(2,1)} %get-tuple-element.88), kind=kOutput, calls=%fused_computation.5 | convolution fusion | flops 4296015872 | bytes 12582912 | tf_op jit(solution)/shard_map/dot_general | solution.py:774
  561.9 9.7 %convolution_convert_fusion.2 = bf16[2048,704]{0,1:T(8,128)(2,1)} fusion(bf16[2048,2048]{1,0:T(8,128)(2,1)} %get-tuple-element.89, bf16[2048,704]{1,0:T(8,128)(2,1)S(1)} %copy-done.38), kind=kOutput, calls=%fused_computation.3 | convolution fusion | flops 5907021824 | bytes 14155776 | tf_op jit(solution)/shard_map/dot_general | solution.py:774
  571.7 10.9 %convolution_convert_fusion.3 = bf16[2048,704]{0,1:T(8,128)(2,1)} fusion(bf16[2048,2048]{1,0:T(8,128)(2,1)} %get-tuple-element.89, bf16[2048,704]{1,0:T(8,128)(2,1)} %get-tuple-element.64.refs_0_), kind=kOutput, calls=%fused_computation.4 | convolution fusion | flops 5907021824 | bytes 14155776 | tf_op jit(solution)/shard_map/dot_general | solution.py:774
  582.7 10.0 %convolution_convert_fusion.1 = bf16[704,2048]{1,0:T(8,128)(2,1)} fusion(bf16[2048,704]{1,0:T(8,128)(2,1)S(1)} %copy-done.37, bf16[2048,2048]{1,0:T(8,128)(2,1)} %get-tuple-element.90), kind=kOutput, calls=%fused_computation.2 | convolution fusion | flops 5907021824 | bytes 14155776 | tf_op jit(solution)/shard_map/dot_general | solution.py:774
  592.8 58.0 %mixer_backward.1 = (bf16[2,1024,256]{2,1,0:T(8,128)(2,1)}, bf16[2,1024,256]{2,1,0:T(8,128)(2,1)}, bf16[2,1024,512]{2,1,0:T(8,128)(2,1)}, bf16[2,1024,512]{2,1,0...) custom-call(f32[2,1024,512]{2,1,0:T(8,128)} %bitcast.78, ...), custom_call_target="tpu_custom_call" | custom-call | tf_op jit(solution)/shard_map/mixer_backward/pallas_call | solution.py:342
  650.7 1.6 copy.75
  653.1 20.7 %convolution_convert_fusion = bf16[2048,1536]{1,0:T(8,128)(2,1)} fusion(bf16[2048,2048]{1,0:T(8,128)(2,1)} %get-tuple-element.82, bf16[2048,512]{1,0:T(8,128)(2,1)} %bitcast.82, bf16[2048,512]{1,0:T(8,128)(2,1)} %bitcast.80, bf16[2048,256]{1,0:T(8,128)(2,1)} %bitcast.86, bf16[2048,256]{1,0:T(8,128)(2,1)} %bitcast.84), kind=kOutput, calls=%fused_computation | convolution fusion | flops 12913213440 | bytes 20971520 | tf_op jit(solution)/shard_map/dot_general | solution.py:774
  673.8 4.9 pad_maximum_fusion.refs_0_
  678.9 4.7 convolution_bitcast_fusion
  683.6 1.7 collective-permute-start.24
  688.7 61.2 %exchange.7 = (f32[2048,256]{1,0:T(8,128)}, f32[8,1,256]{2,1,0:T(1,128)}) custom-call(bf16[2048,1536]{1,0:T(8,128)(2,1)} %pad_maximum_fusion.refs_0_, bf16[2048,4]{1,0:T(8,128)(2,1)} %copy.74.refs_1_, bf16[2048,1536]{1,0:T(8,128)(2,1)} %all-gather.8.cloned.1.call-done.refs_9_.refs_2_, bf16[2048,4]{1,0:T(8,128)(2,1)} %bitcast.79, ...), custom_call_target="tpu_custom_call" | custom-call | flops 62918455296 | bytes 17884160 | tf_op jit(solution)/shard_map/exchange/pallas_call | solution.py:759
  750.7 1.5 collective-permute-start.25
  752.2 2.6 collective-permute-done.25
  755.7 2.2 collective-permute-start.28
  757.8 56.8 %exchange.5 = bf16[2048,256]{1,0:T(8,128)(2,1)} custom-call(bf16[2048,704]{1,0:T(8,128)(2,1)} %get-tuple-element.62.refs_0_, bf16[4,704,512]{2,1,0:T(8,128)(2,1)} %bitcast.120, f32[2048,256]{1,0:T(8,128)} %get-tuple-element.63.refs_2_.refs_5_), custom_call_target="tpu_custom_call" | custom-call | flops 55905579008 | bytes 8912896 | tf_op jit(solution)/shard_map/exchange/pallas_call | solution.py:759
  819.4 2.1 convert_element_type.85
  821.5 2.4 convert_element_type.89
  823.9 2.4 convert_element_type.87
  826.4 2.5 convert_element_type.91
  828.9 64.6 %reduce-scatter.6.cloned.1.call-done = bf16[512,1536]{1,0:T(8,128)(2,1)} async-done(((bf16[2048,1536]{1,0:T(8,128)(2,1)}), bf16[512,1536]{1,0:T(8,128)(2,1)}) %reduce-scatter.6.cloned.1.call-update) | async-done | bytes 1572880 | tf_op jit(solution)/shard_map/reduce_scatter | solution.py:438
  893.4 2.1 fusion.8
  895.5 2.8 fusion.7
  (215 shorter events, 31.3 us)
Async XLA Ops:
  7.3 103.1 %copy-start.16 = (bf16[512,704]{0,1:T(8,128)(2,1)S(1)}, bf16[512,704]{0,1:T(8,128)(2,1)}, u32[]{:S(2)}) copy-start(bf16[512,704]{0,1:T(8,128)(2,1)} %param.38) | copy-start | bytes 2162692
  7.3 150.4 %all-gather.8.cloned.1.call-start = ((), (), s32[]{:S(2)}) async-start(), calls=%async_computation.5 | async-start | bytes 7864320 | tf_op jit(solution)/shard_map/all_gather | solution.py:435
  10.1 101.5 %copy-start.17 = (s32[2048]{0:T(1024)S(1)}, s32[2048]{0:T(1024)}, u32[]{:S(2)}) copy-start(s32[2048]{0:T(1024)} %param.21) | copy-start | bytes 24580
  10.1 135.7 %copy-start.36 = (f32[2]{0:T(128)S(1)}, f32[2]{0:T(128)}, u32[]{:S(2)}) copy-start(f32[2]{0:T(128)} %param.30) | copy-start | bytes 28
  10.1 249.5 %all-gather.14.cloned.1.call-start = ((), (), s32[]{:S(2)}) async-start(), calls=%async_computation.13 | async-start | bytes 2621440 | tf_op jit(solution)/shard_map/all_gather | solution.py:435
  10.8 353.1 %all-gather.16.cloned.1.call-start = ((), (), s32[]{:S(2)}) async-start(), calls=%async_computation.14 | async-start | bytes 3604480 | tf_op jit(solution)/shard_map/all_gather | solution.py:435
  11.6 352.4 %all-gather.10.cloned.1.call-start = ((), (), s32[]{:S(2)}) async-start(), calls=%async_computation.6 | async-start | bytes 3932160 | tf_op jit(solution)/shard_map/all_gather | solution.py:435
  12.8 372.2 %all-gather.12.cloned.1.call-start = ((), (), s32[]{:S(2)}) async-start(), calls=%async_computation.7 | async-start | bytes 3932160 | tf_op jit(solution)/shard_map/all_gather | solution.py:435
  12.9 3.5 collective-permute-start.7
  13.8 28.9 %collective-permute-start.10 = (bf16[4,2048]{0,1:T(8,128)(2,1)S(1)}, bf16[4,2048]{0,1:T(8,128)(2,1)S(1)}, u32[]{:S(2)}, u32[]{:S(2)}) collective-permute-start(bf16[4,2048]{0,1:T(8,128)(2,1)S(1)} %bitcast_dynamic-update-slice_fusion), channel_id=1, source_target_pairs={{0,8},{8,0},{16,24},{24,16},{1,9},{9,1},{17,25},{25,17},{2,10},{10... | collective-permute-start | bytes 49160 | tf_op jit(solution)/shard_map/ppermute | solution.py:421
  16.4 34.4 %collective-permute-start.8 = (f32[2,2048]{1,0:T(2,128)S(1)}, f32[2,2048]{1,0:T(2,128)S(1)}, u32[]{:S(2)}, u32[]{:S(2)}) collective-permute-start(f32[2,2048]{1,0:T(2,128)S(1)} %add_dynamic-update-slice_fusion), channel_id=1, source_target_pairs={{0,2},{1,3},{2,0},{3,1},{4,6},{5,7},{6,4},{7,5},{8,10},{9,11},{10,... | collective-permute-start | bytes 49160 | tf_op jit(solution)/shard_map/ppermute | solution.py:421
  42.7 64.7 %collective-permute-start.11 = (bf16[4,2048]{0,1:T(8,128)(2,1)S(1)}, bf16[4,2048]{0,1:T(8,128)(2,1)S(1)}, u32[]{:S(2)}, u32[]{:S(2)}) collective-permute-start(bf16[4,2048]{0,1:T(8,128)(2,1)S(1)} %fusion), channel_id=1, source_target_pairs={{0,16},{8,24},{16,0},{24,8},{1,17},{9,25},{17,1},{25,9},{2,18},{10... | collective-permute-start | bytes 49160 | tf_op jit(solution)/shard_map/ppermute | solution.py:421
  50.8 58.0 %collective-permute-start.9 = (f32[2,2048]{1,0:T(2,128)S(1)}, f32[2,2048]{1,0:T(2,128)S(1)}, u32[]{:S(2)}, u32[]{:S(2)}) collective-permute-start(f32[2,2048]{1,0:T(2,128)S(1)} %add.81), channel_id=1, source_target_pairs={{0,4},{1,5},{2,6},{3,7},{4,0},{5,1},{6,2},{7,3},{8,12},{9,13},{10,... | collective-permute-start | bytes 49160 | tf_op jit(solution)/shard_map/ppermute | solution.py:421
  52.4 59.6 %collective-permute-start.14 = (bf16[2048,256]{1,0:T(8,128)(2,1)S(1)}, bf16[2048,256]{1,0:T(8,128)(2,1)}, u32[]{:S(2)}, u32[]{:S(2)}) collective-permute-start(bf16[2048,256]{1,0:T(8,128)(2,1)S(1)} %copy-done.34), channel_id=1, source_target_pairs={{0,6},{1,7},{2,4},{3,5},{4,2},{5,3},{6,0},{7,1},{8,14},{9,15},{10,... | collective-permute-start | bytes 3145736 | tf_op jit(solution)/shard_map/ppermute | solution.py:421
  53.8 68.3 %collective-permute-start.13 = (bf16[2048,256]{1,0:T(8,128)(2,1)S(1)}, bf16[2048,256]{1,0:T(8,128)(2,1)}, u32[]{:S(2)}, u32[]{:S(2)}) collective-permute-start(bf16[2048,256]{1,0:T(8,128)(2,1)S(1)} %copy-done.34), channel_id=1, source_target_pairs={{0,4},{1,5},{2,6},{3,7},{4,0},{5,1},{6,2},{7,3},{8,12},{9,13},{10,... | collective-permute-start | bytes 3145736 | tf_op jit(solution)/shard_map/ppermute | solution.py:421
  55.4 66.7 %collective-permute-start.2 = (bf16[2048,256]{1,0:T(8,128)(2,1)}, bf16[2048,256]{1,0:T(8,128)(2,1)}, u32[]{:S(2)}, u32[]{:S(2)}) collective-permute-start(bf16[2048,256]{1,0:T(8,128)(2,1)} %refs_5_.1), channel_id=1, source_target_pairs={{0,6},{1,7},{2,4},{3,5},{4,2},{5,3},{6,0},{7,1},{8,14},{9,15},{10,... | collective-permute-start | bytes 3145736 | tf_op jit(solution)/shard_map/ppermute | solution.py:421
  107.4 37.0 %collective-permute-start.1 = (bf16[2048,256]{1,0:T(8,128)(2,1)}, bf16[2048,256]{1,0:T(8,128)(2,1)}, u32[]{:S(2)}, u32[]{:S(2)}) collective-permute-start(bf16[2048,256]{1,0:T(8,128)(2,1)} %refs_5_.1), channel_id=1, source_target_pairs={{0,4},{1,5},{2,6},{3,7},{4,0},{5,1},{6,2},{7,3},{8,12},{9,13},{10,... | collective-permute-start | bytes 3145736 | tf_op jit(solution)/shard_map/ppermute | solution.py:421
  108.9 35.5 %collective-permute-start = (bf16[2048,256]{1,0:T(8,128)(2,1)}, bf16[2048,256]{1,0:T(8,128)(2,1)}, u32[]{:S(2)}, u32[]{:S(2)}) collective-permute-start(bf16[2048,256]{1,0:T(8,128)(2,1)} %refs_5_.1), channel_id=1, source_target_pairs={{0,2},{1,3},{2,0},{3,1},{4,6},{5,7},{6,4},{7,5},{8,10},{9,11},{10,... | collective-permute-start | bytes 3145736 | tf_op jit(solution)/shard_map/ppermute | solution.py:421
  111.5 707.8 %reduce-scatter.8.cloned.1.call-start = ((), (), s32[]{:S(2)}) async-start(), calls=%async_computation.9 | async-start | bytes 2621440 | tf_op jit(solution)/shard_map/reduce_scatter | solution.py:438
  112.0 44.6 %collective-permute-start.12 = (bf16[2048,256]{1,0:T(8,128)(2,1)S(1)}, bf16[2048,256]{1,0:T(8,128)(2,1)}, u32[]{:S(2)}, u32[]{:S(2)}) collective-permute-start(bf16[2048,256]{1,0:T(8,128)(2,1)S(1)} %copy-done.34), channel_id=1, source_target_pairs={{0,2},{1,3},{2,0},{3,1},{4,6},{5,7},{6,4},{7,5},{8,10},{9,11},{10,... | collective-permute-start | bytes 3145736 | tf_op jit(solution)/shard_map/ppermute | solution.py:421
  122.0 34.6 %collective-permute-start.3 = (bf16[2048,256]{1,0:T(8,128)(2,1)}, bf16[2048,256]{1,0:T(8,128)(2,1)}, u32[]{:S(2)}, u32[]{:S(2)}) collective-permute-start(bf16[2048,256]{1,0:T(8,128)(2,1)} %refs_5_.1), channel_id=1, source_target_pairs={{0,1},{1,0},{2,3},{3,2},{4,5},{5,4},{6,7},{7,6},{8,9},{9,8},{10,11... | collective-permute-start | bytes 3145736 | tf_op jit(solution)/shard_map/ppermute | solution.py:421
  122.0 35.1 %collective-permute-start.6 = (bf16[2048,256]{1,0:T(8,128)(2,1)}, bf16[2048,256]{1,0:T(8,128)(2,1)}, u32[]{:S(2)}, u32[]{:S(2)}) collective-permute-start(bf16[2048,256]{1,0:T(8,128)(2,1)} %collective-permute-done.2.refs_3_), channel_id=1, source_target_pairs={{0,1},{1,0},{2,3},{3,2},{4,5},{5,4},{6,7},{7,6},{8,9},{9,8},{10,11... | collective-permute-start | bytes 3145736 | tf_op jit(solution)/shard_map/ppermute | solution.py:421
  144.3 12.9 %collective-permute-start.5 = (bf16[2048,256]{1,0:T(8,128)(2,1)}, bf16[2048,256]{1,0:T(8,128)(2,1)}, u32[]{:S(2)}, u32[]{:S(2)}) collective-permute-start(bf16[2048,256]{1,0:T(8,128)(2,1)} %collective-permute-done.1.refs_2_), channel_id=1, source_target_pairs={{0,1},{1,0},{2,3},{3,2},{4,5},{5,4},{6,7},{7,6},{8,9},{9,8},{10,11... | collective-permute-start | bytes 3145736 | tf_op jit(solution)/shard_map/ppermute | solution.py:421
  144.3 13.3 %collective-permute-start.4 = (bf16[2048,256]{1,0:T(8,128)(2,1)}, bf16[2048,256]{1,0:T(8,128)(2,1)}, u32[]{:S(2)}, u32[]{:S(2)}) collective-permute-start(bf16[2048,256]{1,0:T(8,128)(2,1)} %collective-permute-done.refs_1_), channel_id=1, source_target_pairs={{0,1},{1,0},{2,3},{3,2},{4,5},{5,4},{6,7},{7,6},{8,9},{9,8},{10,11... | collective-permute-start | bytes 3145736 | tf_op jit(solution)/shard_map/ppermute | solution.py:421
  156.6 207.2 %collective-permute-start.15 = (bf16[2048,256]{1,0:T(8,128)(2,1)S(1)}, bf16[2048,256]{1,0:T(8,128)(2,1)S(1)}, u32[]{:S(2)}, u32[]{:S(2)}) collective-permute-start(bf16[2048,256]{1,0:T(8,128)(2,1)S(1)} %copy-done.34), channel_id=1, source_target_pairs={{0,1},{1,0},{2,3},{3,2},{4,5},{5,4},{6,7},{7,6},{8,9},{9,8},{10,11... | collective-permute-start | bytes 3145736 | tf_op jit(solution)/shard_map/ppermute | solution.py:421
  156.6 207.3 %collective-permute-start.18 = (bf16[2048,256]{1,0:T(8,128)(2,1)}, bf16[2048,256]{1,0:T(8,128)(2,1)}, u32[]{:S(2)}, u32[]{:S(2)}) collective-permute-start(bf16[2048,256]{1,0:T(8,128)(2,1)} %collective-permute-done.14.refs_4_), channel_id=1, source_target_pairs={{0,1},{1,0},{2,3},{3,2},{4,5},{5,4},{6,7},{7,6},{8,9},{9,8},{10,11... | collective-permute-start | bytes 3145736 | tf_op jit(solution)/shard_map/ppermute | solution.py:421
  157.1 206.8 %collective-permute-start.17 = (bf16[2048,256]{1,0:T(8,128)(2,1)}, bf16[2048,256]{1,0:T(8,128)(2,1)}, u32[]{:S(2)}, u32[]{:S(2)}) collective-permute-start(bf16[2048,256]{1,0:T(8,128)(2,1)} %collective-permute-done.13.refs_3_), channel_id=1, source_target_pairs={{0,1},{1,0},{2,3},{3,2},{4,5},{5,4},{6,7},{7,6},{8,9},{9,8},{10,11... | collective-permute-start | bytes 3145736 | tf_op jit(solution)/shard_map/ppermute | solution.py:421
  157.2 206.7 %collective-permute-start.16 = (bf16[2048,256]{1,0:T(8,128)(2,1)}, bf16[2048,256]{1,0:T(8,128)(2,1)}, u32[]{:S(2)}, u32[]{:S(2)}) collective-permute-start(bf16[2048,256]{1,0:T(8,128)(2,1)} %collective-permute-done.12.refs_2_), channel_id=1, source_target_pairs={{0,1},{1,0},{2,3},{3,2},{4,5},{5,4},{6,7},{7,6},{8,9},{9,8},{10,11... | collective-permute-start | bytes 3145736 | tf_op jit(solution)/shard_map/ppermute | solution.py:421
  186.1 71.1 %copy-start.1 = (f32[2,16,1024]{2,1,0:T(8,128)}, f32[2,16,1024]{2,1,0:T(8,128)S(1)}, u32[]{:S(2)}) copy-start(f32[2,16,1024]{2,1,0:T(8,128)S(1)} %concatenate.51.rows) | copy-start | bytes 393220
  186.5 70.8 %copy-start = (f32[2,1024,16]{2,1,0:T(8,128)}, f32[2,1024,16]{2,1,0:T(8,128)S(1)}, u32[]{:S(2)}) copy-start(f32[2,1024,16]{2,1,0:T(8,128)S(1)} %copy.67.cols) | copy-start | bytes 393220
  418.6 1.2 collective-permute-start.19
  419.8 3.7 collective-permute-start.20
  423.5 3.7 collective-permute-start.21
  561.8 259.7 %reduce-scatter.12.cloned.1.call-start = ((), (), s32[]{:S(2)}) async-start(), calls=%async_computation.11 | async-start | bytes 3604480 | tf_op jit(solution)/shard_map/reduce_scatter | solution.py:438
  571.6 252.3 %reduce-scatter.10.cloned.1.call-start = ((), (), s32[]{:S(2)}) async-start(), calls=%async_computation.10 | async-start | bytes 3604480 | tf_op jit(solution)/shard_map/reduce_scatter | solution.py:438
  582.6 243.7 %reduce-scatter.14.cloned.1.call-start = ((), (), s32[]{:S(2)}) async-start(), calls=%async_computation.12 | async-start | bytes 3604480 | tf_op jit(solution)/shard_map/reduce_scatter | solution.py:438
  592.7 300.8 %reduce-scatter.6.cloned.1.call-start = ((), (), s32[]{:S(2)}) async-start(), calls=%async_computation.8 | async-start | bytes 7864320 | tf_op jit(solution)/shard_map/reduce_scatter | solution.py:438
  592.7 59.6 %copy-start.18 = (f32[4,2048]{1,0:T(4,128)S(1)}, f32[4,2048]{1,0:T(4,128)}, u32[]{:S(2)}) copy-start(f32[4,2048]{1,0:T(4,128)} %get-tuple-element.59) | copy-start | bytes 98308
  592.7 59.6 %copy-start.20 = (f32[2,2048]{1,0:T(2,128)S(1)}, f32[2,2048]{1,0:T(2,128)}, u32[]{:S(2)}) copy-start(f32[2,2048]{1,0:T(2,128)} %copy-done.19) | copy-start | bytes 49156
  652.6 26.1 %collective-permute-start.22 = (f32[2048]{0:T(1024)S(1)}, f32[2048]{0:T(1024)S(1)}, u32[]{:S(2)}, u32[]{:S(2)}) collective-permute-start(f32[2048]{0:T(1024)S(1)} %add.92), channel_id=1, source_target_pairs={{0,1},{1,0},{2,3},{3,2},{4,5},{5,4},{6,7},{7,6},{8,9},{9,8},{10,11... | collective-permute-start | bytes 24584 | tf_op jit(solution)/shard_map/ppermute | solution.py:421
  678.8 4.8 collective-permute-start.23
  683.6 3.7 collective-permute-start.24
  685.5 70.1 %collective-permute-start.27 = (f32[13058]{0:T(1024)S(1)}, f32[13058]{0:T(1024)S(1)}, u32[]{:S(2)}, u32[]{:S(2)}) collective-permute-start(f32[13058]{0:T(1024)S(1)} %concatenate.54), channel_id=1, source_target_pairs={{0,8},{8,0},{16,24},{24,16},{1,9},{9,1},{17,25},{25,17},{2,10},{10... | collective-permute-start | bytes 156704 | tf_op jit(solution)/shard_map/ppermute | solution.py:421
  750.7 4.1 collective-permute-start.25
  754.8 59.8 %collective-permute-start.26 = (f32[256]{0:T(256)S(1)}, f32[256]{0:T(256)S(1)}, u32[]{:S(2)}, u32[]{:S(2)}) collective-permute-start(f32[256]{0:T(256)S(1)} %add.96), channel_id=1, source_target_pairs={{0,16},{8,24},{16,0},{24,8},{1,17},{9,25},{17,1},{25,9},{2,18},{10... | collective-permute-start | bytes 3080 | tf_op jit(solution)/shard_map/ppermute | solution.py:421
  755.7 59.5 %collective-permute-start.28 = (f32[13058]{0:T(1024)S(1)}, f32[13058]{0:T(1024)S(1)}, u32[]{:S(2)}, u32[]{:S(2)}) collective-permute-start(f32[13058]{0:T(1024)S(1)} %add.98), channel_id=1, source_target_pairs={{0,16},{8,24},{16,0},{24,8},{1,17},{9,25},{17,1},{25,9},{2,18},{10... | collective-permute-start | bytes 156704 | tf_op jit(solution)/shard_map/ppermute | solution.py:421
  826.4 72.0 %copy-start.14 = (bf16[2048,256]{1,0:T(8,128)(2,1)S(1)}, bf16[2048,256]{1,0:T(8,128)(2,1)}, u32[]{:S(2)}) copy-start(bf16[2048,256]{1,0:T(8,128)(2,1)} %exchange.5) | copy-start | bytes 3145732
  828.9 70.5 %copy-start.10 = (f32[2048,256]{1,0:T(8,128)S(1)}, f32[2048,256]{1,0:T(8,128)}, u32[]{:S(2)}) copy-start(f32[2048,256]{1,0:T(8,128)} %get-tuple-element.134) | copy-start | bytes 6291460
  (30 other events, 500.2 us)
Sparse Core Ops, SparseCore 0:
  10.2 140.3 all-gather.7
  152.2 44.5 all-gather.13
  198.4 58.0 all-gather.15
  258.5 62.1 all-gather.9
  322.7 62.1 all-gather.11
  561.9 41.4 reduce-scatter.7
  605.8 55.4 reduce-scatter.11
  663.8 57.0 reduce-scatter.9
  723.3 57.1 reduce-scatter.13
  782.8 110.6 reduce-scatter.5

commit v3 on v2

v3 whole, which is shorter than its diff:
```python
import functools

import jax
import jax.numpy as jnp
from jax import lax
from jax.experimental import pallas as pl
from jax.experimental.pallas import tpu as pltpu
from jax.sharding import PartitionSpec as P

D = 2048
DK = 128
DV = 256
CONV = 4
SEQ = 1024
CHUNK = 128
EPSILON = 1e-06
SCALE = DK ** (-0.5)
f32 = jnp.float32
bf16 = jnp.bfloat16


def mm(a, b, dims=((1,), (0,))):
    return lax.dot_general(a, b, (dims, ((), ())), preferred_element_type=f32)


def split(a):
    hi = a.astype(bf16)
    return hi, (a - hi.astype(f32)).astype(bf16)


def mm3(a, b):
    ah, al = split(a)
    bh, bl = split(b)
    return mm(ah, bh) + (mm(ah, bl) + mm(al, bh))


def sigmoid(u):
    return 1.0 / (1.0 + jnp.exp(-u))


def iotas(n):
    return (
        lax.broadcasted_iota(jnp.int32, (n, n), 0),
        lax.broadcasted_iota(jnp.int32, (n, n), 1),
    )


def unit_lower_inverses(many, row, col):
    n = many[0].shape[0]
    eye = (row == col).astype(f32)
    base = 8
    inside = row // base == col // base
    ds = [jnp.where(inside, a, 0.0) for a in many]
    squares = [mm3(d, d) for d in ds]
    xs = [eye - d for d in ds]
    xs = [x + mm3(x, d) for x, d in zip(xs, squares)]
    fourths = [mm3(d, d) for d in squares]
    xs = [x + mm3(x, d) for x, d in zip(xs, fourths)]
    size = base
    while size < n:
        at = (row // (2 * size) == col // (2 * size)) & (row // size != col // size)
        offs = [jnp.where(at, a, 0.0).astype(bf16) for a in many]
        highs = [x.astype(bf16) for x in xs]
        steps = [mm(off, x).astype(bf16) for off, x in zip(offs, highs)]
        xs = [x - mm(h, step) for x, h, step in zip(xs, highs, steps)]
        size *= 2
    return xs


def conv_taps(buf, s, width, weights, masks):
    pre = weights[0:1] * buf[s, 8 : 8 + CHUNK, :]
    for j in range(1, CONV):
        pre = pre + weights[j : j + 1] * buf[s, 8 - j : 8 - j + CHUNK, :] * masks[j - 1]
    return pre


def forward_kernel(heads, seqs, pq, pk, pv, pg, cols, rows, wq, wk, wv, gain,
                   gated, inv_out, upd_out, state_out, state, bq, bk, bv):
    step = pl.program_id(0)

    @pl.when(step == 0)
    def _():
        state[...] = jnp.zeros_like(state)
        for buf in (bq, bk, bv):
            buf[:, 0:8, :] = jnp.zeros_like(buf[:, 0:8, :])

    row, col = iotas(CHUNK)
    lower = row >= col
    tril = lower.astype(bf16)
    chains = []
    for s in range(seqs):
        cc = cols[s]
        rr = rows[s]
        masks = [cc[:, j : j + 1] for j in range(CONV - 1)]
        ch, cl = split(cc)
        csum = mm(tril, ch) + mm(tril, cl)
        rh, rl = split(rr)
        rsum = mm(rh, tril, ((1,), (1,))) + mm(rl, tril, ((1,), (1,)))
        same = (cc[:, 6:7] == rr[6:7, :]) & lower
        for src, buf in ((pq, bq), (pk, bk), (pv, bv)):
            buf[s, 8 : 8 + CHUNK, :] = src[s]
        cq = conv_taps(bq, s, heads * DK, wq, masks)
        ck = conv_taps(bk, s, heads * DK, wk, masks)
        cv = conv_taps(bv, s, heads * DV, wv, masks)
        for buf in (bq, bk, bv):
            buf[s, 0:8, :] = buf[s, CHUNK : CHUNK + 8, :]
        aq = cq * sigmoid(cq)
        ak = ck * sigmoid(ck)
        av = cv * sigmoid(cv)
        for h in range(heads):
            keys = slice(h * DK, (h + 1) * DK)
            vals = slice(h * DV, (h + 1) * DV)
            q = aq[:, keys]
            q = (q * lax.rsqrt(jnp.sum(q * q, axis=1, keepdims=True) + EPSILON)).astype(bf16)
            k = ak[:, keys]
            k = (k * lax.rsqrt(jnp.sum(k * k, axis=1, keepdims=True) + EPSILON)).astype(bf16)
            v = av[:, vals].astype(bf16).astype(f32)
            beta = cc[:, 8 + h : 9 + h]
            at = 8 + heads + h
            gcol = csum[:, at : at + 1]
            grow = rsum[at : at + 1, :]
            decay = jnp.where(same, jnp.exp(jnp.minimum(gcol - grow, 0.0)), 0.0)
            start = jnp.exp(gcol) * cc[:, 7:8]
            end = jnp.exp(jnp.minimum(gcol[CHUNK - 1 :, :] - gcol, 0.0)) * jnp.where(
                cc[:, 6:7] == cc[CHUNK - 1 :, 6:7], 1.0, 0.0
            )
            kk = mm(k, k, ((1,), (1,)))
            scores = (decay * mm(q, k, ((1,), (1,)))).astype(bf16)
            coupling = jnp.where(row > col, beta * decay * kk, 0.0)
            kend = (end * k.astype(f32)).astype(bf16)
            chains.append((s, h, vals, q, k, v, beta, start, scores, kend, coupling))
    inverses = unit_lower_inverses([c[-1] for c in chains], row, col)
    inverses = [x.astype(bf16) for x in inverses]
    begins = [state[c[0], c[1]] for c in chains]
    lows = [x.astype(bf16) for x in begins]
    rights = []
    for (s, h, vals, q, k, v, beta, start, scores, kend, _), inv, begin, low in zip(chains, inverses, begins, lows):
        inv_out[s, h] = inv
        state_out[0, s, h] = begin
        rights.append((beta * (v - start * mm(k, low))).astype(bf16))
    upds = [mm(inv, right).astype(bf16) for inv, right in zip(inverses, rights)]
    for (s, h, vals, q, k, v, beta, start, scores, kend, _), begin, low, upd in zip(chains, begins, lows, upds):
        upd_out[s, :, vals] = upd
        state[s, h] = start[CHUNK - 1 :, :] * begin + mm(kend, upd, ((0,), (0,)))
        mixed = (start * mm(q, low) + mm(scores, upd)) * SCALE
        gate = pg[s, :, vals]
        scaled = mixed * lax.rsqrt(jnp.mean(mixed * mixed, axis=1, keepdims=True) + EPSILON)
        gated[s, :, vals] = (scaled * gain[:, vals] * (gate * sigmoid(gate))).astype(bf16)


def backward_kernel(heads, seqs, dgated, pq, pk, pv, pg, hq, hk, hv, cols, rows, inv_in, upd_in, state_in,
                    wq, wk, wv, gain,
                    dproj, dcols, dwq, dwk, dwv, dgain,
                    dstate, bq, bk, bv, tq, tk, tv):
    step = pl.program_id(0)

    @pl.when(step == 0)
    def _():
        dstate[...] = jnp.zeros_like(dstate)
        for buf in (tq, tk, tv):
            buf[:, CHUNK : CHUNK + 8, :] = jnp.zeros_like(buf[:, CHUNK : CHUNK + 8, :])
        for out in (dwq, dwk, dwv, dgain):
            out[...] = jnp.zeros_like(out)

    row, col = iotas(CHUNK)
    lower = row >= col
    tril = lower.astype(bf16)
    lane = lax.broadcasted_iota(jnp.int32, (CHUNK, 2 * heads + 1), 1)
    last = lax.broadcasted_iota(jnp.int32, (CHUNK, 1), 0) == CHUNK - 1
    shared = []
    for s in range(seqs):
        cc = cols[s]
        rr = rows[s]
        masks = [cc[:, j : j + 1] for j in range(CONV - 1)]
        ch, cl = split(cc)
        csum = mm(tril, ch) + mm(tril, cl)
        rh, rl = split(rr)
        rsum = mm(rh, tril, ((1,), (1,))) + mm(rl, tril, ((1,), (1,)))
        same = (cc[:, 6:7] == rr[6:7, :]) & lower
        pres = []
        for src, halo, buf, weights in ((pq, hq, bq, wq), (pk, hk, bk, wk), (pv, hv, bv, wv)):
            buf[s, 0:8, :] = halo[s]
            buf[s, 8 : 8 + CHUNK, :] = src[s]
            pres.append(conv_taps(buf, s, None, weights, masks))
        sigs = [sigmoid(pre) for pre in pres]
        acts = [pre * sig for pre, sig in zip(pres, sigs)]
        shared.append((cc, masks, csum, rsum, same, pres, sigs, acts))
    found = {}

    def chain(s, h):
        cc, _, csum, rsum, same, pres, sigs, acts = shared[s]
        keys = slice(h * DK, (h + 1) * DK)
        vals = slice(h * DV, (h + 1) * DV)
        q = acts[0][:, keys]
        rq = lax.rsqrt(jnp.sum(q * q, axis=1, keepdims=True) + EPSILON)
        qn = q * rq
        q = qn.astype(bf16)
        k = acts[1][:, keys]
        rk = lax.rsqrt(jnp.sum(k * k, axis=1, keepdims=True) + EPSILON)
        kn = k * rk
        k = kn.astype(bf16)
        v = acts[2][:, vals].astype(bf16).astype(f32)
        beta = cc[:, 8 + h : 9 + h]
        at = 8 + heads + h
        gcol = csum[:, at : at + 1]
        grow = rsum[at : at + 1, :]
        decay = jnp.where(same, jnp.exp(jnp.minimum(gcol - grow, 0.0)), 0.0)
        start = jnp.exp(gcol) * cc[:, 7:8]
        end = jnp.exp(jnp.minimum(gcol[CHUNK - 1 :, :] - gcol, 0.0)) * jnp.where(
            cc[:, 6:7] == cc[CHUNK - 1 :, 6:7], 1.0, 0.0
        )
        begin = state_in[0, s, h]
        low = begin.astype(bf16)
        inv = inv_in[s, h]
        upd = upd_in[s, :, vals]
        ds = dstate[s, h]
        dsl = ds.astype(bf16)
        kf = k.astype(f32)
        kend = (end * kf).astype(bf16)
        kk = mm(k, k, ((1,), (1,)))
        qk = mm(q, k, ((1,), (1,)))
        ks = mm(k, low)
        qs = mm(q, low)
        uds = mm(upd, dsl, ((1,), (1,)))
        kds = mm(kend, dsl)
        yield
        plain = jnp.where(row > col, decay * kk, 0.0)
        scores = decay * qk
        scores_low = scores.astype(bf16)
        mixed = (start * qs + mm(scores_low, upd)) * SCALE
        yield
        gate = pg[s, :, vals]
        sg = sigmoid(gate)
        silu = gate * sg
        rm = lax.rsqrt(jnp.mean(mixed * mixed, axis=1, keepdims=True) + EPSILON)
        scaled = mixed * rm
        dy = dgated[s, :, vals]
        dyn = dy * scaled
        gains = gain[:, vals]
        dgain[:, vals] += jnp.sum(dyn * silu, axis=0, keepdims=True)
        dgate = dyn * gains * (sg * (1.0 + gate * (1.0 - sg)))
        dproj[s, :, 2 * heads * DK + h * DV : 2 * heads * DK + (h + 1) * DV] = dgate.astype(bf16)
        weigh = jnp.sum(dgate * gate, axis=1, keepdims=True)
        dscaled = dy * gains * silu
        dmixed = rm * (dscaled - scaled * jnp.mean(dscaled * scaled, axis=1, keepdims=True))
        dout = dmixed * SCALE
        dlow = dout.astype(bf16)
        dupd = mm(scores_low, dlow, ((0,), (0,))) + kds
        dscore = mm(dlow, upd, ((1,), (1,)))
        dqs = mm(dlow, low, ((1,), (1,)))
        dfirst = mm((start * q.astype(f32)).astype(bf16), dlow, ((0,), (0,)))
        yield
        dright = mm(inv, dupd.astype(bf16), ((0,), (0,)))
        dsc = (dscore * decay).astype(bf16)
        dqn = start * dqs + mm(dsc, k)
        dkn = end * uds + mm(dsc, q, ((0,), (0,)))
        yield
        drl = dright.astype(bf16)
        dcoup = -mm(drl, upd, ((1,), (1,)))
        w = beta * dright
        wa = (start * w).astype(bf16)
        dkn = dkn - mm(wa, low, ((1,), (1,)))
        final = start[CHUNK - 1 :, :]
        dstate[s, h] = dfirst + final * ds - mm(k, wa, ((0,), (0,)))
        yield
        g = jnp.where(row > col, beta * dcoup * decay, 0.0)
        dkn = dkn + mm((g + g.T).astype(bf16), k)
        dbeta = jnp.sum(dright * (v - start * ks), axis=1, keepdims=True) + jnp.sum(
            dcoup * plain, axis=1, keepdims=True
        )
        dstart = jnp.sum(dout * qs - w * ks, axis=1, keepdims=True)
        dend = jnp.sum(kf * uds, axis=1, keepdims=True) * end
        z = dscore * scores + dcoup * (beta * plain)
        carried = jnp.sum(jnp.sum(ds * begin, axis=1, keepdims=True), axis=0, keepdims=True) * final
        carried = carried + jnp.sum(dend, axis=0, keepdims=True)
        dg = jnp.sum(z - z.T, axis=1, keepdims=True) + dstart * start - dend
        dg = dg + jnp.where(last, carried, 0.0)
        found[s, h] = (dbeta, dg, weigh)
        yield
        dq = rq * (dqn - qn * jnp.sum(dqn * qn, axis=1, keepdims=True))
        dk = rk * (dkn - kn * jnp.sum(dkn * kn, axis=1, keepdims=True))
        for grad, n, buf, part in ((dq, 0, tq, keys), (dk, 1, tk, keys), (w, 2, tv, vals)):
            sig = sigs[n][:, part]
            buf[s, 0:CHUNK, part] = grad * (sig * (1.0 + pres[n][:, part] * (1.0 - sig)))

    chains = [chain(s, h) for s in range(seqs) for h in range(heads)]
    while chains:
        chains = [c for c in chains if next(c, chains) is None]

    kw, vw = heads * DK, heads * DV
    for s in range(seqs):
        cc, masks = shared[s][:2]
        ahead = [cc[:, 3 + j : 4 + j] for j in range(CONV - 1)]
        dcol = jnp.zeros((CHUNK, 2 * heads + 1), f32)
        weigh = jnp.zeros((CHUNK, 1), f32)
        for h in range(heads):
            dbeta, dg, more = found[s, h]
            dcol = dcol + jnp.where(lane == h, dbeta, 0.0) + jnp.where(lane == heads + h, dg, 0.0)
            weigh = weigh + more
        dh, dl = split(dcol)
        dl2 = (dcol - dh.astype(f32) - dl.astype(f32)).astype(bf16)
        tail = ((0,), (0,))
        rev = mm(tril, dh, tail) + (mm(tril, dl, tail) + mm(tril, dl2, tail))
        for buf, src, at, weights, dw in ((tq, bq, 0, wq, dwq), (tk, bk, kw, wk, dwk), (tv, bv, 2 * kw + vw, wv, dwv)):
            pre = buf[s, 0:CHUNK, :]
            total = weights[0:1] * pre
            dw[0:1, :] += jnp.sum(pre * src[s, 8 : 8 + CHUNK, :], axis=0, keepdims=True)
            for j in range(1, CONV):
                total = total + weights[j : j + 1] * buf[s, j : j + CHUNK, :] * ahead[j - 1]
                dw[j : j + 1, :] += jnp.sum(
                    pre * masks[j - 1] * src[s, 8 - j : 8 - j + CHUNK, :], axis=0, keepdims=True
                )
            dproj[s, :, at : at + total.shape[1]] = total.astype(bf16)
            weigh = weigh + jnp.sum(total * src[s, 8 : 8 + CHUNK, :], axis=1, keepdims=True)
            buf[s, CHUNK : CHUNK + 8, :] = buf[s, 0:8, :]
        dcols[s] = jnp.where(lane < heads, dcol, jnp.where(lane < 2 * heads, rev, weigh))


def whole(shape):
    return pl.BlockSpec(shape, lambda c: (0,) * len(shape))


def mixer_forward(pq, pk, pv, pg, cols, rows, wq, wk, wv, gain):
    seqs = pq.shape[0]
    heads = pq.shape[2] // DK
    steps = SEQ // CHUNK
    kw, vw = heads * DK, heads * DV

    def tok(width):
        return pl.BlockSpec((seqs, CHUNK, width), lambda c: (0, c, 0))

    return pl.pallas_call(
        functools.partial(forward_kernel, heads, seqs),
        grid=(steps,),
        in_specs=[tok(kw), tok(kw), tok(vw), tok(vw), tok(cols.shape[2]),
                  pl.BlockSpec((seqs, rows.shape[1], CHUNK), lambda c: (0, 0, c)),
                  whole((CONV, kw)), whole((CONV, kw)), whole((CONV, vw)), whole((1, vw))],
        out_specs=[tok(vw),
                   pl.BlockSpec((seqs, heads, CHUNK, CHUNK), lambda c: (0, 0, c, 0)),
                   tok(vw),
                   pl.BlockSpec((1, seqs, heads, DK, DV), lambda c: (c, 0, 0, 0, 0))],
        out_shape=[jax.ShapeDtypeStruct((seqs, SEQ, vw), bf16),
                   jax.ShapeDtypeStruct((seqs, heads, SEQ, CHUNK), bf16),
                   jax.ShapeDtypeStruct((seqs, SEQ, vw), bf16),
                   jax.ShapeDtypeStruct((steps, seqs, heads, DK, DV), f32)],
        scratch_shapes=[pltpu.VMEM((seqs, heads, DK, DV), f32),
                        pltpu.VMEM((seqs, 8 + CHUNK, kw), f32),
                        pltpu.VMEM((seqs, 8 + CHUNK, kw), f32),
                        pltpu.VMEM((seqs, 8 + CHUNK, vw), f32)],
        compiler_params=pltpu.CompilerParams(dimension_semantics=("arbitrary",), vmem_limit_bytes=48 << 20),
        name="mixer_forward",
    )(pq, pk, pv, pg, cols, rows, wq, wk, wv, gain)


def mixer_backward(dgated, pq, pk, pv, pg, cols, rows, inv, upd, states, wq, wk, wv, gain):
    seqs = pq.shape[0]
    heads = pq.shape[2] // DK
    steps = SEQ // CHUNK
    kw, vw = heads * DK, heads * DV

    def tok(width):
        return pl.BlockSpec((seqs, CHUNK, width), lambda c: (0, steps - 1 - c, 0))

    def halo(width):
        return pl.BlockSpec(
            (seqs, 8, width),
            lambda c: (0, jnp.maximum((steps - 1 - c) * (CHUNK // 8) - 1, 0), 0),
        )

    return pl.pallas_call(
        functools.partial(backward_kernel, heads, seqs),
        grid=(steps,),
        in_specs=[tok(vw), tok(kw), tok(kw), tok(vw), tok(vw), halo(kw), halo(kw), halo(vw), tok(cols.shape[2]),
                  pl.BlockSpec((seqs, rows.shape[1], CHUNK), lambda c: (0, 0, steps - 1 - c)),
                  pl.BlockSpec((seqs, heads, CHUNK, CHUNK), lambda c: (0, 0, steps - 1 - c, 0)),
                  tok(vw),
                  pl.BlockSpec((1, seqs, heads, DK, DV), lambda c: (steps - 1 - c, 0, 0, 0, 0)),
                  whole((CONV, kw)), whole((CONV, kw)), whole((CONV, vw)), whole((1, vw))],
        out_specs=[tok(2 * kw + 2 * vw), tok(2 * heads + 1),
                   whole((CONV, kw)), whole((CONV, kw)), whole((CONV, vw)), whole((1, vw))],
        out_shape=[jax.ShapeDtypeStruct((seqs, SEQ, 2 * kw + 2 * vw), bf16),
                   jax.ShapeDtypeStruct((seqs, SEQ, 2 * heads + 1), f32),
                   jax.ShapeDtypeStruct((CONV, kw), f32),
                   jax.ShapeDtypeStruct((CONV, kw), f32),
                   jax.ShapeDtypeStruct((CONV, vw), f32),
                   jax.ShapeDtypeStruct((1, vw), f32)],
        scratch_shapes=[pltpu.VMEM((seqs, heads, DK, DV), f32)]
        + [pltpu.VMEM((seqs, 8 + CHUNK, width), f32) for width in (kw, kw, vw)] * 2,
        compiler_params=pltpu.CompilerParams(dimension_semantics=("arbitrary",), vmem_limit_bytes=56 << 20),
        name="mixer_backward",
    )(dgated, pq, pk, pv, pg, pq, pk, pv, cols, rows, inv, upd, states, wq, wk, wv, gain)


def token_tables(seg_ids, strength, log_decay):
    seqs = seg_ids.shape[0] // SEQ
    seg = seg_ids.reshape(seqs, 1, SEQ)
    position = lax.broadcasted_iota(jnp.int32, (1, 1, SEQ), 2)
    back, ahead = [], []
    for j in range(1, CONV):
        same = seg[:, :, j:] == seg[:, :, : SEQ - j]
        none = jnp.zeros((seqs, 1, j), jnp.bool_)
        back.append(jnp.concatenate([none, same], axis=2))
        ahead.append(jnp.concatenate([same, none], axis=2))
    before = jnp.concatenate([jnp.full((seqs, 1, 1), -1, jnp.int32), seg[:, :, CHUNK - 1 : SEQ - 1 : CHUNK]], axis=2)
    carry = seg == jnp.repeat(before, CHUNK, axis=2)
    heads = strength.shape[0]
    tables = [m.astype(f32) for m in back + ahead] + [seg.astype(f32), carry.astype(f32)]
    tables += [
        jnp.swapaxes(strength.reshape(heads, seqs, SEQ), 0, 1),
        jnp.swapaxes(log_decay.reshape(heads, seqs, SEQ), 0, 1),
    ]
    pad = 16 - 8 - 2 * heads
    if pad:
        tables.append(jnp.zeros((seqs, pad, SEQ), f32))
    rows = jnp.concatenate(tables, axis=1)
    return rows, jnp.swapaxes(rows, 1, 2)

TILE = 256
MESH = pl.DeviceIdType.MESH


def flip(value, bits):
    bit = 1
    while bit <= bits:
        if bits & bit:
            value = value + bit - 2 * bit * ((value // bit) % 2)
        bit *= 2
    return value


class Grid:
    def __init__(self):
        self.rows = lax.axis_size("row")
        self.cols = lax.axis_size("col")
        self.shard = D // self.rows
        self.block = D // self.cols
        self.parts = self.cols // self.rows
        self.half = self.cols // 2
        self.me = lax.axis_index("col")
        self.at = lax.axis_index("row")
        self.ids = jnp.stack([self.me, self.at]).astype(jnp.int32)
        self.slots = list(range(0, self.cols, 2)) + list(range(1, self.cols, 2))

    def swap(self, values, axis, bits):
        count = self.rows if axis == "row" else self.cols
        return lax.ppermute(values, axis, [(i, i ^ bits) for i in range(count)])

    def total(self, values, axis):
        bits = 1
        while bits < (self.rows if axis == "row" else self.cols):
            values = values + self.swap(values, axis, bits)
            bits *= 2
        return values

    def spread(self, values):
        return jnp.stack(
            [values]
            + [
                lax.ppermute(values, "row", [(i, (i + n) % self.rows) for i in range(self.rows)])
                for n in range(1, self.rows)
            ]
        )

    def gather_rows(self, values):
        return lax.all_gather(values, "row", axis=0, tiled=True)

    def sum_rows(self, term, axis):
        return lax.psum_scatter(term, "row", scatter_dimension=axis, tiled=True)


def fixed(array):
    return pl.BlockSpec(array.shape, lambda i, ids: (0,) * array.ndim, pipeline_mode=pl.Buffered(1))


def tokens_of(width, tile=TILE):
    return pl.BlockSpec((tile, width), lambda i, ids: (i, 0))


def slots_of(g):
    return pl.BlockSpec((g.cols, TILE, g.block), lambda i, ids: (0, i, 0))


def cost(flops, operands, outs):
    moved = sum(o.size * o.dtype.itemsize for o in operands)
    moved += sum(o.size * o.dtype.itemsize for o in outs)
    return pl.CostEstimate(flops=flops, bytes_accessed=moved, transcendentals=0)


def launch(kernel, grid, ids, operands, in_specs, out_specs, out_shape, scratch, name, flops):
    return pl.pallas_call(
        kernel,
        grid_spec=pltpu.PrefetchScalarGridSpec(
            num_scalar_prefetch=1, grid=grid, in_specs=in_specs, out_specs=out_specs, scratch_shapes=scratch
        ),
        out_shape=out_shape,
        compiler_params=pltpu.CompilerParams(
            dimension_semantics=("arbitrary",) * len(grid), vmem_limit_bytes=56 << 20
        ),
        cost_estimate=cost(flops, operands, out_shape),
        name=name,
    )(ids, *operands)


def place(g, ids, k):
    return pl.multiple_of((ids[0] ^ k) * g.block, g.block)


def dot_back(g, x, weights):
    return sum(
        mm(x[:, s * g.shard : (s + 1) * g.shard], weights[s], ((1,), (1,))) for s in range(g.rows)
    )


def dot_back_ring(g, ids, x, weights):
    total = 0.0
    for s in range(g.rows):
        shard = lax.rem(ids[1] - s + g.rows, g.rows)
        part = pl.ds(pl.multiple_of(shard * g.shard, g.shard), g.shard)
        total = total + mm(x[:, part], weights[s], ((1,), (1,)))
    return total


def project_kernel(g, widths, few, ids, blocks, gain, weight, ring, normed, scale, pq, pk, pg, pv, small):
    values = [blocks[k].astype(f32) for k in g.slots]
    squares = sum(jnp.sum(v * v, axis=1, keepdims=True) for v in values)
    scales = lax.rsqrt(squares / D + EPSILON)
    scale[...] = scales
    for k, v in zip(g.slots, values):
        at = place(g, ids, k)
        normed[:, pl.ds(at, g.block)] = (v * scales * gain[:, pl.ds(at, g.block)]).astype(bf16)
    x = normed[...]
    at = 0
    for out, width in zip((pq, pk, pg), widths):
        out[...] = mm(x, weight[:, at : at + width])
        at += width
    parts = [x[:, r * g.shard : (r + 1) * g.shard] for r in range(g.rows)]
    pv[...] = sum(mm(p, ring[r, : g.shard, :]) for r, p in enumerate(parts))
    small[...] = sum(
        mm(ring[r, g.shard : g.shard + few, : g.shard], p, ((1,), (1,))) for r, p in enumerate(parts)
    )


def project(g, blocks, gains, weight, ring, widths, few):
    tokens = blocks.shape[1]
    last = ring.shape[2]
    return launch(
        functools.partial(project_kernel, g, widths, few),
        (tokens // TILE,),
        g.ids,
        [blocks, gains, weight, ring],
        [slots_of(g)] + [fixed(w) for w in (gains, weight, ring)],
        [tokens_of(D), tokens_of(1)]
        + [tokens_of(w) for w in widths + [last]]
        + [pl.BlockSpec((few, TILE), lambda i, ids: (0, i))],
        [jax.ShapeDtypeStruct((tokens, D), bf16), jax.ShapeDtypeStruct((tokens, 1), f32)]
        + [jax.ShapeDtypeStruct((tokens, w), f32) for w in widths + [last]]
        + [jax.ShapeDtypeStruct((few, tokens), f32)],
        [],
        "project",
        2 * tokens * D * (sum(widths) + last + few),
    )


def ffn_kernel(g, ids, xs, ts, undo, wg, wu, wd, xr, tr, inner, dgate, dup, total, scale):
    squares = 0.0
    for k in g.slots:
        at = place(g, ids, k)
        x = xs[k]
        xr[:, pl.ds(at, g.block)] = x
        tr[:, pl.ds(at, g.block)] = ts[k]
        v = x.astype(f32)
        squares = squares + jnp.sum(v * v * undo[:, pl.ds(at, g.block)], axis=1, keepdims=True)
    scales = lax.rsqrt(squares / D + EPSILON)
    scale[...] = scales
    x = xr[...]
    gate = mm(x, wg[...]) * scales
    up = mm(x, wu[...]) * scales
    grad = dot_back_ring(g, ids, tr, wd)
    sig = sigmoid(gate)
    silu = gate * sig
    inner[...] = (silu * up).astype(bf16)
    dg = grad * up * (sig * (1.0 + gate * (1.0 - sig)))
    du = grad * silu
    total[...] = jnp.sum(dg * gate + du * up, axis=1, keepdims=True)
    dgate[...] = (dg * scales).astype(bf16)
    dup[...] = (du * scales).astype(bf16)


def ffn(g, xs, ts, undo, wg, wu, wd):
    tokens = xs.shape[1]
    width = wg.shape[1]
    return launch(
        functools.partial(ffn_kernel, g),
        (tokens // TILE,),
        g.ids,
        [xs, ts, undo, wg, wu, wd],
        [slots_of(g)] * 2 + [fixed(w) for w in (undo, wg, wu, wd)],
        [tokens_of(D)] * 2 + [tokens_of(width)] * 3 + [tokens_of(1)] * 2,
        [jax.ShapeDtypeStruct((tokens, D), bf16)] * 2
        + [jax.ShapeDtypeStruct((tokens, width), bf16)] * 3
        + [jax.ShapeDtypeStruct((tokens, 1), f32)] * 2,
        [],
        "ffn",
        6 * tokens * D * width,
    )


def back_gate_kernel(g, ids, ms, wo, mr, out):
    for k in g.slots:
        mr[:, pl.ds(place(g, ids, k), g.block)] = ms[k]
    out[...] = dot_back(g, mr, wo)


def back_gate(g, ms, wo):
    tokens = ms.shape[1]
    width = wo.shape[1]
    return launch(
        functools.partial(back_gate_kernel, g),
        (tokens // TILE,),
        g.ids,
        [ms, wo],
        [slots_of(g), fixed(wo)],
        [tokens_of(D), tokens_of(width)],
        [jax.ShapeDtypeStruct((tokens, D), bf16), jax.ShapeDtypeStruct((tokens, width), f32)],
        [],
        "back_gate",
        2 * tokens * D * width,
    )


class Sizes:
    def __init__(self, g):
        self.rows, self.cols, self.block, self.parts, self.shard, self.half = (
            g.rows, g.cols, g.block, g.parts, g.shard, g.half
        )


def piece(z, kind, y, weight, owner):
    if kind == "rows":
        return mm(y, weight[pl.ds(pl.multiple_of(owner * z.block, z.block), z.block), :], ((1,), (1,)))
    shard = owner // z.parts
    part = pl.ds(pl.multiple_of((owner % z.parts) * z.block, z.block), z.block)
    if kind == "cols":
        return mm(y, weight[shard, :, part])
    if kind == "ring":
        return mm(y, weight[(lax.axis_index("row") - shard + z.rows) % z.rows, :, part])
    if kind == "shards":
        return mm(y, weight[shard, part, :], ((1,), (1,)))
    return mm(y, weight[shard, z.shard : z.shard + y.shape[1], part])


def greet(devices):
    barrier = pltpu.get_barrier_semaphore()
    for axis, index in devices:
        pl.semaphore_signal(barrier, inc=1, device_id={axis: index}, device_id_type=MESH)
    pl.semaphore_wait(barrier, len(devices))


def remote(source, target, send, receive, axis, index):
    return pltpu.make_async_remote_copy(
        src_ref=source, dst_ref=target, send_sem=send, recv_sem=receive,
        device_id={axis: index}, device_id_type=MESH,
    )


class Ride:
    def __init__(self, z, own, whole, keep, send, receive):
        self.z, self.own, self.whole, self.kept, self.send, self.receive = z, own, whole, keep, send, receive
        self.at = lax.axis_index("row")

    def neighbours(self):
        rows = self.z.rows
        return [("row", (self.at + 1) % rows), ("row", (self.at + rows - 1) % rows)]

    def keep(self):
        return pltpu.make_async_copy(self.own, self.whole.at[self.at], self.kept)

    def step(self, n):
        rows = self.z.rows
        shard = (self.at + rows + 1 - n) % rows
        source = self.own if n == 1 else self.whole.at[shard]
        return remote(
            source, self.whole.at[shard], self.send.at[n], self.receive.at[n], "row", (self.at + 1) % rows
        )


class Rider:
    def __init__(self, z, kind, own, given, refs):
        self.z, self.kind, self.own, self.given = z, kind, own, given
        self.at = lax.axis_index("row")
        self.send, self.receive, self.spare = refs

    def step(self, n):
        rows = self.z.rows
        to = (self.at + n) % rows
        if self.kind == "spread":
            source, target = self.own, self.given.at[self.at]
        elif self.kind == "share":
            source = target = self.spare.at[self.at]
        else:
            part = pl.ds(pl.multiple_of(to * self.z.shard, self.z.shard), self.z.shard)
            source = self.own.at[:, part] if self.kind == "deal" else self.own.at[part, :]
            target = self.given.at[n - 1]
        return remote(source, target, self.send.at[n], self.receive.at[n], "row", to)

    def keep(self):
        return pltpu.make_async_copy(self.own, self.given.at[self.at], self.spare)

    def begin(self):
        if self.kind == "share":
            self.spare[self.at] = self.own[...]
        if self.kind == "spread":
            self.keep().start()
        for n in range(1, self.z.rows):
            self.step(n).start()

    def end(self):
        for n in range(1, self.z.rows):
            self.step(n).wait()
        if self.kind == "spread":
            self.keep().wait()
        if self.kind == "share":
            total = self.spare[0]
            for n in range(1, self.z.rows):
                total = total + self.spare[n]
            self.given[...] = total


DEEP = 4


def exchange_kernel(z, plan, steps, tile, *refs):
    groups, arrays, weights, gathers, kinds = plan
    ys, refs = refs[:arrays], refs[arrays:]
    ws, refs = refs[:weights], refs[weights:]
    extras, outs = [], []
    for group in groups:
        extras.append(refs[: group[2]])
        refs = refs[group[2] :]
    own, refs = refs[: len(kinds)], refs[len(kinds) :]
    for group in groups:
        outs.append(refs[: group[3]])
        refs = refs[group[3] :]
    if gathers:
        slots, refs = refs[0], refs[1:]
    given, refs = refs[: len(kinds)], refs[len(kinds) :]
    near, far, far_got, pair_got, refs = *refs[:4], refs[4:]
    far_s, far_r, pair_s, pair_r, refs = *refs[:4], refs[4:]
    if gathers:
        block, own_s, same_s, same_r, turn_s, turn_r, part_s, part_r, refs = *refs[:8], refs[8:]
    me = lax.axis_index("col")
    partner = flip(me, 1)
    peers = [flip(me, 2 * j) for j in range(1, z.half)]
    met = [("col", device) for device in [partner] + peers]
    riders = [
        Rider(z, kind, own[n], given[n], refs[3 * n : 3 * n + 3]) for n, kind in enumerate(kinds)
    ]
    if riders:
        met = met + [("row", (riders[0].at + n) % z.rows) for n in range(1, z.rows)]
    greet(met)

    def rows_at(i):
        return pl.ds(pl.multiple_of(i * tile, tile), tile)

    def send_far(n, i):
        return remote(far.at[n, i % DEEP], far_got.at[n, i], far_s.at[n, i], far_r.at[n, i], "col", partner)

    def send_pair(n, i, j):
        return remote(
            near.at[n, i % DEEP, j], pair_got.at[n, i, j - 1], pair_s.at[n, i, j], pair_r.at[n, i, j],
            "col", peers[j - 1],
        )

    def keep(i):
        return pltpu.make_async_copy(block.at[i], slots.at[0, rows_at(i), :], own_s.at[i])

    def send_part(i):
        return remote(block.at[i], slots.at[1, rows_at(i), :], part_s.at[i], part_r.at[i], "col", partner)

    def send_same(i, j):
        return remote(
            block.at[i], slots.at[2 * j, rows_at(i), :], same_s.at[i, j], same_r.at[i, j], "col", peers[j - 1]
        )

    def send_turn(i, j):
        return remote(
            slots.at[2 * j, rows_at(i), :], slots.at[2 * j + 1, rows_at(i), :],
            turn_s.at[i, j], turn_r.at[i, j], "col", partner,
        )

    def sent(i):
        for n in range(len(groups)):
            send_far(n, i).wait_send()
            for j in range(1, z.half):
                send_pair(n, i, j).wait_send()

    lag = 4 if gathers else 3
    loops = steps + lag - 1
    for rider in riders:
        rider.begin()

    @pl.loop(0, loops)
    def _(it):
        @pl.when((it >= DEEP) & (it < steps))
        def _():
            sent(it - DEEP)

        @pl.when(it < steps)
        def _():
            for n, group in enumerate(groups):
                terms = group[0]
                tiles = [ys[t[1]][rows_at(it), t[2] : t[3]] for t in terms]
                for side, held in ((1, far), (0, near)):
                    for j in range(z.half):
                        owner = flip(me, 2 * j + side)
                        total = sum(piece(z, t[0], y, ws[t[4]], owner) for t, y in zip(terms, tiles))
                        held[n, it % DEEP, j] = total.astype(bf16)
                    if side == 1:
                        send_far(n, it).start()

        @pl.when((it >= 1) & (it < steps + 1))
        def _():
            i = it - 1
            for n in range(len(groups)):
                send_far(n, i).wait_recv()
                for j in range(1, z.half):
                    near[n, i % DEEP, j] = (
                        near[n, i % DEEP, j].astype(f32) + far_got[n, i, j].astype(f32)
                    ).astype(bf16)
                    send_pair(n, i, j).start()

        @pl.when((it >= 2) & (it < steps + 2))
        def _():
            i = it - 2
            for n, group in enumerate(groups):
                total = near[n, i % DEEP, 0].astype(f32) + far_got[n, i, 0].astype(f32)
                for j in range(1, z.half):
                    send_pair(n, i, j).wait_recv()
                    total = total + pair_got[n, i, j - 1].astype(f32)
                result = group[1](rows_at(i), i, total, extras[n], outs[n])
                if gathers and n == 0:
                    block[i] = result
                    for j in range(1, z.half):
                        send_same(i, j).start()
                    send_part(i).start()
                    keep(i).start()

        if gathers:
            @pl.when(it >= 3)
            def _():
                i = it - 3
                for j in range(1, z.half):
                    send_same(i, j).wait_recv()
                    send_turn(i, j).start()

    @pl.loop(max(0, steps - DEEP), steps)
    def _(i):
        sent(i)

    if gathers:
        @pl.loop(0, steps)
        def _(i):
            keep(i).wait()
            send_part(i).wait()
            for j in range(1, z.half):
                send_same(i, j).wait_send()
                send_turn(i, j).wait()

    for rider in riders:
        rider.end()


def finish_middle(rows, i, total, extra, out):
    hidden, gain = extra
    middle = hidden[rows, :].astype(f32) + total
    out[0][rows, :] = middle
    return (middle * gain[...]).astype(bf16)


def finish_gradient(rows, i, total, extra, out):
    top, middle, gain, weigh = extra
    before = middle[rows, :]
    grad = top[rows, :].astype(f32) + gain[...] * total - before * weigh[rows, :]
    out[0][rows, :] = grad
    out[1][i] = jnp.sum(total * before, axis=0, keepdims=True)
    return grad.astype(bf16)


def finish_input(rows, i, total, extra, out):
    above, hidden, gain, scale, weigh = extra
    before = hidden[rows, :].astype(f32)
    scaled = scale[rows, :] * total
    out[0][rows, :] = above[rows, :] + gain[...] * scaled - before * weigh[rows, :]
    out[1][i] = jnp.sum(scaled * before, axis=0, keepdims=True)


def finish_out(rows, i, total, extra, out):
    (middle,) = extra
    out[0][rows, :] = (middle[rows, :] + total).astype(bf16)


def exchange(z, ys, ws, groups, gathers, number, riders=(), tile=TILE):
    tokens = ys[0].shape[0]
    steps = tokens // tile
    half, block, count = z.half, z.block, len(groups)
    vmem = pl.BlockSpec(memory_space=pltpu.VMEM)
    anywhere = pl.BlockSpec(memory_space=pl.ANY)
    dma = pltpu.SemaphoreType.DMA
    operands = [*ys, *ws]
    shapes = []
    for group in groups:
        operands += group[2]
        shapes += group[3]
    in_specs = [vmem] * len(operands)
    specs = [vmem] * len(shapes)
    scratch = [pltpu.VMEM((count, DEEP, half, tile, block), bf16)] * 2
    scratch += [pltpu.VMEM((count, steps, half, tile, block), bf16)]
    scratch += [pltpu.VMEM((count, steps, half - 1, tile, block), bf16)]
    scratch += [dma((count, steps))] * 2 + [dma((count, steps, half))] * 2
    if gathers:
        shapes.append(jax.ShapeDtypeStruct((z.cols, tokens, block), bf16))
        specs.append(anywhere)
        scratch += [pltpu.VMEM((steps, tile, block), bf16), dma((steps,))]
        scratch += [dma((steps, half))] * 4 + [dma((steps,))] * 2
    by_row = dma((z.rows,))
    for kind, own in riders:
        operands.append(own)
        in_specs.append(vmem if kind == "share" else anywhere)
        specs.append(in_specs[-1])
        scratch += [by_row] * 2
        if kind == "spread":
            shapes.append(jax.ShapeDtypeStruct((z.rows,) + own.shape, bf16))
            scratch.append(dma(()))
        elif kind == "share":
            shapes.append(jax.ShapeDtypeStruct(own.shape, f32))
            scratch.append(pltpu.VMEM((z.rows,) + own.shape, f32))
        else:
            part = (own.shape[0], z.shard) if kind == "deal" else (z.shard, own.shape[1])
            shapes.append(jax.ShapeDtypeStruct((z.rows - 1,) + part, bf16))
            scratch.append(dma(()))
    kinds = [(group[0], group[1], len(group[2]), len(group[3])) for group in groups]
    depth = sum(t[3] - t[2] for group in groups for t in group[0])
    return pl.pallas_call(
        functools.partial(
            exchange_kernel, z, (kinds, len(ys), len(ws), gathers, [kind for kind, _ in riders]), steps, tile
        ),
        in_specs=in_specs,
        out_specs=specs,
        out_shape=shapes,
        scratch_shapes=scratch,
        compiler_params=pltpu.CompilerParams(
            collective_id=number, has_side_effects=True, vmem_limit_bytes=60 << 20
        ),
        cost_estimate=cost(2 * tokens * z.cols * block * depth, operands, shapes),
        name="exchange",
    )(*operands)


def begin_kernel(z, count, *refs):
    owns, own, slots, whole = refs[:count], refs[count], refs[count + 1 : 2 * count + 1], refs[2 * count + 1]
    kept, same_s, same_r, part_s, part_r, turn_s, turn_r, keep_s, step_s, step_r = refs[2 * count + 2 :]
    me = lax.axis_index("col")
    partner = flip(me, 1)
    peers = [flip(me, 2 * j) for j in range(1, z.half)]
    ride = Ride(z, own, whole, keep_s, step_s, step_r)
    greet([("col", device) for device in [partner] + peers] + ride.neighbours())

    def keep(n):
        return pltpu.make_async_copy(owns[n], slots[n].at[0], kept.at[n])

    def send_same(n, j):
        return remote(owns[n], slots[n].at[2 * j], same_s.at[n, j], same_r.at[n, j], "col", peers[j - 1])

    def send_part(n):
        return remote(owns[n], slots[n].at[1], part_s.at[n], part_r.at[n], "col", partner)

    def send_turn(n, j):
        return remote(slots[n].at[2 * j], slots[n].at[2 * j + 1], turn_s.at[n, j], turn_r.at[n, j], "col", partner)

    ride.step(1).start()
    ride.keep().start()
    for n in range(count):
        for j in range(1, z.half):
            send_same(n, j).start()
        send_part(n).start()
        keep(n).start()
    for s in range(2, z.rows):
        ride.step(s - 1).wait_recv()
        ride.step(s).start()
    for n in range(count):
        for j in range(1, z.half):
            send_same(n, j).wait_recv()
            send_turn(n, j).start()
    ride.keep().wait()
    ride.step(z.rows - 1).wait_recv()
    for s in range(1, z.rows):
        ride.step(s).wait_send()
    for n in range(count):
        keep(n).wait()
        send_part(n).wait()
        for j in range(1, z.half):
            send_same(n, j).wait_send()
            send_turn(n, j).wait()


def begin(z, owns, own, number):
    anywhere = pl.BlockSpec(memory_space=pl.ANY)
    dma = pltpu.SemaphoreType.DMA
    count = len(owns)
    shapes = [jax.ShapeDtypeStruct((z.cols,) + o.shape, o.dtype) for o in owns]
    shapes.append(jax.ShapeDtypeStruct((z.rows,) + own.shape, own.dtype))
    operands = [*owns, own]
    return pl.pallas_call(
        functools.partial(begin_kernel, z, count),
        in_specs=[anywhere] * len(operands),
        out_specs=[anywhere] * len(shapes),
        out_shape=shapes,
        scratch_shapes=[dma((count,))] + [dma((count, z.half))] * 2 + [dma((count,))] * 2
        + [dma((count, z.half))] * 2 + [dma(())] + [dma((z.rows,))] * 2,
        compiler_params=pltpu.CompilerParams(collective_id=number, has_side_effects=True),
        cost_estimate=cost(10**6, operands, shapes),
        name="begin",
    )(*operands)


def rows_product(first_op, second_op):
    return lax.dot_general(
        first_op, second_op, (((0,), (0,)), ((), ())), preferred_element_type=f32
    )


def on_device(
    hidden_in,
    seg_ids,
    cotangent,
    norm_mixer,
    w_query,
    w_key,
    w_value,
    w_gate,
    w_beta,
    w_decay,
    decay_log,
    conv_query,
    conv_key,
    conv_value,
    norm_gated,
    w_out,
    norm_ffn,
    w_ffn_gate,
    w_ffn_up,
    w_ffn_down,
):
    g = Grid()
    z = Sizes(g)
    tokens = seg_ids.shape[0]
    seqs = tokens // SEQ
    heads = decay_log.shape[0]
    local = jax.ShapeDtypeStruct((tokens, g.block), f32)
    sums = jax.ShapeDtypeStruct((tokens // TILE, 1, g.block), f32)

    def by_seq(values):
        return values.reshape(seqs, SEQ, values.shape[1])

    def flat(values):
        return values.reshape(tokens, values.shape[2])

    few = 2 * heads
    ins = (w_query, w_key, w_gate)
    widths = [w.shape[1] for w in ins]
    inw = g.gather_rows(jnp.concatenate(ins, axis=1))
    wide = max(w_value.shape[1], g.shard)
    value_in = jnp.pad(w_value, ((0, 16), (0, wide - w_value.shape[1])))
    value_in = lax.dynamic_update_slice(
        value_in, jnp.concatenate([w_beta, w_decay], axis=1).T, (g.shard, 0)
    )
    ow = g.gather_rows(w_out[None])
    ew, uw = g.gather_rows(w_ffn_gate), g.gather_rows(w_ffn_up)
    own_gains = jnp.stack([norm_mixer, norm_ffn])
    own_gains = jnp.pad(own_gains, ((0, 6), (0, 0)))
    blocks, tops, gains, vw = begin(z, [hidden_in, cotangent, own_gains], value_in, 3)
    order = jnp.arange(g.cols) ^ g.me
    gains = jnp.swapaxes(jnp.take(gains[:, :2], order, axis=0), 0, 1).reshape(2, D)

    normed, scale_mixer, pq, pk, pg, pv, proj_small = project(g, blocks, gains[:1], inw, vw, widths, few)
    down_own, _ = lax.optimization_barrier((w_ffn_down, proj_small))
    dw = g.spread(down_own)
    projected = [by_seq(p) for p in (pq, pk, pv, pg)]
    proj_beta, proj_decay = proj_small[:heads], proj_small[heads:]
    strength = jax.nn.sigmoid(proj_beta)
    rate = -jnp.exp(decay_log)[:, None]
    log_decay = rate * jax.nn.softplus(proj_decay)
    rows, cols = token_tables(seg_ids, strength, log_decay)
    gain_gated = norm_gated[None]
    gated, inv, upd, states = mixer_forward(
        *projected, cols, rows, conv_query, conv_key, conv_value, gain_gated
    )
    gated = flat(gated)
    middle, mids = exchange(
        z, [gated], [ow],
        [([("cols", 0, 0, gated.shape[1], 0)], finish_middle, [hidden_in, norm_ffn[None]], [local])],
        True, 0,
    )
    undo = 1.0 / (gains[1:] * gains[1:])
    xr, tr, inner, dgate, dup, weigh, scale_ffn = ffn(g, mids, tops, undo, ew, uw, dw)
    weigh = scale_ffn * scale_ffn * g.total(weigh[:, 0], "col")[:, None] / D
    wide = [rows_product(xr, dgate), rows_product(xr, dup), rows_product(inner, tr)]
    wide = [w.astype(bf16) for w in wide]
    weigh = lax.optimization_barrier((weigh, *wide))[0]
    gate_grad, up_grad = (g.sum_rows(w, 0) for w in wide[:2])
    hidden_units = dgate.shape[1]
    grad_middle, norm_sums, downs, dealt = exchange(
        z, [dgate, dup], [ew, uw],
        [(
            [("rows", 0, 0, hidden_units, 0), ("rows", 1, 0, hidden_units, 1)], finish_gradient,
            [cotangent, middle, norm_ffn[None], weigh], [local, sums],
        )],
        True, 1, [("deal", wide[2])],
    )
    down_grad = lax.dynamic_slice(wide[2], (0, g.at * g.shard), (hidden_units, g.shard)).astype(f32)
    down_grad = sum((dealt[n].astype(f32) for n in range(g.rows - 1)), start=down_grad)
    grad_norm_ffn = jnp.sum(norm_sums, axis=(0, 1))
    mr, grad_gated = back_gate(g, downs, ow)
    out_term = rows_product(gated, mr).astype(bf16)
    grad_gated = lax.optimization_barrier((grad_gated, out_term))[0]
    out_term, up_grad = lax.optimization_barrier((out_term, up_grad))
    out_grad = g.sum_rows(out_term, 1)
    dproj, dcols, dwq, dwk, dwv, dgain = mixer_backward(
        by_seq(grad_gated), *projected, cols, rows, inv, upd, states,
        conv_query, conv_key, conv_value, gain_gated,
    )
    dproj = flat(dproj)
    most = sum(widths)
    in_grads = g.sum_rows(rows_product(normed, dproj).astype(bf16), 0)
    dsmall = flat(dcols).T
    dstrength, dlog = dsmall[:heads], dsmall[heads:few]
    grad_small = jnp.concatenate(
        [dstrength * strength * (1.0 - strength), dlog * rate * jax.nn.sigmoid(proj_decay)], axis=0
    )
    weigh = g.total(dsmall[few] + jnp.sum(grad_small * proj_small, axis=0), "col")[:, None]
    weigh = scale_mixer * scale_mixer * weigh / D
    grad_small = grad_small.astype(bf16)
    small_grads = jnp.dot(grad_small, normed, preferred_element_type=f32)
    grad_decay_log = jnp.sum(dlog * log_decay, axis=1)
    pieces = [dwq, dwk, dwv, dgain, grad_norm_ffn, grad_decay_log, small_grads]
    count = sum(p.size for p in pieces)
    fill = jnp.zeros((-count % 1024,), f32)
    joined = jnp.concatenate([p.reshape(-1) for p in pieces] + [fill]).reshape(-1, 128)
    grad_input, mixer_sums, block_out, joined = exchange(
        z, [dproj, grad_small.T, inner], [inw, vw, dw],
        [
            (
                [("rows", 0, 0, most, 0), ("shards", 0, most, dproj.shape[1], 1), ("small", 1, 0, few, 1)],
                finish_input, [grad_middle, hidden_in, norm_mixer[None], scale_mixer, weigh], [local, sums],
            ),
            (
                [("ring", 2, 0, hidden_units, 2)], finish_out, [middle],
                [jax.ShapeDtypeStruct((tokens, g.block), bf16)],
            ),
        ],
        False, 2, [("share", joined)],
    )
    joined = joined.reshape(-1)
    grad_norm_mixer = g.total(jnp.sum(mixer_sums, axis=(0, 1)), "row")
    summed, at = [], 0
    for p in pieces:
        summed.append(joined[at : at + p.size].reshape(p.shape))
        at += p.size
    small_grads = lax.dynamic_slice(summed[6], (0, g.at * g.shard), (few, g.shard)).T
    grads, at = [], 0
    for w in widths + [w_value.shape[1]]:
        grads.append(in_grads[:, at : at + w].astype(f32))
        at += w
    return (
        block_out,
        grad_input,
        grad_norm_mixer,
        grads[0],
        grads[1],
        grads[3],
        grads[2],
        small_grads[:, :heads],
        small_grads[:, heads:],
        summed[5],
        summed[0],
        summed[1],
        summed[2],
        summed[3][0],
        out_grad.astype(f32),
        summed[4],
        gate_grad.astype(f32),
        up_grad.astype(f32),
        down_grad,
    )


def solution(mesh):
    placed = (
        P("row", "col"),
        P("row"),
        P("row", "col"),
        P("col"),
        P("row", "col"),
        P("row", "col"),
        P("row", "col"),
        P("row", "col"),
        P("row", "col"),
        P("row", "col"),
        P("col"),
        P(None, "col"),
        P(None, "col"),
        P(None, "col"),
        P("col"),
        P("col", "row"),
        P("col"),
        P("row", "col"),
        P("row", "col"),
        P("col", "row"),
    )
    return jax.shard_map(
        on_device,
        mesh=mesh,
        in_specs=placed,
        out_specs=(
            P("row", "col"),
            P("row", "col"),
            P("col"),
            P("row", "col"),
            P("row", "col"),
            P("row", "col"),
            P("row", "col"),
            P("row", "col"),
            P("row", "col"),
            P("col"),
            P(None, "col"),
            P(None, "col"),
            P(None, "col"),
            P("col"),
            P("col", "row"),
            P("col"),
            P("row", "col"),
            P("row", "col"),
            P("col", "row"),
        ),
        check_vma=False,
    )
```

time: 912 us -> 797 us (0.87)
  waiting for transfers between devices: 212 us -> 57.8 us
  Pallas kernels: 533 us -> 592 us
  starting transfers between devices: 33.9 us -> 13.8 us
    ppermute x29 -> x8, waiting for transfers between devices: 125 us -> 3.87 us  [swap(): return lax.ppermute(values, axis, [(i, i ^ bits) for i in range(count)])]
    pallas_call x4, Pallas kernels: 332 us -> 444 us  [the longest x3 342 us: exchange(): pl.pallas_call(functools.partial(exchange_kernel, z, (kinds, len(ys), len...]
    reduce_scatter x5 -> x4, waiting for transfers between devices: 64.6 us -> 0.01 us  [sum_rows(): return lax.psum_scatter(term, 'row', scatter_dimension=axis, tiled=True)]
    pallas_call x1, Pallas kernels: 70.8 us -> 32 us  [mixer_forward(): pl.pallas_call(functools.partial(forward_kernel, heads, seqs), grid=(step...]
    all_gather x5 -> x4, waiting for transfers between devices: 21 us -> 53.1 us  [gather_rows(): return lax.all_gather(values, 'row', axis=0, tiled=True)]
    ppermute x29 -> x8, starting transfers between devices: 33.5 us -> 7.93 us  [swap(): return lax.ppermute(values, axis, [(i, i ^ bits) for i in range(count)])]
    pallas_call x1, Pallas kernels: 58 us -> 45 us  [mixer_backward(): pl.pallas_call(functools.partial(backward_kernel, heads, seqs), grid=(ste...]
  transfers between devices with their start and end apart: 39 -> 19, of which waited for: 12 -> 6; matrix products, arithmetic and copies ran while one was open for 10% -> 11% of each run, Pallas kernels for 42% -> 71%
where the time goes in v3:
time: 797 us; the launch traced here: 792 us
  Pallas kernels  592 us (74%)
  matrix products  64.6 us (8%)
  waiting for transfers between devices  57.8 us (7%)
  other arithmetic  26.1 us (3%)
  local copies, waits for them, and re-layouts  22.9 us (3%)
  between operations  15 us (2%)
  starting transfers between devices  13.8 us (2%)
    pallas_call x3, Pallas kernels, exchange(): pl.pallas_call(functools.partial(exchange_kernel, z, (kinds, len(ys), len...  342 us
    pallas_call x1, Pallas kernels, begin(): pl.pallas_call(functools.partial(begin_kernel, z, count), in_specs=[anywh...  102 us
    pallas_call x3, Pallas kernels, launch(): pl.pallas_call(kernel, grid_spec=pltpu.PrefetchScalarGridSpec(num_scalar_...  71.7 us
    dot_general x5, matrix products, rows_product(): lax.dot_general(first_op, second_op, (((0,), (0,)), ((), ())), preferred_...  60 us
    all_gather x4, waiting for transfers between devices, gather_rows(): return lax.all_gather(values, 'row', axis=0, tiled=True)  53.1 us
    pallas_call x1, Pallas kernels, mixer_backward(): pl.pallas_call(functools.partial(backward_kernel, heads, seqs), grid=(ste...  45 us
    pallas_call x1, Pallas kernels, mixer_forward(): pl.pallas_call(functools.partial(forward_kernel, heads, seqs), grid=(step...  32 us
  transfers between devices with their start and end apart: 19, of which 6 were waited for; matrix products, arithmetic and copies ran while one was open for 11% of the time, Pallas kernels for 71%

profile of v3, /device:TPU:0, one launch (start us, length us, event | category | flops | bytes accessed | tf_op | source)
XLA Modules:
  0.0 792.4 jit_solution(6203349966916499454)
XLA Ops:
  7.3 2.4 pad_maximum_fusion.1
  10.5 1.2 copy.61
  11.7 1.2 copy.60
  14.6 101.6 %begin.1 = (bf16[8,2048,256]{2,1,0:T(8,128)(2,1)}, bf16[8,2048,256]{2,1,0:T(8,128)(2,1)}, f32[8,8,256]{2,1,0:T(8,128)}, bf16[4,528,512]{2,1,0:T(8,128)(2,1)}) custom-call(bf16[2048,256]{1,0:T(8,128)(2,1)} %refs_7_.1, bf16[2048,256]{1,0:T(8,128)(2,1)} %refs_4_.1, f32[8,256]{1,0:T(8,128)} %select_maximum_fusion.refs_2_, bf16[528,512]{1,0:T(8,128)(2,1)} %copy-done.10), custom_call_target="tpu_custom_call" | custom-call | flops 1000000 | bytes 21651456 | tf_op jit(solution)/shard_map/begin/pallas_call | solution.py:1013
  119.6 5.8 all-gather.6.cloned.1.call-done.weight.refs_3_
  125.5 26.3 %project.1 = (bf16[2048,2048]{1,0:T(8,128)(2,1)}, f32[2048,1]{1,0:T(8,128)}, f32[2048,256]{1,0:T(8,128)}, f32[2048,256]{1,0:T(8,128)}, f32[2048,512]{1,0:T(8,128...) custom-call(s32[2]{0:T(128)} %pad_add_fusion.ids, bf16[8,2048,256]{2,1,0:T(8,128)(2,1)} %get-tuple-element.64.blocks, ...), custom_call_target="tpu_custom_call" | custom-call | flops 12918456320 | bytes 35766272 | tf_op jit(solution)/shard_map/project/pallas_call | solution.py:490
  151.8 2.1 collective-permute-start.1
  153.9 2.8 collective-permute-start.2
  156.7 0.9 fusion.1
  158.2 32.0 %mixer_forward.1 = (bf16[2,1024,512]{2,1,0:T(8,128)(2,1)S(1)}, bf16[2,2,1024,128]{3,2,1,0:T(8,128)(2,1)S(1)}, bf16[2,1024,512]{2,1,0:T(8,128)(2,1)}, f32[8,2,2,128,256]{4,3,2,1,0:T(8,128)}) custom-call(f32[2,1024,256]{2,1,0:T(8,128)} %bitcast.92, f32[2,1024,256]{2,1,0:T(8,128)} %bitcast.95, f32[2,1024,512]{2,1,0:T(8,128)} %bitcast.89, ...), custom_call_target="tpu_custom_call" | custom-call | tf_op jit(solution)/shard_map/mixer_forward/pallas_call | solution.py:332
  190.2 1.0 copy-done.2
  191.1 1.4 copy-done.7
  192.5 15.8 %all-gather.12.cloned.1.call-done = bf16[2048,512]{1,0:T(8,128)(2,1)} async-done(((bf16[512,512]{1,0:T(8,128)(2,1)}), bf16[2048,512]{1,0:T(8,128)(2,1)}) %all-gather.12.cloned.1.call-update) | async-done | bytes 2097168 | tf_op jit(solution)/shard_map/all_gather | solution.py:465
  208.3 104.7 %exchange.3 = (f32[2048,256]{1,0:T(8,128)}, bf16[8,2048,256]{2,1,0:T(8,128)(2,1)}) custom-call(bf16[2048,512]{1,0:T(8,128)(2,1)} %bitcast.87, bf16[4,512,512]{2,1,0:T(8,128)(2,1)} %bitcast.141, bf16[2048,256]{1,0:T(8,128)(2,1)} %refs_7_.1, f32[1,256]{1,0:T(1,128)} %bitcast.134), custom_call_target="tpu_custom_call" | custom-call | flops 4294967296 | bytes 15729664 | tf_op jit(solution)/shard_map/exchange/pallas_call | solution.py:943
  313.0 2.7 pad_maximum_fusion.wd.refs_5_
  315.8 31.4 %all-gather.8.cloned.1.call-done.wg.refs_2_ = bf16[2048,704]{1,0:T(8,128)(2,1)} async-done(((bf16[512,704]{1,0:T(8,128)(2,1)}), bf16[2048,704]{1,0:T(8,128)(2,1)}) %all-gather.8.cloned.1.call-update) | async-done | bytes 2883600 | tf_op jit(solution)/shard_map/all_gather | solution.py:465
  347.2 31.9 %ffn.1 = (bf16[2048,2048]{1,0:T(8,128)(2,1)}, bf16[2048,2048]{1,0:T(8,128)(2,1)}, bf16[2048,704]{1,0:T(8,128)(2,1)}, bf16[2048,704]{1,0:T(8,128)(2,1)}, bf16[204...) custom-call(s32[2]{0:T(128)} %pad_add_fusion.ids, bf16[8,2048,256]{2,1,0:T(8,128)(2,1)} %get-tuple-element.73.xs, ...), custom_call_target="tpu_custom_call" | custom-call | flops 17716740096 | bytes 50880512 | tf_op jit(solution)/shard_map/ffn/pallas_call | solution.py:490
  379.2 10.9 %convolution_convert_fusion.2 = bf16[2048,704]{0,1:T(8,128)(2,1)} fusion(bf16[2048,2048]{1,0:T(8,128)(2,1)} %get-tuple-element.81, bf16[2048,704]{1,0:T(8,128)(2,1)} %get-tuple-element.77.refs_1_), kind=kOutput, calls=%fused_computation.3 | convolution fusion | flops 5907021824 | bytes 14155776 | tf_op jit(solution)/shard_map/dot_general | solution.py:1027
  390.3 9.8 %convolution_convert_fusion.3 = bf16[2048,704]{0,1:T(8,128)(2,1)} fusion(bf16[2048,2048]{1,0:T(8,128)(2,1)} %get-tuple-element.81, bf16[2048,704]{1,0:T(8,128)(2,1)S(1)} %copy-done.35), kind=kOutput, calls=%fused_computation.4 | convolution fusion | flops 5907021824 | bytes 14155776 | tf_op jit(solution)/shard_map/dot_general | solution.py:1027
  400.2 1.1 copy-done.17
  401.8 1.2 collective-permute-done.3
  402.9 1.4 collective-permute-start.4
  404.3 2.2 collective-permute-done.4
  406.6 1.4 collective-permute-start.5
  408.0 10.8 %convolution_convert_fusion.1.refs_8_ = bf16[704,2048]{1,0:T(8,128)(2,1)} fusion(bf16[2048,704]{1,0:T(8,128)(2,1)} %get-tuple-element.82.refs_2_, bf16[2048,2048]{1,0:T(8,128)(2,1)} %get-tuple-element.83), kind=kOutput, calls=%fused_computation.2 | convolution fusion | flops 5907021824 | bytes 14155776 | tf_op jit(solution)/shard_map/dot_general | solution.py:1027
  419.2 1.1 multiply_multiply_fusion.1.refs_7_
  420.3 107.5 %exchange.4 = (f32[2048,256]{1,0:T(8,128)}, f32[8,1,256]{2,1,0:T(1,128)}, bf16[8,2048,256]{2,1,0:T(8,128)(2,1)}, bf16[3,704,512]{2,1,0:T(8,128)(2,1)}) custom-call(bf16[2048,704]{1,0:T(8,128)(2,1)} %get-tuple-element.76.refs_0_, bf16[2048,704]{1,0:T(8,128)(2,1)} %get-tuple-element.77.refs_1_, bf16[2048,704]{1,0:T(8,128)(2,1)} %all-gather.8.cloned.1.call-done.wg.refs_2_, ...), custom_call_target="tpu_custom_call" | custom-call | flops 11811160064 | bytes 30229504 | tf_op jit(solution)/shard_map/exchange/pallas_call | solution.py:943
  527.8 13.4 %back_gate.1 = (bf16[2048,2048]{1,0:T(8,128)(2,1)}, f32[2048,512]{1,0:T(8,128)}) custom-call(s32[2]{0:T(128)} %pad_add_fusion.ids, bf16[8,2048,256]{2,1,0:T(8,128)(2,1)} %get-tuple-element.85.ms, bf16[4,512,512]{2,1,0:T(8,128)(2,1)} %bitcast.142), custom_call_target="tpu_custom_call" | custom-call | flops 4294967296 | bytes 23068672 | tf_op jit(solution)/shard_map/back_gate/pallas_call | solution.py:490
  541.3 9.1 %convolution_convert_fusion.4 = bf16[512,2048]{1,0:T(8,128)(2,1)} fusion(bf16[2048,512]{1,0:T(8,128)(2,1)S(1)} %bitcast.88, bf16[2048,2048]{1,0:T(8,128)(2,1)} %get-tuple-element.87), kind=kOutput, calls=%fused_computation.5 | convolution fusion | flops 4296015872 | bytes 12582912 | tf_op jit(solution)/shard_map/dot_general | solution.py:1027
  550.9 45.0 %mixer_backward.1 = (bf16[2,1024,1536]{2,1,0:T(8,128)(2,1)}, f32[2,1024,5]{2,1,0:T(8,128)}, f32[4,256]{1,0:T(4,128)}, f32[4,256]{1,0:T(4,128)}, f32[4,512]{1,0:T(4,128)}, /*index=5*/f32[1,512]{1,0:T(1,128)}) custom-call(f32[2,1024,512]{2,1,0:T(8,128)} %bitcast.101, f32[2,1024,256]{2,1,0:T(8,128)} %bitcast.93, f32[2,1024,256]{2,1,0:T(8,128)} %bitcast.96, ...), custom_call_target="tpu_custom_call" | custom-call | tf_op jit(solution)/shard_map/mixer_backward/pallas_call | solution.py:370
  595.9 19.4 %convolution_convert_fusion = bf16[2048,1536]{1,0:T(8,128)(2,1)} fusion(bf16[2048,2048]{1,0:T(8,128)(2,1)} %get-tuple-element.101, bf16[2048,1536]{1,0:T(8,128)(2,1)} %bitcast.139), kind=kOutput, calls=%fused_computation.1 | convolution fusion | flops 12888047616 | bytes 20971520 | tf_op jit(solution)/shard_map/dot_general | solution.py:1027
  615.4 1.2 copy-done.16
  618.5 2.0 collective-permute-start.7
  620.5 4.6 convolution_bitcast_fusion
  625.4 2.6 convert_add_fusion
  629.3 1.1 multiply_multiply_fusion.refs_10_
  630.3 129.9 %exchange.5 = (f32[2048,256]{1,0:T(8,128)}, f32[8,1,256]{2,1,0:T(1,128)}, bf16[2048,256]{1,0:T(8,128)(2,1)}, f32[104,128]{1,0:T(8,128)}) custom-call(bf16[2048,1536]{1,0:T(8,128)(2,1)} %bitcast.140, bf16[2048,4]{1,0:T(8,128)(2,1)} %bitcast.100, bf16[2048,704]{1,0:T(8,128)(2,1)} %get-tuple-element.82.refs_2_, ...), custom_call_target="tpu_custom_call" | custom-call | flops 18824036352 | bytes 26952704 | tf_op jit(solution)/shard_map/exchange/pallas_call | solution.py:943
  763.8 1.3 slice_bitcast_fusion
  765.0 1.6 collective-permute-start.10
  766.6 1.2 slice_bitcast_fusion.1
  768.5 1.2 slice.161
  772.1 1.3 convert_element_type.124
  773.4 2.4 convert_element_type.123
  775.8 2.2 convert_element_type.122
  778.1 3.0 slice_convert_fusion
  781.0 2.1 slice_convert_fusion.2
  783.1 1.0 copy.74
  784.1 1.3 copy.75
  (163 shorter events, 18.1 us)
Async XLA Ops:
  7.2 3.3 copy-start.18
  7.2 4.5 copy-start.19
  7.2 118.2 %all-gather.6.cloned.1.call-start = ((), (), s32[]{:S(2)}) async-start(), calls=%async_computation.4 | async-start | bytes 5242880 | tf_op jit(solution)/shard_map/all_gather | solution.py:465
  9.6 3.4 copy-start.22
  9.6 3.5 copy-start.32
  9.6 3.5 copy-start.33
  9.6 4.1 copy-start.23
  9.7 4.1 copy-start.29
  9.7 4.1 copy-start.30
  9.7 198.6 %all-gather.12.cloned.1.call-start = ((), (), s32[]{:S(2)}) async-start(), calls=%async_computation.11 | async-start | bytes 2621440 | tf_op jit(solution)/shard_map/all_gather | solution.py:465
  10.4 305.3 %all-gather.10.cloned.1.call-start = ((), (), s32[]{:S(2)}) async-start(), calls=%async_computation.6 | async-start | bytes 3932160 | tf_op jit(solution)/shard_map/all_gather | solution.py:465
  11.7 107.1 %copy-start.34 = (f32[2]{0:T(128)S(1)}, f32[2]{0:T(128)}, u32[]{:S(2)}) copy-start(f32[2]{0:T(128)} %param.30) | copy-start | bytes 28
  11.7 335.5 %all-gather.8.cloned.1.call-start = ((), (), s32[]{:S(2)}) async-start(), calls=%async_computation.5 | async-start | bytes 3932160 | tf_op jit(solution)/shard_map/all_gather | solution.py:465
  12.9 537.5 %reduce-scatter.7.cloned.1.call-start = ((), (), s32[]{:S(2)}) async-start(), calls=%async_computation.8 | async-start | bytes 3604480 | tf_op jit(solution)/shard_map/reduce_scatter | solution.py:468
  125.4 26.3 %copy-start.21 = (bf16[704,512]{1,0:T(8,128)(2,1)S(1)}, bf16[704,512]{1,0:T(8,128)(2,1)}, u32[]{:S(2)}) copy-start(bf16[704,512]{1,0:T(8,128)(2,1)} %param.39) | copy-start | bytes 2162692
  125.4 32.7 %copy-start.3 = (f32[4,512]{1,0:T(4,128)S(1)}, f32[4,512]{1,0:T(4,128)}, u32[]{:S(2)}) copy-start(f32[4,512]{1,0:T(4,128)} %wv.3) | copy-start | bytes 24580
  125.5 32.7 %copy-start.4 = (f32[4,256]{1,0:T(4,128)S(1)}, f32[4,256]{1,0:T(4,128)}, u32[]{:S(2)}) copy-start(f32[4,256]{1,0:T(4,128)} %wq.3) | copy-start | bytes 12292
  125.5 32.7 %copy-start.5 = (f32[4,256]{1,0:T(4,128)S(1)}, f32[4,256]{1,0:T(4,128)}, u32[]{:S(2)}) copy-start(f32[4,256]{1,0:T(4,128)} %wk.3) | copy-start | bytes 12292
  125.5 32.7 %copy-start.6 = (f32[512]{0:T(512)S(1)}, f32[512]{0:T(512)}, u32[]{:S(2)}) copy-start(f32[512]{0:T(512)} %param.34) | copy-start | bytes 6148
  151.8 161.2 %collective-permute-start = (bf16[704,512]{1,0:T(8,128)(2,1)S(1)}, bf16[704,512]{1,0:T(8,128)(2,1)S(1)}, u32[]{:S(2)}, u32[]{:S(2)}) collective-permute-start(bf16[704,512]{1,0:T(8,128)(2,1)S(1)} %copy-done.21), channel_id=1, source_target_pairs={{0,8},{8,16},{16,24},{24,0},{1,9},{9,17},{17,25},{25,1},{2,10},{10... | collective-permute-start | bytes 2162696 | tf_op jit(solution)/shard_map/ppermute | solution.py:459
  151.8 161.2 %collective-permute-start.1 = (bf16[704,512]{1,0:T(8,128)(2,1)S(1)}, bf16[704,512]{1,0:T(8,128)(2,1)S(1)}, u32[]{:S(2)}, u32[]{:S(2)}) collective-permute-start(bf16[704,512]{1,0:T(8,128)(2,1)S(1)} %copy-done.21), channel_id=1, source_target_pairs={{0,16},{8,24},{16,0},{24,8},{1,17},{9,25},{17,1},{25,9},{2,18},{10... | collective-permute-start | bytes 2162696 | tf_op jit(solution)/shard_map/ppermute | solution.py:459
  153.9 159.1 %collective-permute-start.2 = (bf16[704,512]{1,0:T(8,128)(2,1)S(1)}, bf16[704,512]{1,0:T(8,128)(2,1)}, u32[]{:S(2)}, u32[]{:S(2)}) collective-permute-start(bf16[704,512]{1,0:T(8,128)(2,1)S(1)} %copy-done.21), channel_id=1, source_target_pairs={{0,24},{8,0},{16,8},{24,16},{1,25},{9,1},{17,9},{25,17},{2,26},{10... | collective-permute-start | bytes 2162696 | tf_op jit(solution)/shard_map/ppermute | solution.py:459
  157.8 32.4 %copy-start.1 = (f32[2,16,1024]{2,1,0:T(8,128)}, f32[2,16,1024]{2,1,0:T(8,128)S(1)}, u32[]{:S(2)}) copy-start(f32[2,16,1024]{2,1,0:T(8,128)S(1)} %concatenate.48.rows) | copy-start | bytes 393220
  158.1 32.0 %copy-start = (f32[2,1024,16]{2,1,0:T(8,128)}, f32[2,1024,16]{2,1,0:T(8,128)S(1)}, u32[]{:S(2)}) copy-start(f32[2,1024,16]{2,1,0:T(8,128)S(1)} %copy.59.cols) | copy-start | bytes 393220
  379.1 11.2 %copy-start.35 = (bf16[2048,704]{1,0:T(8,128)(2,1)S(1)}, bf16[2048,704]{1,0:T(8,128)(2,1)}, u32[]{:S(2)}) copy-start(bf16[2048,704]{1,0:T(8,128)(2,1)} %get-tuple-element.76.refs_0_) | copy-start | bytes 8650756
  390.1 383.4 %reduce-scatter.11.cloned.1.call-start = ((), (), s32[]{:S(2)}) async-start(), calls=%async_computation.10 | async-start | bytes 3604480 | tf_op jit(solution)/shard_map/reduce_scatter | solution.py:468
  400.1 375.7 %reduce-scatter.9.cloned.1.call-start = ((), (), s32[]{:S(2)}) async-start(), calls=%async_computation.9 | async-start | bytes 2621440 | tf_op jit(solution)/shard_map/reduce_scatter | solution.py:468
  401.7 1.2 collective-permute-start.3
  402.9 3.7 collective-permute-start.4
  406.6 12.2 %collective-permute-start.5 = (f32[2048]{0:T(1024)S(1)}, f32[2048]{0:T(1024)S(1)}, u32[]{:S(2)}, u32[]{:S(2)}) collective-permute-start(f32[2048]{0:T(1024)S(1)} %add.84), channel_id=1, source_target_pairs={{0,4},{1,5},{2,6},{3,7},{4,0},{5,1},{6,2},{7,3},{8,12},{9,13},{10,... | collective-permute-start | bytes 24584 | tf_op jit(solution)/shard_map/ppermute | solution.py:446
  408.0 11.2 %copy-start.14 = (f32[2048,1]{1,0:T(8,128)S(1)}, f32[2048,1]{1,0:T(8,128)}, u32[]{:S(2)}) copy-start(f32[2048,1]{1,0:T(8,128)} %get-tuple-element.79) | copy-start | bytes 24580
  527.8 13.4 %copy-start.8 = (bf16[2,1024,512]{2,1,0:T(8,128)(2,1)S(1)}, bf16[2,1024,512]{2,1,0:T(8,128)(2,1)}, u32[]{:S(2)}) copy-start(bf16[2,1024,512]{2,1,0:T(8,128)(2,1)} %copy-done.7) | copy-start | bytes 6291460
  550.4 227.7 %reduce-scatter.5.cloned.1.call-start = ((), (), s32[]{:S(2)}) async-start(), calls=%async_computation.7 | async-start | bytes 7864320 | tf_op jit(solution)/shard_map/reduce_scatter | solution.py:468
  617.1 1.4 collective-permute-start.6
  618.0 7.1 copy-start.9
  618.5 6.9 copy-start.11
  618.5 6.6 collective-permute-start.7
  625.1 3.0 copy-start.28
  625.1 3.0 copy-start.27
  625.1 3.0 copy-start.25
  625.1 3.1 copy-start.31
  625.1 4.1 copy-start.13
  625.2 3.7 collective-permute-start.8
  630.3 141.8 %copy-start.20 = (bf16[512,704]{0,1:T(8,128)(2,1)S(1)}, bf16[512,704]{0,1:T(8,128)(2,1)}, u32[]{:S(2)}) copy-start(bf16[512,704]{0,1:T(8,128)(2,1)} %reduce-scatter.7.cloned.1.call-done) | copy-start | bytes 2162692
  761.0 4.1 collective-permute-start.9
  765.0 6.5 collective-permute-start.10
  775.8 7.3 copy-start.15
  778.1 6.0 copy-start.12
  (7 other events, 10.2 us)
Sparse Core Ops, SparseCore 0:
  10.2 115.2 all-gather.5
  127.0 81.2 all-gather.11
  210.5 71.9 all-gather.9
  284.5 62.6 all-gather.7
  390.2 80.5 reduce-scatter.6
  472.9 79.8 reduce-scatter.10
  555.1 55.9 reduce-scatter.8
  615.5 130.8 reduce-scatter.4

commit v4 on v3

--- a/solution.py
+++ b/solution.py
@@ -416,6 +416,7 @@
     return rows, jnp.swapaxes(rows, 1, 2)
 
 TILE = 256
+STEP = 256
 MESH = pl.DeviceIdType.MESH
 
 
@@ -511,12 +512,12 @@
     )
 
 
-def dot_back_ring(g, ids, x, weights):
+def ring_dot(g, ids, x, weights):
     total = 0.0
     for s in range(g.rows):
         shard = lax.rem(ids[1] - s + g.rows, g.rows)
         part = pl.ds(pl.multiple_of(shard * g.shard, g.shard), g.shard)
-        total = total + mm(x[:, part], weights[s], ((1,), (1,)))
+        total = total + mm(x[:, part], weights[s])
     return total
 
 
@@ -561,21 +562,42 @@
     )
 
 
-def ffn_kernel(g, ids, xs, ts, undo, wg, wu, wd, xr, tr, inner, dgate, dup, total, scale):
+def inner_kernel(g, ids, ts, wd, tr, grad):
+    for k in g.slots:
+        tr[:, pl.ds(place(g, ids, k), g.block)] = ts[k]
+    grad[...] = dot_back(g, tr, wd)
+
+
+def inner_gradient(g, ts, wd):
+    tokens = ts.shape[1]
+    width = wd.shape[1]
+    return launch(
+        functools.partial(inner_kernel, g),
+        (tokens // TILE,),
+        g.ids,
+        [ts, wd],
+        [slots_of(g), fixed(wd)],
+        [tokens_of(D), tokens_of(width)],
+        [jax.ShapeDtypeStruct((tokens, D), bf16), jax.ShapeDtypeStruct((tokens, width), f32)],
+        [],
+        "inner_gradient",
+        2 * tokens * D * width,
+    )
+
+
+def ffn_kernel(g, ids, xs, grads, undo, wg, wu, xr, inner, dgate, dup, total, scale):
     squares = 0.0
     for k in g.slots:
         at = place(g, ids, k)
         x = xs[k]
         xr[:, pl.ds(at, g.block)] = x
-        tr[:, pl.ds(at, g.block)] = ts[k]
         v = x.astype(f32)
         squares = squares + jnp.sum(v * v * undo[:, pl.ds(at, g.block)], axis=1, keepdims=True)
     scales = lax.rsqrt(squares / D + EPSILON)
     scale[...] = scales
-    x = xr[...]
-    gate = mm(x, wg[...]) * scales
-    up = mm(x, wu[...]) * scales
-    grad = dot_back_ring(g, ids, tr, wd)
+    gate = mm(xr[...], wg[...]) * scales
+    up = ring_dot(g, ids, xr, wu) * scales
+    grad = grads[...]
     sig = sigmoid(gate)
     silu = gate * sig
     inner[...] = (silu * up).astype(bf16)
@@ -586,22 +608,22 @@
     dup[...] = (du * scales).astype(bf16)
 
 
-def ffn(g, xs, ts, undo, wg, wu, wd):
+def ffn(g, xs, grads, undo, wg, wu):
     tokens = xs.shape[1]
     width = wg.shape[1]
     return launch(
         functools.partial(ffn_kernel, g),
         (tokens // TILE,),
         g.ids,
-        [xs, ts, undo, wg, wu, wd],
-        [slots_of(g)] * 2 + [fixed(w) for w in (undo, wg, wu, wd)],
-        [tokens_of(D)] * 2 + [tokens_of(width)] * 3 + [tokens_of(1)] * 2,
-        [jax.ShapeDtypeStruct((tokens, D), bf16)] * 2
+        [xs, grads, undo, wg, wu],
+        [slots_of(g), tokens_of(width)] + [fixed(w) for w in (undo, wg, wu)],
+        [tokens_of(D)] + [tokens_of(width)] * 3 + [tokens_of(1)] * 2,
+        [jax.ShapeDtypeStruct((tokens, D), bf16)]
         + [jax.ShapeDtypeStruct((tokens, width), bf16)] * 3
         + [jax.ShapeDtypeStruct((tokens, 1), f32)] * 2,
         [],
         "ffn",
-        6 * tokens * D * width,
+        4 * tokens * D * width,
     )
 
 
@@ -642,8 +664,9 @@
     part = pl.ds(pl.multiple_of((owner % z.parts) * z.block, z.block), z.block)
     if kind == "cols":
         return mm(y, weight[shard, :, part])
-    if kind == "ring":
-        return mm(y, weight[(lax.axis_index("row") - shard + z.rows) % z.rows, :, part])
+    slot = (lax.axis_index("row") - shard + z.rows) % z.rows
+    if kind == "ring_rows":
+        return mm(y, weight[slot, part, :], ((1,), (1,)))
     if kind == "shards":
         return mm(y, weight[shard, part, :], ((1,), (1,)))
     return mm(y, weight[shard, z.shard : z.shard + y.shape[1], part])
@@ -695,7 +718,7 @@
         to = (self.at + n) % rows
         if self.kind == "spread":
             source, target = self.own, self.given.at[self.at]
-        elif self.kind == "share":
+        elif self.kind in ("share", "late"):
             source = target = self.spare.at[self.at]
         else:
             part = pl.ds(pl.multiple_of(to * self.z.shard, self.z.shard), self.z.shard)
@@ -706,7 +729,14 @@
     def keep(self):
         return pltpu.make_async_copy(self.own, self.given.at[self.at], self.spare)
 
+    def fill(self, values):
+        self.spare[self.at] = jnp.broadcast_to(values, self.own.shape)
+        for n in range(1, self.z.rows):
+            self.step(n).start()
+
     def begin(self):
+        if self.kind == "late":
+            return
         if self.kind == "share":
             self.spare[self.at] = self.own[...]
         if self.kind == "spread":
@@ -719,7 +749,7 @@
             self.step(n).wait()
         if self.kind == "spread":
             self.keep().wait()
-        if self.kind == "share":
+        if self.kind in ("share", "late"):
             total = self.spare[0]
             for n in range(1, self.z.rows):
                 total = total + self.spare[n]
@@ -867,6 +897,13 @@
                 send_turn(i, j).wait()
 
     for rider in riders:
+        if rider.kind == "late":
+            partial = outs[0][1]
+            total = partial[0]
+            for i in range(1, steps):
+                total = total + partial[i]
+            rider.fill(total)
+    for rider in riders:
         rider.end()
 
 
@@ -899,7 +936,7 @@
     out[0][rows, :] = (middle[rows, :] + total).astype(bf16)
 
 
-def exchange(z, ys, ws, groups, gathers, number, riders=(), tile=TILE):
+def exchange(z, ys, ws, groups, gathers, number, riders=(), tile=STEP):
     tokens = ys[0].shape[0]
     steps = tokens // tile
     half, block, count = z.half, z.block, len(groups)
@@ -925,13 +962,13 @@
     by_row = dma((z.rows,))
     for kind, own in riders:
         operands.append(own)
-        in_specs.append(vmem if kind == "share" else anywhere)
+        in_specs.append(vmem if kind in ("share", "late") else anywhere)
         specs.append(in_specs[-1])
         scratch += [by_row] * 2
         if kind == "spread":
             shapes.append(jax.ShapeDtypeStruct((z.rows,) + own.shape, bf16))
             scratch.append(dma(()))
-        elif kind == "share":
+        elif kind in ("share", "late"):
             shapes.append(jax.ShapeDtypeStruct(own.shape, f32))
             scratch.append(pltpu.VMEM((z.rows,) + own.shape, f32))
         else:
@@ -1057,7 +1094,7 @@
     seqs = tokens // SEQ
     heads = decay_log.shape[0]
     local = jax.ShapeDtypeStruct((tokens, g.block), f32)
-    sums = jax.ShapeDtypeStruct((tokens // TILE, 1, g.block), f32)
+    sums = jax.ShapeDtypeStruct((tokens // STEP, 1, g.block), f32)
 
     def by_seq(values):
         return values.reshape(seqs, SEQ, values.shape[1])
@@ -1075,7 +1112,8 @@
         value_in, jnp.concatenate([w_beta, w_decay], axis=1).T, (g.shard, 0)
     )
     ow = g.gather_rows(w_out[None])
-    ew, uw = g.gather_rows(w_ffn_gate), g.gather_rows(w_ffn_up)
+    dw = g.gather_rows(w_ffn_down[None])
+    ew = g.gather_rows(w_ffn_gate)
     own_gains = jnp.stack([norm_mixer, norm_ffn])
     own_gains = jnp.pad(own_gains, ((0, 6), (0, 0)))
     blocks, tops, gains, vw = begin(z, [hidden_in, cotangent, own_gains], value_in, 3)
@@ -1083,8 +1121,8 @@
     gains = jnp.swapaxes(jnp.take(gains[:, :2], order, axis=0), 0, 1).reshape(2, D)
 
     normed, scale_mixer, pq, pk, pg, pv, proj_small = project(g, blocks, gains[:1], inw, vw, widths, few)
-    down_own, _ = lax.optimization_barrier((w_ffn_down, proj_small))
-    dw = g.spread(down_own)
+    up_own, _ = lax.optimization_barrier((w_ffn_up, proj_small))
+    uw = g.spread(up_own)
     projected = [by_seq(p) for p in (pq, pk, pv, pg)]
     proj_beta, proj_decay = proj_small[:heads], proj_small[heads:]
     strength = jax.nn.sigmoid(proj_beta)
@@ -1102,23 +1140,34 @@
         True, 0,
     )
     undo = 1.0 / (gains[1:] * gains[1:])
-    xr, tr, inner, dgate, dup, weigh, scale_ffn = ffn(g, mids, tops, undo, ew, uw, dw)
-    weigh = scale_ffn * scale_ffn * g.total(weigh[:, 0], "col")[:, None] / D
-    wide = [rows_product(xr, dgate), rows_product(xr, dup), rows_product(inner, tr)]
-    wide = [w.astype(bf16) for w in wide]
+    tops = lax.optimization_barrier((tops, middle))[0]
+    tr, grad_inner = inner_gradient(g, tops, dw)
+    mids = lax.optimization_barrier((mids, grad_inner))[0]
+    xr, inner, dgate, dup, weigh, scale_ffn = ffn(g, mids, grad_inner, undo, ew, uw)
+    weigh = weigh[:, 0]
+    wide = [rows_product(xr, dgate).astype(bf16)]
+    weigh = weigh + g.swap(weigh, "col", 1)
+    weigh, left = lax.optimization_barrier((weigh, dup))
+    wide.append(rows_product(xr, left).astype(bf16))
+    weigh = weigh + g.swap(weigh, "col", 2)
+    weigh, left = lax.optimization_barrier((weigh, inner))
+    wide.append(rows_product(left, tr).astype(bf16))
+    bits = 4
+    while bits < g.cols:
+        weigh = weigh + g.swap(weigh, "col", bits)
+        bits *= 2
+    weigh = scale_ffn * scale_ffn * weigh[:, None] / D
     weigh = lax.optimization_barrier((weigh, *wide))[0]
-    gate_grad, up_grad = (g.sum_rows(w, 0) for w in wide[:2])
+    gate_grad, up_grad, down_grad = (g.sum_rows(w, axis) for w, axis in zip(wide, (0, 0, 1)))
     hidden_units = dgate.shape[1]
-    grad_middle, norm_sums, downs, dealt = exchange(
+    grad_middle, norm_sums, downs = exchange(
         z, [dgate, dup], [ew, uw],
         [(
-            [("rows", 0, 0, hidden_units, 0), ("rows", 1, 0, hidden_units, 1)], finish_gradient,
+            [("rows", 0, 0, hidden_units, 0), ("ring_rows", 1, 0, hidden_units, 1)], finish_gradient,
             [cotangent, middle, norm_ffn[None], weigh], [local, sums],
         )],
-        True, 1, [("deal", wide[2])],
-    )
-    down_grad = lax.dynamic_slice(wide[2], (0, g.at * g.shard), (hidden_units, g.shard)).astype(f32)
-    down_grad = sum((dealt[n].astype(f32) for n in range(g.rows - 1)), start=down_grad)
+        True, 1,
+    )
     grad_norm_ffn = jnp.sum(norm_sums, axis=(0, 1))
     mr, grad_gated = back_gate(g, downs, ow)
     out_term = rows_product(gated, mr).astype(bf16)
@@ -1146,7 +1195,7 @@
     count = sum(p.size for p in pieces)
     fill = jnp.zeros((-count % 1024,), f32)
     joined = jnp.concatenate([p.reshape(-1) for p in pieces] + [fill]).reshape(-1, 128)
-    grad_input, mixer_sums, block_out, joined = exchange(
+    grad_input, _, block_out, joined, grad_norm_mixer = exchange(
         z, [dproj, grad_small.T, inner], [inw, vw, dw],
         [
             (
@@ -1154,14 +1203,14 @@
                 finish_input, [grad_middle, hidden_in, norm_mixer[None], scale_mixer, weigh], [local, sums],
             ),
             (
-                [("ring", 2, 0, hidden_units, 2)], finish_out, [middle],
+                [("cols", 2, 0, hidden_units, 2)], finish_out, [middle],
                 [jax.ShapeDtypeStruct((tokens, g.block), bf16)],
             ),
         ],
-        False, 2, [("share", joined)],
+        False, 2, [("share", joined), ("late", jnp.zeros((8, g.block), f32))],
     )
     joined = joined.reshape(-1)
-    grad_norm_mixer = g.total(jnp.sum(mixer_sums, axis=(0, 1)), "row")
+    grad_norm_mixer = grad_norm_mixer[0]
     summed, at = [], 0
     for p in pieces:
         summed.append(joined[at : at + p.size].reshape(p.shape))
@@ -1190,7 +1239,7 @@
         summed[4],
         gate_grad.astype(f32),
         up_grad.astype(f32),
-        down_grad,
+        down_grad.astype(f32),
     )
 
 

time: 797 us -> 775 us (0.972)
  waiting for transfers between devices: 57.8 us -> 43.7 us
    all_gather x4, waiting for transfers between devices: 53.1 us -> 32.6 us  [gather_rows(): return lax.all_gather(values, 'row', axis=0, tiled=True)]
    pallas_call x3, Pallas kernels: 342 us -> 330 us  [exchange(): pl.pallas_call(functools.partial(exchange_kernel, z, (kinds, len(ys), len...]
    pallas_call x3 -> x4, Pallas kernels: 71.7 us -> 78.8 us  [launch(): pl.pallas_call(kernel, grid_spec=pltpu.PrefetchScalarGridSpec(num_scalar_...]
  transfers between devices with their start and end apart: 19 -> 18, of which waited for: 6 -> 8; matrix products, arithmetic and copies ran while one was open for 11% -> 12% of each run, Pallas kernels for 71% -> 73%
where the time goes in v4:
time: 775 us; the launch traced here: 770 us
  Pallas kernels  587 us (76%)
  matrix products  65.6 us (8%)
  waiting for transfers between devices  43.7 us (6%)
  local copies, waits for them, and re-layouts  25.6 us (3%)
  other arithmetic  24.9 us (3%)
  between operations  14.7 us (2%)
  starting transfers between devices  8.12 us (1%)
    pallas_call x3, Pallas kernels, exchange(): pl.pallas_call(functools.partial(exchange_kernel, z, (kinds, len(ys), len...  330 us
    pallas_call x1, Pallas kernels, begin(): pl.pallas_call(functools.partial(begin_kernel, z, count), in_specs=[anywh...  102 us
    pallas_call x4, Pallas kernels, launch(): pl.pallas_call(kernel, grid_spec=pltpu.PrefetchScalarGridSpec(num_scalar_...  78.8 us
    dot_general x5, matrix products, rows_product(): lax.dot_general(first_op, second_op, (((0,), (0,)), ((), ())), preferred_...  60.9 us
    pallas_call x1, Pallas kernels, mixer_backward(): pl.pallas_call(functools.partial(backward_kernel, heads, seqs), grid=(ste...  45.5 us
    all_gather x4, waiting for transfers between devices, gather_rows(): return lax.all_gather(values, 'row', axis=0, tiled=True)  32.6 us
    pallas_call x1, Pallas kernels, mixer_forward(): pl.pallas_call(functools.partial(forward_kernel, heads, seqs), grid=(step...  32 us
  transfers between devices with their start and end apart: 18, of which 8 were waited for; matrix products, arithmetic and copies ran while one was open for 12% of the time, Pallas kernels for 73%

profile of v4, /device:TPU:0, one launch (start us, length us, event | category | flops | bytes accessed | tf_op | source)
XLA Modules:
  0.0 770.0 jit_solution(2359875504789972106)
XLA Ops:
  7.3 2.3 pad_maximum_fusion.1
  11.2 1.2 copy.66
  14.2 101.6 %begin.1 = (bf16[8,2048,256]{2,1,0:T(8,128)(2,1)}, bf16[8,2048,256]{2,1,0:T(8,128)(2,1)}, f32[8,8,256]{2,1,0:T(8,128)}, bf16[4,528,512]{2,1,0:T(8,128)(2,1)}) custom-call(bf16[2048,256]{1,0:T(8,128)(2,1)} %refs_7_.1, bf16[2048,256]{1,0:T(8,128)(2,1)} %refs_4_.1, f32[8,256]{1,0:T(8,128)} %select_maximum_fusion.refs_2_, bf16[528,512]{1,0:T(8,128)(2,1)} %copy-done.10), custom_call_target="tpu_custom_call" | custom-call | flops 1000000 | bytes 21651456 | tf_op jit(solution)/shard_map/begin/pallas_call | solution.py:1050
  119.1 6.0 all-gather.7.cloned.1.call-done.weight.refs_3_
  125.1 26.3 %project.1 = (bf16[2048,2048]{1,0:T(8,128)(2,1)}, f32[2048,1]{1,0:T(8,128)}, f32[2048,256]{1,0:T(8,128)}, f32[2048,256]{1,0:T(8,128)}, f32[2048,512]{1,0:T(8,128...) custom-call(s32[2]{0:T(128)} %pad_add_fusion.ids, bf16[8,2048,256]{2,1,0:T(8,128)(2,1)} %get-tuple-element.70.blocks, ...), custom_call_target="tpu_custom_call" | custom-call | flops 12918456320 | bytes 35766272 | tf_op jit(solution)/shard_map/project/pallas_call | solution.py:491
  151.4 1.8 collective-permute-start.1
  153.3 2.1 collective-permute-start.2
  156.9 32.0 %mixer_forward.1 = (bf16[2,1024,512]{2,1,0:T(8,128)(2,1)S(1)}, bf16[2,2,1024,128]{3,2,1,0:T(8,128)(2,1)S(1)}, bf16[2,1024,512]{2,1,0:T(8,128)(2,1)}, f32[8,2,2,128,256]{4,3,2,1,0:T(8,128)}) custom-call(f32[2,1024,256]{2,1,0:T(8,128)} %bitcast.85, f32[2,1024,256]{2,1,0:T(8,128)} %bitcast.88, f32[2,1024,512]{2,1,0:T(8,128)} %bitcast.82, ...), custom_call_target="tpu_custom_call" | custom-call | tf_op jit(solution)/shard_map/mixer_forward/pallas_call | solution.py:332
  189.9 1.3 copy-done.7
  191.2 16.7 %all-gather.11.cloned.1.call-done = bf16[2048,512]{1,0:T(8,128)(2,1)} async-done(((bf16[512,512]{1,0:T(8,128)(2,1)}), bf16[2048,512]{1,0:T(8,128)(2,1)}) %all-gather.11.cloned.1.call-update) | async-done | bytes 2097168 | tf_op jit(solution)/shard_map/all_gather | solution.py:466
  207.9 104.7 %exchange.3 = (f32[2048,256]{1,0:T(8,128)}, bf16[8,2048,256]{2,1,0:T(8,128)(2,1)}) custom-call(bf16[2048,512]{1,0:T(8,128)(2,1)} %bitcast.80, bf16[4,512,512]{2,1,0:T(8,128)(2,1)} %bitcast.138, bf16[2048,256]{1,0:T(8,128)(2,1)} %refs_7_.1, f32[1,256]{1,0:T(1,128)} %bitcast.128), custom_call_target="tpu_custom_call" | custom-call | flops 4294967296 | bytes 15729664 | tf_op jit(solution)/shard_map/exchange/pallas_call | solution.py:980
  312.9 14.7 %inner_gradient.1 = (bf16[2048,2048]{1,0:T(8,128)(2,1)}, f32[2048,704]{1,0:T(8,128)}) custom-call(s32[2]{0:T(128)} %pad_add_fusion.ids, bf16[8,2048,256]{2,1,0:T(8,128)(2,1)} %get-tuple-element.82.ts, bf16[4,704,512]{2,1,0:T(8,128)(2,1)} %bitcast.136), custom_call_target="tpu_custom_call" | custom-call | flops 5905580032 | bytes 25427968 | tf_op jit(solution)/shard_map/inner_gradient/pallas_call | solution.py:491
  328.0 1.4 copy.69
  329.4 1.4 copy.70
  330.8 1.9 pad_maximum_fusion.wu.refs_3_
  332.7 9.9 %all-gather.9.cloned.1.call-done.wg.refs_2_ = bf16[2048,704]{1,0:T(8,128)(2,1)} async-done(((bf16[512,704]{1,0:T(8,128)(2,1)}), bf16[2048,704]{1,0:T(8,128)(2,1)}) %all-gather.9.cloned.1.call-update) | async-done | bytes 2883600 | tf_op jit(solution)/shard_map/all_gather | solution.py:466
  342.6 24.3 %ffn.1 = (bf16[2048,2048]{1,0:T(8,128)(2,1)}, bf16[2048,704]{1,0:T(8,128)(2,1)}, bf16[2048,704]{1,0:T(8,128)(2,1)}, bf16[2048,704]{1,0:T(8,128)(2,1)}, f32[2048,1]{1,0:T(8,128)}, /*index=5*/f32[2048,1]{1,0:T(8,128)}) custom-call(s32[2]{0:T(128)} %pad_add_fusion.ids, bf16[8,2048,256]{2,1,0:T(8,128)(2,1)} %get-tuple-element.84.xs, ...), custom_call_target="tpu_custom_call" | custom-call | flops 11811160064 | bytes 36986880 | tf_op jit(solution)/shard_map/ffn/pallas_call | solution.py:491
  366.9 1.6 reduce
  368.5 1.2 collective-permute-done.3
  369.7 10.9 %convolution_convert_fusion.2 = bf16[2048,704]{0,1:T(8,128)(2,1)} fusion(bf16[2048,2048]{1,0:T(8,128)(2,1)} %get-tuple-element.93, bf16[2048,704]{1,0:T(8,128)(2,1)} %get-tuple-element.94.refs_1_), kind=kOutput, calls=%fused_computation.3 | convolution fusion | flops 5907021824 | bytes 14155776 | tf_op jit(solution)/shard_map/dot_general | solution.py:1064
  380.6 10.8 %convolution_convert_fusion.3 = bf16[2048,704]{0,1:T(8,128)(2,1)} fusion(bf16[2048,2048]{1,0:T(8,128)(2,1)} %get-tuple-element.93, bf16[2048,704]{1,0:T(8,128)(2,1)} %get-tuple-element.86.refs_0_), kind=kOutput, calls=%fused_computation.4 | convolution fusion | flops 5907021824 | bytes 14155776 | tf_op jit(solution)/shard_map/dot_general | solution.py:1064
  391.5 1.5 collective-permute-start.4
  393.0 2.2 collective-permute-done.4
  395.2 10.7 %convolution_convert_fusion.1 = bf16[704,2048]{1,0:T(8,128)(2,1)} fusion(bf16[2048,704]{1,0:T(8,128)(2,1)} %get-tuple-element.95.refs_2_, bf16[2048,2048]{1,0:T(8,128)(2,1)} %get-tuple-element.96), kind=kOutput, calls=%fused_computation.2 | convolution fusion | flops 5907021824 | bytes 14155776 | tf_op jit(solution)/shard_map/dot_general | solution.py:1064
  406.0 1.5 collective-permute-start.5
  407.5 2.2 collective-permute-done.5
  410.1 1.1 multiply_multiply_fusion.1.refs_7_
  411.2 109.2 %exchange.4 = (f32[2048,256]{1,0:T(8,128)}, f32[8,1,256]{2,1,0:T(1,128)}, bf16[8,2048,256]{2,1,0:T(8,128)(2,1)}) custom-call(bf16[2048,704]{1,0:T(8,128)(2,1)} %get-tuple-element.86.refs_0_, bf16[2048,704]{1,0:T(8,128)(2,1)} %get-tuple-element.94.refs_1_, bf16[2048,704]{1,0:T(8,128)(2,1)} %all-gather.9.cloned.1.call-done.wg.refs_2_, ...), custom_call_target="tpu_custom_call" | custom-call | flops 11811160064 | bytes 25183232 | tf_op jit(solution)/shard_map/exchange/pallas_call | solution.py:980
  520.4 13.5 %back_gate.1 = (bf16[2048,2048]{1,0:T(8,128)(2,1)}, f32[2048,512]{1,0:T(8,128)}) custom-call(s32[2]{0:T(128)} %pad_add_fusion.ids, bf16[8,2048,256]{2,1,0:T(8,128)(2,1)} %get-tuple-element.98.ms, bf16[4,512,512]{2,1,0:T(8,128)(2,1)} %bitcast.139), custom_call_target="tpu_custom_call" | custom-call | flops 4294967296 | bytes 23068672 | tf_op jit(solution)/shard_map/back_gate/pallas_call | solution.py:491
  533.9 9.1 %convolution_convert_fusion.4 = bf16[512,2048]{1,0:T(8,128)(2,1)} fusion(bf16[2048,512]{1,0:T(8,128)(2,1)S(1)} %bitcast.81, bf16[2048,2048]{1,0:T(8,128)(2,1)} %get-tuple-element.100), kind=kOutput, calls=%fused_computation.6 | convolution fusion | flops 4296015872 | bytes 12582912 | tf_op jit(solution)/shard_map/dot_general | solution.py:1064
  543.1 45.5 %mixer_backward.1 = (bf16[2,1024,1536]{2,1,0:T(8,128)(2,1)}, f32[2,1024,5]{2,1,0:T(8,128)}, f32[4,256]{1,0:T(4,128)}, f32[4,256]{1,0:T(4,128)}, f32[4,512]{1,0:T(4,128)}, /*index=5*/f32[1,512]{1,0:T(1,128)}) custom-call(f32[2,1024,512]{2,1,0:T(8,128)} %bitcast.94, f32[2,1024,256]{2,1,0:T(8,128)} %bitcast.86, f32[2,1024,256]{2,1,0:T(8,128)} %bitcast.89, ...), custom_call_target="tpu_custom_call" | custom-call | tf_op jit(solution)/shard_map/mixer_backward/pallas_call | solution.py:370
  588.5 19.4 %convolution_convert_fusion = bf16[2048,1536]{1,0:T(8,128)(2,1)} fusion(bf16[2048,2048]{1,0:T(8,128)(2,1)} %get-tuple-element.114, bf16[2048,1536]{1,0:T(8,128)(2,1)} %bitcast.134), kind=kOutput, calls=%fused_computation.1 | convolution fusion | flops 12888047616 | bytes 20971520 | tf_op jit(solution)/shard_map/dot_general | solution.py:1064
  608.0 1.2 copy-done.15
  611.5 3.1 collective-permute-done.7
  614.8 4.7 convolution_bitcast_fusion
  620.7 1.1 multiply_multiply_fusion.refs_10_
  622.4 115.6 %exchange.5 = (f32[2048,256]{1,0:T(8,128)}, f32[8,1,256]{2,1,0:T(1,128)}, bf16[2048,256]{1,0:T(8,128)(2,1)}, f32[104,128]{1,0:T(8,128)}, f32[8,256]{1,0:T(8,128)}) custom-call(bf16[2048,1536]{1,0:T(8,128)(2,1)} %bitcast.135, bf16[2048,4]{1,0:T(8,128)(2,1)} %bitcast.93, bf16[2048,704]{1,0:T(8,128)(2,1)} %get-tuple-element.95.refs_2_, ...), custom_call_target="tpu_custom_call" | custom-call | flops 18824036352 | bytes 26969088 | tf_op jit(solution)/shard_map/exchange/pallas_call | solution.py:980
  739.6 1.2 slice.153
  743.3 1.3 slice.117
  744.5 1.2 slice_bitcast_fusion.1
  745.8 1.3 slice_bitcast_fusion
  747.6 2.4 convert_element_type.105
  750.0 1.3 convert_element_type.106
  751.3 2.4 convert_element_type.107
  753.8 2.2 convert_element_type.104
  756.0 3.0 slice_convert_fusion
  758.9 2.1 slice_convert_fusion.2
  762.0 1.3 copy.84
  (157 shorter events, 20.1 us)
Async XLA Ops:
  7.2 4.0 copy-start.16
  7.2 5.3 copy-start.19
  7.2 5.5 copy-start.29
  7.2 5.5 copy-start.30
  7.2 6.1 copy-start.20
  7.2 117.8 %all-gather.7.cloned.1.call-start = ((), (), s32[]{:S(2)}) async-start(), calls=%async_computation.5 | async-start | bytes 5242880 | tf_op jit(solution)/shard_map/all_gather | solution.py:466
  9.6 3.7 copy-start.26
  9.6 3.7 copy-start.27
  9.7 198.3 %all-gather.11.cloned.1.call-start = ((), (), s32[]{:S(2)}) async-start(), calls=%async_computation.12 | async-start | bytes 2621440 | tf_op jit(solution)/shard_map/all_gather | solution.py:466
  10.4 302.5 %all-gather.13.cloned.1.call-start = ((), (), s32[]{:S(2)}) async-start(), calls=%async_computation.13 | async-start | bytes 3604480 | tf_op jit(solution)/shard_map/all_gather | solution.py:466
  11.2 107.1 %copy-start.31 = (f32[2]{0:T(128)S(1)}, f32[2]{0:T(128)}, u32[]{:S(2)}) copy-start(f32[2]{0:T(128)} %param.30) | copy-start | bytes 28
  11.2 331.4 %all-gather.9.cloned.1.call-start = ((), (), s32[]{:S(2)}) async-start(), calls=%async_computation.6 | async-start | bytes 3932160 | tf_op jit(solution)/shard_map/all_gather | solution.py:466
  12.4 530.6 %reduce-scatter.8.cloned.1.call-start = ((), (), s32[]{:S(2)}) async-start(), calls=%async_computation.8 | async-start | bytes 3604480 | tf_op jit(solution)/shard_map/reduce_scatter | solution.py:469
  125.1 26.3 %copy-start.17 = (bf16[512,704]{0,1:T(8,128)(2,1)S(1)}, bf16[512,704]{0,1:T(8,128)(2,1)}, u32[]{:S(2)}) copy-start(bf16[512,704]{0,1:T(8,128)(2,1)} %param.38) | copy-start | bytes 2162692
  125.1 31.8 %copy-start.3 = (f32[4,512]{1,0:T(4,128)S(1)}, f32[4,512]{1,0:T(4,128)}, u32[]{:S(2)}) copy-start(f32[4,512]{1,0:T(4,128)} %wv.3) | copy-start | bytes 24580
  125.1 31.8 %copy-start.4 = (f32[4,256]{1,0:T(4,128)S(1)}, f32[4,256]{1,0:T(4,128)}, u32[]{:S(2)}) copy-start(f32[4,256]{1,0:T(4,128)} %wq.3) | copy-start | bytes 12292
  125.1 31.8 %copy-start.5 = (f32[4,256]{1,0:T(4,128)S(1)}, f32[4,256]{1,0:T(4,128)}, u32[]{:S(2)}) copy-start(f32[4,256]{1,0:T(4,128)} %wk.3) | copy-start | bytes 12292
  125.1 31.8 %copy-start.6 = (f32[512]{0:T(512)S(1)}, f32[512]{0:T(512)}, u32[]{:S(2)}) copy-start(f32[512]{0:T(512)} %param.34) | copy-start | bytes 6148
  151.4 176.3 %collective-permute-start = (bf16[512,704]{0,1:T(8,128)(2,1)S(1)}, bf16[512,704]{0,1:T(8,128)(2,1)S(1)}, u32[]{:S(2)}, u32[]{:S(2)}) collective-permute-start(bf16[512,704]{0,1:T(8,128)(2,1)S(1)} %copy-done.17), channel_id=1, source_target_pairs={{0,8},{8,16},{16,24},{24,0},{1,9},{9,17},{17,25},{25,1},{2,10},{10... | collective-permute-start | bytes 2162696 | tf_op jit(solution)/shard_map/ppermute | solution.py:460
  151.4 176.5 %collective-permute-start.1 = (bf16[512,704]{0,1:T(8,128)(2,1)S(1)}, bf16[512,704]{0,1:T(8,128)(2,1)}, u32[]{:S(2)}, u32[]{:S(2)}) collective-permute-start(bf16[512,704]{0,1:T(8,128)(2,1)S(1)} %copy-done.17), channel_id=1, source_target_pairs={{0,16},{8,24},{16,0},{24,8},{1,17},{9,25},{17,1},{25,9},{2,18},{10... | collective-permute-start | bytes 2162696 | tf_op jit(solution)/shard_map/ppermute | solution.py:460
  153.3 176.1 %collective-permute-start.2 = (bf16[512,704]{0,1:T(8,128)(2,1)S(1)}, bf16[512,704]{0,1:T(8,128)(2,1)}, u32[]{:S(2)}, u32[]{:S(2)}) collective-permute-start(bf16[512,704]{0,1:T(8,128)(2,1)S(1)} %copy-done.17), channel_id=1, source_target_pairs={{0,24},{8,0},{16,8},{24,16},{1,25},{9,1},{17,9},{25,17},{2,26},{10... | collective-permute-start | bytes 2162696 | tf_op jit(solution)/shard_map/ppermute | solution.py:460
  156.5 32.4 %copy-start.1 = (f32[2,16,1024]{2,1,0:T(8,128)}, f32[2,16,1024]{2,1,0:T(8,128)S(1)}, u32[]{:S(2)}) copy-start(f32[2,16,1024]{2,1,0:T(8,128)S(1)} %concatenate.48.rows) | copy-start | bytes 393220
  156.8 32.1 %copy-start = (f32[2,1024,16]{2,1,0:T(8,128)}, f32[2,1024,16]{2,1,0:T(8,128)S(1)}, u32[]{:S(2)}) copy-start(f32[2,1024,16]{2,1,0:T(8,128)S(1)} %copy.65.cols) | copy-start | bytes 393220
  189.9 1.3 copy-start.7
  368.4 1.2 collective-permute-start.3
  380.6 367.0 %reduce-scatter.12.cloned.1.call-start = ((), (), s32[]{:S(2)}) async-start(), calls=%async_computation.10 | async-start | bytes 3604480 | tf_op jit(solution)/shard_map/reduce_scatter | solution.py:469
  391.4 359.9 %reduce-scatter.14.cloned.1.call-start = ((), (), s32[]{:S(2)}) async-start(), calls=%async_computation.11 | async-start | bytes 3604480 | tf_op jit(solution)/shard_map/reduce_scatter | solution.py:469
  391.5 3.7 collective-permute-start.4
  405.9 4.2 copy-start.13
  406.0 347.8 %reduce-scatter.10.cloned.1.call-start = ((), (), s32[]{:S(2)}) async-start(), calls=%async_computation.9 | async-start | bytes 2621440 | tf_op jit(solution)/shard_map/reduce_scatter | solution.py:469
  406.0 3.7 collective-permute-start.5
  520.4 13.5 %copy-start.8 = (bf16[2,1024,512]{2,1,0:T(8,128)(2,1)S(1)}, bf16[2,1024,512]{2,1,0:T(8,128)(2,1)}, u32[]{:S(2)}) copy-start(bf16[2,1024,512]{2,1,0:T(8,128)(2,1)} %copy-done.7) | copy-start | bytes 6291460
  543.0 213.0 %reduce-scatter.6.cloned.1.call-start = ((), (), s32[]{:S(2)}) async-start(), calls=%async_computation.7 | async-start | bytes 7864320 | tf_op jit(solution)/shard_map/reduce_scatter | solution.py:469
  608.0 1.2 copy-start.15
  608.0 1.6 copy-start.21
  609.8 1.2 collective-permute-start.6
  611.0 3.7 collective-permute-start.7
  611.5 8.0 %copy-start.9 = (bf16[4,2048]{0,1:T(8,128)(2,1)}, bf16[4,2048]{0,1:T(8,128)(2,1)S(1)}, u32[]{:S(2)}) copy-start(bf16[4,2048]{0,1:T(8,128)(2,1)S(1)} %copy.74) | copy-start | bytes 49156
  614.7 4.8 copy-start.23
  614.7 4.9 copy-start.25
  614.7 4.9 copy-start.24
  614.7 4.9 copy-start.22
  614.7 4.9 copy-start.28
  614.7 6.0 copy-start.12
  614.7 5.6 collective-permute-start.8
  622.4 127.7 %copy-start.18 = (bf16[512,704]{0,1:T(8,128)(2,1)S(1)}, bf16[512,704]{0,1:T(8,128)(2,1)}, u32[]{:S(2)}) copy-start(bf16[512,704]{0,1:T(8,128)(2,1)} %reduce-scatter.8.cloned.1.call-done) | copy-start | bytes 2162692
  753.7 7.3 copy-start.14
  756.0 6.0 copy-start.11
  (2 other events, 1.8 us)
Sparse Core Ops, SparseCore 0:
  10.2 114.7 all-gather.6
  126.6 81.2 all-gather.10
  209.5 68.3 all-gather.12
  279.9 62.6 all-gather.8
  380.7 54.8 reduce-scatter.7
  437.8 56.0 reduce-scatter.11
  496.1 56.0 reduce-scatter.13
  554.5 43.7 reduce-scatter.9
  608.1 111.5 reduce-scatter.5

commit v5 on v4

--- a/solution.py
+++ b/solution.py
@@ -774,10 +774,11 @@
     if gathers:
         slots, refs = refs[0], refs[1:]
     given, refs = refs[: len(kinds)], refs[len(kinds) :]
-    near, far, far_got, pair_got, refs = *refs[:4], refs[4:]
-    far_s, far_r, pair_s, pair_r, refs = *refs[:4], refs[4:]
+    near, far, far_got, pair_got, relay_got, refs = *refs[:5], refs[5:]
+    far_s, far_r, pair_s, pair_r, relay_s, relay_r, refs = *refs[:6], refs[6:]
     if gathers:
         block, own_s, same_s, same_r, turn_s, turn_r, part_s, part_r, refs = *refs[:8], refs[8:]
+        cross_s, cross_r, refs = *refs[:2], refs[2:]
     me = lax.axis_index("col")
     partner = flip(me, 1)
     peers = [flip(me, 2 * j) for j in range(1, z.half)]
@@ -804,6 +805,20 @@
     def keep(i):
         return pltpu.make_async_copy(block.at[i], slots.at[0, rows_at(i), :], own_s.at[i])
 
+    def send_relay(n, i, side):
+        part = pl.ds(side * (tile // 2), tile // 2)
+        return remote(
+            near.at[n, i % DEEP, 3, part], relay_got.at[n, i, side], relay_s.at[n, i, side], relay_r.at[n, i, side],
+            "col", peers[side],
+        )
+
+    def send_cross(i, side):
+        part = pl.ds(pl.multiple_of(i * tile + side * (tile // 2), tile // 2), tile // 2)
+        return remote(
+            slots.at[2 + 2 * side, part, :], slots.at[6, part, :], cross_s.at[i, side], cross_r.at[i, side],
+            "col", peers[1 - side],
+        )
+
     def send_part(i):
         return remote(block.at[i], slots.at[1, rows_at(i), :], part_s.at[i], part_r.at[i], "col", partner)
 
@@ -821,10 +836,16 @@
     def sent(i):
         for n in range(len(groups)):
             send_far(n, i).wait_send()
-            for j in range(1, z.half):
+            for j in direct:
                 send_pair(n, i, j).wait_send()
-
-    lag = 4 if gathers else 3
+            for side in sides:
+                send_relay(n, i, side).wait_send()
+
+    fold = z.half == 4
+    direct = (1, 2) if fold else tuple(range(1, z.half))
+    sides = (0, 1) if fold else ()
+    late = 1 if fold else 0
+    lag = 3 + late + ((1 + late) if gathers else 0)
     loops = steps + lag - 1
     for rider in riders:
         rider.begin()
@@ -857,31 +878,56 @@
                     near[n, i % DEEP, j] = (
                         near[n, i % DEEP, j].astype(f32) + far_got[n, i, j].astype(f32)
                     ).astype(bf16)
-                    send_pair(n, i, j).start()
-
-        @pl.when((it >= 2) & (it < steps + 2))
+                    if not fold:
+                        send_pair(n, i, j).start()
+                for side in sides:
+                    send_relay(n, i, side).start()
+
+        if fold:
+            @pl.when((it >= 2) & (it < steps + 2))
+            def _():
+                i = it - 2
+                for n in range(len(groups)):
+                    for side in sides:
+                        send_relay(n, i, side).wait_recv()
+                        at = (n, i % DEEP, 2 - side, slice(side * (tile // 2), (side + 1) * (tile // 2)))
+                        near[at] = (near[at].astype(f32) + relay_got[n, i, side].astype(f32)).astype(bf16)
+                        send_pair(n, i, 2 - side).start()
+
+        @pl.when((it >= 2 + late) & (it < steps + 2 + late))
         def _():
-            i = it - 2
+            i = it - 2 - late
             for n, group in enumerate(groups):
                 total = near[n, i % DEEP, 0].astype(f32) + far_got[n, i, 0].astype(f32)
-                for j in range(1, z.half):
+                for j in direct:
                     send_pair(n, i, j).wait_recv()
                     total = total + pair_got[n, i, j - 1].astype(f32)
                 result = group[1](rows_at(i), i, total, extras[n], outs[n])
                 if gathers and n == 0:
                     block[i] = result
-                    for j in range(1, z.half):
+                    for j in direct:
                         send_same(i, j).start()
                     send_part(i).start()
                     keep(i).start()
 
         if gathers:
-            @pl.when(it >= 3)
+            @pl.when((it >= 3 + late) & (it < steps + 3 + late))
             def _():
-                i = it - 3
-                for j in range(1, z.half):
+                i = it - 3 - late
+                for j in direct:
                     send_same(i, j).wait_recv()
+                for side in sides:
+                    send_cross(i, side).start()
+                for j in direct:
                     send_turn(i, j).start()
+
+            if fold:
+                @pl.when(it >= 5)
+                def _():
+                    i = it - 5
+                    for side in sides:
+                        send_cross(i, side).wait_recv()
+                    send_turn(i, 3).start()
 
     @pl.loop(max(0, steps - DEEP), steps)
     def _(i):
@@ -892,8 +938,11 @@
         def _(i):
             keep(i).wait()
             send_part(i).wait()
+            for j in direct:
+                send_same(i, j).wait_send()
+            for side in sides:
+                send_cross(i, side).wait_send()
             for j in range(1, z.half):
-                send_same(i, j).wait_send()
                 send_turn(i, j).wait()
 
     for rider in riders:
@@ -952,13 +1001,14 @@
     specs = [vmem] * len(shapes)
     scratch = [pltpu.VMEM((count, DEEP, half, tile, block), bf16)] * 2
     scratch += [pltpu.VMEM((count, steps, half, tile, block), bf16)]
-    scratch += [pltpu.VMEM((count, steps, half - 1, tile, block), bf16)]
-    scratch += [dma((count, steps))] * 2 + [dma((count, steps, half))] * 2
+    scratch += [pltpu.VMEM((count, steps, 2 if half == 4 else half - 1, tile, block), bf16)]
+    scratch += [pltpu.VMEM((count, steps if half == 4 else 1, 2, tile // 2, block), bf16)]
+    scratch += [dma((count, steps))] * 2 + [dma((count, steps, half))] * 2 + [dma((count, steps, 2))] * 2
     if gathers:
         shapes.append(jax.ShapeDtypeStruct((z.cols, tokens, block), bf16))
         specs.append(anywhere)
         scratch += [pltpu.VMEM((steps, tile, block), bf16), dma((steps,))]
-        scratch += [dma((steps, half))] * 4 + [dma((steps,))] * 2
+        scratch += [dma((steps, half))] * 4 + [dma((steps,))] * 2 + [dma((steps, 2))] * 2
     by_row = dma((z.rows,))
     for kind, own in riders:
         operands.append(own)

time: 775 us -> 735 us (0.948)
  Pallas kernels: 587 us -> 527 us
  waiting for transfers between devices: 43.7 us -> 64.1 us
    pallas_call x3, Pallas kernels: 330 us -> 269 us  [exchange(): pl.pallas_call(functools.partial(exchange_kernel, z, (kinds, len(ys), len...]
    all_gather x4, waiting for transfers between devices: 32.6 us -> 53.2 us  [gather_rows(): return lax.all_gather(values, 'row', axis=0, tiled=True)]
  transfers between devices with their start and end apart: 18 -> 18, of which waited for: 8 -> 8; matrix products, arithmetic and copies ran while one was open for 12% -> 12% of each run, Pallas kernels for 73% -> 69%
where the time goes in v5:
time: 735 us; the launch traced here: 731 us
  Pallas kernels  527 us (72%)
  matrix products  65.5 us (9%)
  waiting for transfers between devices  64.1 us (9%)
  local copies, waits for them, and re-layouts  25.6 us (3%)
  other arithmetic  24.9 us (3%)
  between operations  14.7 us (2%)
  starting transfers between devices  8.72 us (1%)
    pallas_call x3, Pallas kernels, exchange(): pl.pallas_call(functools.partial(exchange_kernel, z, (kinds, len(ys), len...  269 us
    pallas_call x1, Pallas kernels, begin(): pl.pallas_call(functools.partial(begin_kernel, z, count), in_specs=[anywh...  102 us
    pallas_call x4, Pallas kernels, launch(): pl.pallas_call(kernel, grid_spec=pltpu.PrefetchScalarGridSpec(num_scalar_...  79.3 us
    dot_general x5, matrix products, rows_product(): lax.dot_general(first_op, second_op, (((0,), (0,)), ((), ())), preferred_...  60.9 us
    all_gather x4, waiting for transfers between devices, gather_rows(): return lax.all_gather(values, 'row', axis=0, tiled=True)  53.2 us
    pallas_call x1, Pallas kernels, mixer_backward(): pl.pallas_call(functools.partial(backward_kernel, heads, seqs), grid=(ste...  45.4 us
    pallas_call x1, Pallas kernels, mixer_forward(): pl.pallas_call(functools.partial(forward_kernel, heads, seqs), grid=(step...  32 us
  transfers between devices with their start and end apart: 18, of which 8 were waited for; matrix products, arithmetic and copies ran while one was open for 12% of the time, Pallas kernels for 69%

profile of v5, /device:TPU:0, one launch (start us, length us, event | category | flops | bytes accessed | tf_op | source)
XLA Modules:
  0.0 730.6 jit_solution(10151840640454968847)
XLA Ops:
  7.3 2.3 pad_maximum_fusion.1
  11.2 1.2 copy.66
  14.2 101.6 %begin.1 = (bf16[8,2048,256]{2,1,0:T(8,128)(2,1)}, bf16[8,2048,256]{2,1,0:T(8,128)(2,1)}, f32[8,8,256]{2,1,0:T(8,128)}, bf16[4,528,512]{2,1,0:T(8,128)(2,1)}) custom-call(bf16[2048,256]{1,0:T(8,128)(2,1)} %refs_7_.1, bf16[2048,256]{1,0:T(8,128)(2,1)} %refs_4_.1, f32[8,256]{1,0:T(8,128)} %select_maximum_fusion.refs_2_, bf16[528,512]{1,0:T(8,128)(2,1)} %copy-done.10), custom_call_target="tpu_custom_call" | custom-call | flops 1000000 | bytes 21651456 | tf_op jit(solution)/shard_map/begin/pallas_call | solution.py:1100
  119.1 6.0 all-gather.7.cloned.1.call-done.weight.refs_3_
  125.1 26.3 %project.1 = (bf16[2048,2048]{1,0:T(8,128)(2,1)}, f32[2048,1]{1,0:T(8,128)}, f32[2048,256]{1,0:T(8,128)}, f32[2048,256]{1,0:T(8,128)}, f32[2048,512]{1,0:T(8,128...) custom-call(s32[2]{0:T(128)} %pad_add_fusion.ids, bf16[8,2048,256]{2,1,0:T(8,128)(2,1)} %get-tuple-element.70.blocks, ...), custom_call_target="tpu_custom_call" | custom-call | flops 12918456320 | bytes 35766272 | tf_op jit(solution)/shard_map/project/pallas_call | solution.py:491
  151.4 1.8 collective-permute-start.1
  153.3 2.1 collective-permute-start.2
  156.9 32.0 %mixer_forward.1 = (bf16[2,1024,512]{2,1,0:T(8,128)(2,1)S(1)}, bf16[2,2,1024,128]{3,2,1,0:T(8,128)(2,1)S(1)}, bf16[2,1024,512]{2,1,0:T(8,128)(2,1)}, f32[8,2,2,128,256]{4,3,2,1,0:T(8,128)}) custom-call(f32[2,1024,256]{2,1,0:T(8,128)} %bitcast.85, f32[2,1024,256]{2,1,0:T(8,128)} %bitcast.88, f32[2,1024,512]{2,1,0:T(8,128)} %bitcast.82, ...), custom_call_target="tpu_custom_call" | custom-call | tf_op jit(solution)/shard_map/mixer_forward/pallas_call | solution.py:332
  189.9 1.3 copy-done.7
  191.2 16.7 %all-gather.11.cloned.1.call-done = bf16[2048,512]{1,0:T(8,128)(2,1)} async-done(((bf16[512,512]{1,0:T(8,128)(2,1)}), bf16[2048,512]{1,0:T(8,128)(2,1)}) %all-gather.11.cloned.1.call-update) | async-done | bytes 2097168 | tf_op jit(solution)/shard_map/all_gather | solution.py:466
  207.9 84.1 %exchange.3 = (f32[2048,256]{1,0:T(8,128)}, bf16[8,2048,256]{2,1,0:T(8,128)(2,1)}) custom-call(bf16[2048,512]{1,0:T(8,128)(2,1)} %bitcast.80, bf16[4,512,512]{2,1,0:T(8,128)(2,1)} %bitcast.138, bf16[2048,256]{1,0:T(8,128)(2,1)} %refs_7_.1, f32[1,256]{1,0:T(1,128)} %bitcast.128), custom_call_target="tpu_custom_call" | custom-call | flops 4294967296 | bytes 15729664 | tf_op jit(solution)/shard_map/exchange/pallas_call | solution.py:1030
  292.3 14.7 %inner_gradient.1 = (bf16[2048,2048]{1,0:T(8,128)(2,1)}, f32[2048,704]{1,0:T(8,128)}) custom-call(s32[2]{0:T(128)} %pad_add_fusion.ids, bf16[8,2048,256]{2,1,0:T(8,128)(2,1)} %get-tuple-element.82.ts, bf16[4,704,512]{2,1,0:T(8,128)(2,1)} %bitcast.136), custom_call_target="tpu_custom_call" | custom-call | flops 5905580032 | bytes 25427968 | tf_op jit(solution)/shard_map/inner_gradient/pallas_call | solution.py:491
  307.4 1.4 copy.69
  308.8 1.4 copy.70
  310.2 1.9 pad_maximum_fusion.wu.refs_3_
  312.0 30.5 %all-gather.9.cloned.1.call-done.wg.refs_2_ = bf16[2048,704]{1,0:T(8,128)(2,1)} async-done(((bf16[512,704]{1,0:T(8,128)(2,1)}), bf16[2048,704]{1,0:T(8,128)(2,1)}) %all-gather.9.cloned.1.call-update) | async-done | bytes 2883600 | tf_op jit(solution)/shard_map/all_gather | solution.py:466
  342.6 24.3 %ffn.1 = (bf16[2048,2048]{1,0:T(8,128)(2,1)}, bf16[2048,704]{1,0:T(8,128)(2,1)}, bf16[2048,704]{1,0:T(8,128)(2,1)}, bf16[2048,704]{1,0:T(8,128)(2,1)}, f32[2048,1]{1,0:T(8,128)}, /*index=5*/f32[2048,1]{1,0:T(8,128)}) custom-call(s32[2]{0:T(128)} %pad_add_fusion.ids, bf16[8,2048,256]{2,1,0:T(8,128)(2,1)} %get-tuple-element.84.xs, ...), custom_call_target="tpu_custom_call" | custom-call | flops 11811160064 | bytes 36986880 | tf_op jit(solution)/shard_map/ffn/pallas_call | solution.py:491
  366.9 1.6 reduce
  368.5 1.2 collective-permute-done.3
  369.7 10.9 %convolution_convert_fusion.2 = bf16[2048,704]{0,1:T(8,128)(2,1)} fusion(bf16[2048,2048]{1,0:T(8,128)(2,1)} %get-tuple-element.93, bf16[2048,704]{1,0:T(8,128)(2,1)} %get-tuple-element.94.refs_1_), kind=kOutput, calls=%fused_computation.3 | convolution fusion | flops 5907021824 | bytes 14155776 | tf_op jit(solution)/shard_map/dot_general | solution.py:1114
  380.6 10.8 %convolution_convert_fusion.3 = bf16[2048,704]{0,1:T(8,128)(2,1)} fusion(bf16[2048,2048]{1,0:T(8,128)(2,1)} %get-tuple-element.93, bf16[2048,704]{1,0:T(8,128)(2,1)} %get-tuple-element.86.refs_0_), kind=kOutput, calls=%fused_computation.4 | convolution fusion | flops 5907021824 | bytes 14155776 | tf_op jit(solution)/shard_map/dot_general | solution.py:1114
  391.5 1.5 collective-permute-start.4
  393.0 2.2 collective-permute-done.4
  395.2 10.7 %convolution_convert_fusion.1 = bf16[704,2048]{1,0:T(8,128)(2,1)} fusion(bf16[2048,704]{1,0:T(8,128)(2,1)} %get-tuple-element.95.refs_2_, bf16[2048,2048]{1,0:T(8,128)(2,1)} %get-tuple-element.96), kind=kOutput, calls=%fused_computation.2 | convolution fusion | flops 5907021824 | bytes 14155776 | tf_op jit(solution)/shard_map/dot_general | solution.py:1114
  406.0 1.5 collective-permute-start.5
  407.5 2.2 collective-permute-done.5
  410.1 1.1 multiply_multiply_fusion.1.refs_7_
  411.2 88.7 %exchange.4 = (f32[2048,256]{1,0:T(8,128)}, f32[8,1,256]{2,1,0:T(1,128)}, bf16[8,2048,256]{2,1,0:T(8,128)(2,1)}) custom-call(bf16[2048,704]{1,0:T(8,128)(2,1)} %get-tuple-element.86.refs_0_, bf16[2048,704]{1,0:T(8,128)(2,1)} %get-tuple-element.94.refs_1_, bf16[2048,704]{1,0:T(8,128)(2,1)} %all-gather.9.cloned.1.call-done.wg.refs_2_, ...), custom_call_target="tpu_custom_call" | custom-call | flops 11811160064 | bytes 25183232 | tf_op jit(solution)/shard_map/exchange/pallas_call | solution.py:1030
  499.9 14.0 %back_gate.1 = (bf16[2048,2048]{1,0:T(8,128)(2,1)}, f32[2048,512]{1,0:T(8,128)}) custom-call(s32[2]{0:T(128)} %pad_add_fusion.ids, bf16[8,2048,256]{2,1,0:T(8,128)(2,1)} %get-tuple-element.98.ms, bf16[4,512,512]{2,1,0:T(8,128)(2,1)} %bitcast.139), custom_call_target="tpu_custom_call" | custom-call | flops 4294967296 | bytes 23068672 | tf_op jit(solution)/shard_map/back_gate/pallas_call | solution.py:491
  513.8 9.1 %convolution_convert_fusion.4 = bf16[512,2048]{1,0:T(8,128)(2,1)} fusion(bf16[2048,512]{1,0:T(8,128)(2,1)S(1)} %bitcast.81, bf16[2048,2048]{1,0:T(8,128)(2,1)} %get-tuple-element.100), kind=kOutput, calls=%fused_computation.6 | convolution fusion | flops 4296015872 | bytes 12582912 | tf_op jit(solution)/shard_map/dot_general | solution.py:1114
  523.0 45.4 %mixer_backward.1 = (bf16[2,1024,1536]{2,1,0:T(8,128)(2,1)}, f32[2,1024,5]{2,1,0:T(8,128)}, f32[4,256]{1,0:T(4,128)}, f32[4,256]{1,0:T(4,128)}, f32[4,512]{1,0:T(4,128)}, /*index=5*/f32[1,512]{1,0:T(1,128)}) custom-call(f32[2,1024,512]{2,1,0:T(8,128)} %bitcast.94, f32[2,1024,256]{2,1,0:T(8,128)} %bitcast.86, f32[2,1024,256]{2,1,0:T(8,128)} %bitcast.89, ...), custom_call_target="tpu_custom_call" | custom-call | tf_op jit(solution)/shard_map/mixer_backward/pallas_call | solution.py:370
  568.4 19.4 %convolution_convert_fusion = bf16[2048,1536]{1,0:T(8,128)(2,1)} fusion(bf16[2048,2048]{1,0:T(8,128)(2,1)} %get-tuple-element.114, bf16[2048,1536]{1,0:T(8,128)(2,1)} %bitcast.134), kind=kOutput, calls=%fused_computation.1 | convolution fusion | flops 12888047616 | bytes 20971520 | tf_op jit(solution)/shard_map/dot_general | solution.py:1114
  587.9 1.2 copy-done.15
  591.6 3.0 collective-permute-done.7
  595.1 4.6 convolution_bitcast_fusion
  600.9 1.1 multiply_multiply_fusion.refs_10_
  602.6 95.9 %exchange.5 = (f32[2048,256]{1,0:T(8,128)}, f32[8,1,256]{2,1,0:T(1,128)}, bf16[2048,256]{1,0:T(8,128)(2,1)}, f32[104,128]{1,0:T(8,128)}, f32[8,256]{1,0:T(8,128)}) custom-call(bf16[2048,1536]{1,0:T(8,128)(2,1)} %bitcast.135, bf16[2048,4]{1,0:T(8,128)(2,1)} %bitcast.93, bf16[2048,704]{1,0:T(8,128)(2,1)} %get-tuple-element.95.refs_2_, ...), custom_call_target="tpu_custom_call" | custom-call | flops 18824036352 | bytes 26969088 | tf_op jit(solution)/shard_map/exchange/pallas_call | solution.py:1030
  700.1 1.2 slice.153
  703.8 1.3 slice.117
  705.1 1.2 slice_bitcast_fusion.1
  706.3 1.3 slice_bitcast_fusion
  708.2 2.4 convert_element_type.105
  710.6 1.3 convert_element_type.106
  711.9 2.4 convert_element_type.107
  714.3 2.3 convert_element_type.104
  716.5 3.0 slice_convert_fusion
  719.5 2.1 slice_convert_fusion.2
  722.5 1.3 copy.84
  (157 shorter events, 20.6 us)
Async XLA Ops:
  7.2 4.0 copy-start.16
  7.2 5.3 copy-start.19
  7.2 5.5 copy-start.29
  7.2 5.5 copy-start.30
  7.2 6.1 copy-start.20
  7.2 117.8 %all-gather.7.cloned.1.call-start = ((), (), s32[]{:S(2)}) async-start(), calls=%async_computation.5 | async-start | bytes 5242880 | tf_op jit(solution)/shard_map/all_gather | solution.py:466
  9.6 3.7 copy-start.26
  9.6 3.7 copy-start.27
  9.7 198.3 %all-gather.11.cloned.1.call-start = ((), (), s32[]{:S(2)}) async-start(), calls=%async_computation.12 | async-start | bytes 2621440 | tf_op jit(solution)/shard_map/all_gather | solution.py:466
  10.4 281.9 %all-gather.13.cloned.1.call-start = ((), (), s32[]{:S(2)}) async-start(), calls=%async_computation.13 | async-start | bytes 3604480 | tf_op jit(solution)/shard_map/all_gather | solution.py:466
  11.2 107.1 %copy-start.31 = (f32[2]{0:T(128)S(1)}, f32[2]{0:T(128)}, u32[]{:S(2)}) copy-start(f32[2]{0:T(128)} %param.30) | copy-start | bytes 28
  11.2 331.4 %all-gather.9.cloned.1.call-start = ((), (), s32[]{:S(2)}) async-start(), calls=%async_computation.6 | async-start | bytes 3932160 | tf_op jit(solution)/shard_map/all_gather | solution.py:466
  12.4 510.5 %reduce-scatter.8.cloned.1.call-start = ((), (), s32[]{:S(2)}) async-start(), calls=%async_computation.8 | async-start | bytes 3604480 | tf_op jit(solution)/shard_map/reduce_scatter | solution.py:469
  125.1 26.3 %copy-start.17 = (bf16[512,704]{0,1:T(8,128)(2,1)S(1)}, bf16[512,704]{0,1:T(8,128)(2,1)}, u32[]{:S(2)}) copy-start(bf16[512,704]{0,1:T(8,128)(2,1)} %param.38) | copy-start | bytes 2162692
  125.1 31.8 %copy-start.3 = (f32[4,512]{1,0:T(4,128)S(1)}, f32[4,512]{1,0:T(4,128)}, u32[]{:S(2)}) copy-start(f32[4,512]{1,0:T(4,128)} %wv.3) | copy-start | bytes 24580
  125.1 31.8 %copy-start.4 = (f32[4,256]{1,0:T(4,128)S(1)}, f32[4,256]{1,0:T(4,128)}, u32[]{:S(2)}) copy-start(f32[4,256]{1,0:T(4,128)} %wq.3) | copy-start | bytes 12292
  125.1 31.8 %copy-start.5 = (f32[4,256]{1,0:T(4,128)S(1)}, f32[4,256]{1,0:T(4,128)}, u32[]{:S(2)}) copy-start(f32[4,256]{1,0:T(4,128)} %wk.3) | copy-start | bytes 12292
  125.1 31.8 %copy-start.6 = (f32[512]{0:T(512)S(1)}, f32[512]{0:T(512)}, u32[]{:S(2)}) copy-start(f32[512]{0:T(512)} %param.34) | copy-start | bytes 6148
  151.4 155.7 %collective-permute-start = (bf16[512,704]{0,1:T(8,128)(2,1)S(1)}, bf16[512,704]{0,1:T(8,128)(2,1)S(1)}, u32[]{:S(2)}, u32[]{:S(2)}) collective-permute-start(bf16[512,704]{0,1:T(8,128)(2,1)S(1)} %copy-done.17), channel_id=1, source_target_pairs={{0,8},{8,16},{16,24},{24,0},{1,9},{9,17},{17,25},{25,1},{2,10},{10... | collective-permute-start | bytes 2162696 | tf_op jit(solution)/shard_map/ppermute | solution.py:460
  151.4 155.9 %collective-permute-start.1 = (bf16[512,704]{0,1:T(8,128)(2,1)S(1)}, bf16[512,704]{0,1:T(8,128)(2,1)}, u32[]{:S(2)}, u32[]{:S(2)}) collective-permute-start(bf16[512,704]{0,1:T(8,128)(2,1)S(1)} %copy-done.17), channel_id=1, source_target_pairs={{0,16},{8,24},{16,0},{24,8},{1,17},{9,25},{17,1},{25,9},{2,18},{10... | collective-permute-start | bytes 2162696 | tf_op jit(solution)/shard_map/ppermute | solution.py:460
  153.3 155.5 %collective-permute-start.2 = (bf16[512,704]{0,1:T(8,128)(2,1)S(1)}, bf16[512,704]{0,1:T(8,128)(2,1)}, u32[]{:S(2)}, u32[]{:S(2)}) collective-permute-start(bf16[512,704]{0,1:T(8,128)(2,1)S(1)} %copy-done.17), channel_id=1, source_target_pairs={{0,24},{8,0},{16,8},{24,16},{1,25},{9,1},{17,9},{25,17},{2,26},{10... | collective-permute-start | bytes 2162696 | tf_op jit(solution)/shard_map/ppermute | solution.py:460
  156.5 32.4 %copy-start.1 = (f32[2,16,1024]{2,1,0:T(8,128)}, f32[2,16,1024]{2,1,0:T(8,128)S(1)}, u32[]{:S(2)}) copy-start(f32[2,16,1024]{2,1,0:T(8,128)S(1)} %concatenate.48.rows) | copy-start | bytes 393220
  156.8 32.1 %copy-start = (f32[2,1024,16]{2,1,0:T(8,128)}, f32[2,1024,16]{2,1,0:T(8,128)S(1)}, u32[]{:S(2)}) copy-start(f32[2,1024,16]{2,1,0:T(8,128)S(1)} %copy.65.cols) | copy-start | bytes 393220
  189.9 1.3 copy-start.7
  368.4 1.2 collective-permute-start.3
  380.6 327.6 %reduce-scatter.12.cloned.1.call-start = ((), (), s32[]{:S(2)}) async-start(), calls=%async_computation.10 | async-start | bytes 3604480 | tf_op jit(solution)/shard_map/reduce_scatter | solution.py:469
  391.4 320.4 %reduce-scatter.14.cloned.1.call-start = ((), (), s32[]{:S(2)}) async-start(), calls=%async_computation.11 | async-start | bytes 3604480 | tf_op jit(solution)/shard_map/reduce_scatter | solution.py:469
  391.5 3.7 collective-permute-start.4
  405.9 4.2 copy-start.13
  406.0 308.3 %reduce-scatter.10.cloned.1.call-start = ((), (), s32[]{:S(2)}) async-start(), calls=%async_computation.9 | async-start | bytes 2621440 | tf_op jit(solution)/shard_map/reduce_scatter | solution.py:469
  406.0 3.7 collective-permute-start.5
  499.9 14.0 %copy-start.8 = (bf16[2,1024,512]{2,1,0:T(8,128)(2,1)S(1)}, bf16[2,1024,512]{2,1,0:T(8,128)(2,1)}, u32[]{:S(2)}) copy-start(bf16[2,1024,512]{2,1,0:T(8,128)(2,1)} %copy-done.7) | copy-start | bytes 6291460
  522.9 193.6 %reduce-scatter.6.cloned.1.call-start = ((), (), s32[]{:S(2)}) async-start(), calls=%async_computation.7 | async-start | bytes 7864320 | tf_op jit(solution)/shard_map/reduce_scatter | solution.py:469
  587.8 1.2 copy-start.15
  587.8 1.6 copy-start.21
  589.6 1.3 collective-permute-start.6
  591.0 3.7 collective-permute-start.7
  591.6 8.1 %copy-start.9 = (bf16[4,2048]{0,1:T(8,128)(2,1)}, bf16[4,2048]{0,1:T(8,128)(2,1)S(1)}, u32[]{:S(2)}) copy-start(bf16[4,2048]{0,1:T(8,128)(2,1)S(1)} %copy.74) | copy-start | bytes 49156
  594.6 5.1 copy-start.23
  594.6 5.1 copy-start.25
  594.6 5.1 copy-start.24
  594.6 5.1 copy-start.22
  594.6 5.2 copy-start.28
  594.7 6.3 copy-start.12
  594.7 5.9 collective-permute-start.8
  602.6 108.0 %copy-start.18 = (bf16[512,704]{0,1:T(8,128)(2,1)S(1)}, bf16[512,704]{0,1:T(8,128)(2,1)}, u32[]{:S(2)}) copy-start(bf16[512,704]{0,1:T(8,128)(2,1)} %reduce-scatter.8.cloned.1.call-done) | copy-start | bytes 2162692
  714.3 7.3 copy-start.14
  716.5 6.0 copy-start.11
  (2 other events, 1.8 us)
Sparse Core Ops, SparseCore 0:
  10.2 114.7 all-gather.6
  126.6 81.2 all-gather.10
  209.5 68.3 all-gather.12
  279.9 62.6 all-gather.8
  380.7 54.8 reduce-scatter.7
  437.7 56.0 reduce-scatter.11
  496.1 56.0 reduce-scatter.13
  554.5 43.7 reduce-scatter.9
  600.7 114.0 reduce-scatter.5

commit v6 on v5

--- a/solution.py
+++ b/solution.py
@@ -562,68 +562,70 @@
     )
 
 
-def inner_kernel(g, ids, ts, wd, tr, grad):
-    for k in g.slots:
-        tr[:, pl.ds(place(g, ids, k), g.block)] = ts[k]
-    grad[...] = dot_back(g, tr, wd)
-
-
-def inner_gradient(g, ts, wd):
-    tokens = ts.shape[1]
-    width = wd.shape[1]
-    return launch(
-        functools.partial(inner_kernel, g),
-        (tokens // TILE,),
-        g.ids,
-        [ts, wd],
-        [slots_of(g), fixed(wd)],
-        [tokens_of(D), tokens_of(width)],
-        [jax.ShapeDtypeStruct((tokens, D), bf16), jax.ShapeDtypeStruct((tokens, width), f32)],
-        [],
-        "inner_gradient",
-        2 * tokens * D * width,
-    )
-
-
-def ffn_kernel(g, ids, xs, grads, undo, wg, wu, xr, inner, dgate, dup, total, scale):
+def ffn_kernel(g, ids, xs, ts, undo, wg, wu, xr, tr, gate_out, up_out, inner, scale):
     squares = 0.0
     for k in g.slots:
         at = place(g, ids, k)
         x = xs[k]
         xr[:, pl.ds(at, g.block)] = x
+        tr[:, pl.ds(at, g.block)] = ts[k]
         v = x.astype(f32)
         squares = squares + jnp.sum(v * v * undo[:, pl.ds(at, g.block)], axis=1, keepdims=True)
     scales = lax.rsqrt(squares / D + EPSILON)
     scale[...] = scales
     gate = mm(xr[...], wg[...]) * scales
     up = ring_dot(g, ids, xr, wu) * scales
-    grad = grads[...]
-    sig = sigmoid(gate)
-    silu = gate * sig
-    inner[...] = (silu * up).astype(bf16)
-    dg = grad * up * (sig * (1.0 + gate * (1.0 - sig)))
-    du = grad * silu
-    total[...] = jnp.sum(dg * gate + du * up, axis=1, keepdims=True)
-    dgate[...] = (dg * scales).astype(bf16)
-    dup[...] = (du * scales).astype(bf16)
-
-
-def ffn(g, xs, grads, undo, wg, wu):
+    gate_out[...] = gate
+    up_out[...] = up
+    inner[...] = (gate * sigmoid(gate) * up).astype(bf16)
+
+
+def ffn(g, xs, ts, undo, wg, wu):
     tokens = xs.shape[1]
     width = wg.shape[1]
     return launch(
         functools.partial(ffn_kernel, g),
         (tokens // TILE,),
         g.ids,
-        [xs, grads, undo, wg, wu],
-        [slots_of(g), tokens_of(width)] + [fixed(w) for w in (undo, wg, wu)],
-        [tokens_of(D)] + [tokens_of(width)] * 3 + [tokens_of(1)] * 2,
-        [jax.ShapeDtypeStruct((tokens, D), bf16)]
-        + [jax.ShapeDtypeStruct((tokens, width), bf16)] * 3
-        + [jax.ShapeDtypeStruct((tokens, 1), f32)] * 2,
+        [xs, ts, undo, wg, wu],
+        [slots_of(g)] * 2 + [fixed(w) for w in (undo, wg, wu)],
+        [tokens_of(D)] * 2 + [tokens_of(width)] * 3 + [tokens_of(1)],
+        [jax.ShapeDtypeStruct((tokens, D), bf16)] * 2
+        + [jax.ShapeDtypeStruct((tokens, width), f32)] * 2
+        + [jax.ShapeDtypeStruct((tokens, width), bf16), jax.ShapeDtypeStruct((tokens, 1), f32)],
         [],
         "ffn",
         4 * tokens * D * width,
+    )
+
+
+def ffn_back_kernel(g, ids, tr, gates, ups, scale, wd, dgate, dup, total):
+    scales = scale[...]
+    grad = dot_back(g, tr, wd)
+    gate = gates[...]
+    up = ups[...]
+    sig = sigmoid(gate)
+    dg = grad * up * (sig * (1.0 + gate * (1.0 - sig)))
+    du = grad * gate * sig
+    total[...] = jnp.sum(dg * gate + du * up, axis=1, keepdims=True)
+    dgate[...] = (dg * scales).astype(bf16)
+    dup[...] = (du * scales).astype(bf16)
+
+
+def ffn_back(g, tr, gates, ups, scale, wd):
+    tokens = tr.shape[0]
+    width = gates.shape[1]
+    return launch(
+        functools.partial(ffn_back_kernel, g),
+        (tokens // TILE,),
+        g.ids,
+        [tr, gates, ups, scale, wd],
+        [tokens_of(D), tokens_of(width), tokens_of(width), tokens_of(1), fixed(wd)],
+        [tokens_of(width)] * 2 + [tokens_of(1)],
+        [jax.ShapeDtypeStruct((tokens, width), bf16)] * 2 + [jax.ShapeDtypeStruct((tokens, 1), f32)],
+        [],
+        "ffn_back",
+        2 * tokens * D * width,
     )
 
 
@@ -1190,25 +1192,24 @@
         True, 0,
     )
     undo = 1.0 / (gains[1:] * gains[1:])
-    tops = lax.optimization_barrier((tops, middle))[0]
-    tr, grad_inner = inner_gradient(g, tops, dw)
-    mids = lax.optimization_barrier((mids, grad_inner))[0]
-    xr, inner, dgate, dup, weigh, scale_ffn = ffn(g, mids, grad_inner, undo, ew, uw)
+    xr, tr, gates, ups, inner, scale_ffn = ffn(g, mids, tops, undo, ew, uw)
+    down_term = rows_product(inner, tr).astype(bf16)
+    gates, held = lax.optimization_barrier((gates, down_term))
+    dgate, dup, weigh = ffn_back(g, tr, gates, ups, scale_ffn, dw)
     weigh = weigh[:, 0]
     wide = [rows_product(xr, dgate).astype(bf16)]
     weigh = weigh + g.swap(weigh, "col", 1)
     weigh, left = lax.optimization_barrier((weigh, dup))
     wide.append(rows_product(xr, left).astype(bf16))
     weigh = weigh + g.swap(weigh, "col", 2)
-    weigh, left = lax.optimization_barrier((weigh, inner))
-    wide.append(rows_product(left, tr).astype(bf16))
     bits = 4
     while bits < g.cols:
         weigh = weigh + g.swap(weigh, "col", bits)
         bits *= 2
     weigh = scale_ffn * scale_ffn * weigh[:, None] / D
     weigh = lax.optimization_barrier((weigh, *wide))[0]
-    gate_grad, up_grad, down_grad = (g.sum_rows(w, axis) for w, axis in zip(wide, (0, 0, 1)))
+    gate_grad, up_grad = (g.sum_rows(w, 0) for w in wide)
+    down_grad = g.sum_rows(down_term, 1)
     hidden_units = dgate.shape[1]
     grad_middle, norm_sums, downs = exchange(
         z, [dgate, dup], [ew, uw],

time: 735 us -> 724 us (0.985)
  waiting for transfers between devices: 64.1 us -> 46.5 us
    all_gather x4, waiting for transfers between devices: 53.2 us -> 29.4 us  [gather_rows(): return lax.all_gather(values, 'row', axis=0, tiled=True)]
  transfers between devices with their start and end apart: 18 -> 18, of which waited for: 8 -> 9; matrix products, arithmetic and copies ran while one was open for 12% -> 13% of each run, Pallas kernels for 69% -> 71%
where the time goes in v6:
time: 724 us; the launch traced here: 718 us
  Pallas kernels  530 us (73%)
  matrix products  65.6 us (9%)
  waiting for transfers between devices  46.5 us (6%)
  local copies, waits for them, and re-layouts  26.8 us (4%)
  other arithmetic  24.9 us (3%)
  between operations  14.7 us (2%)
  starting transfers between devices  9.52 us (1%)
    pallas_call x3, Pallas kernels, exchange(): pl.pallas_call(functools.partial(exchange_kernel, z, (kinds, len(ys), len...  267 us
    pallas_call x1, Pallas kernels, begin(): pl.pallas_call(functools.partial(begin_kernel, z, count), in_specs=[anywh...  102 us
    pallas_call x4, Pallas kernels, launch(): pl.pallas_call(kernel, grid_spec=pltpu.PrefetchScalarGridSpec(num_scalar_...  84.5 us
    dot_general x5, matrix products, rows_product(): lax.dot_general(first_op, second_op, (((0,), (0,)), ((), ())), preferred_...  61 us
    pallas_call x1, Pallas kernels, mixer_backward(): pl.pallas_call(functools.partial(backward_kernel, heads, seqs), grid=(ste...  45.5 us
    pallas_call x1, Pallas kernels, mixer_forward(): pl.pallas_call(functools.partial(forward_kernel, heads, seqs), grid=(step...  32 us
    all_gather x4, waiting for transfers between devices, gather_rows(): return lax.all_gather(values, 'row', axis=0, tiled=True)  29.4 us
  transfers between devices with their start and end apart: 18, of which 9 were waited for; matrix products, arithmetic and copies ran while one was open for 13% of the time, Pallas kernels for 71%

profile of v6, /device:TPU:0, one launch (start us, length us, event | category | flops | bytes accessed | tf_op | source)
XLA Modules:
  0.0 718.5 jit_solution(13836906970051381526)
XLA Ops:
  7.3 2.3 pad_maximum_fusion.1
  10.5 1.2 copy.66
  14.2 101.6 %begin.1 = (bf16[8,2048,256]{2,1,0:T(8,128)(2,1)}, bf16[8,2048,256]{2,1,0:T(8,128)(2,1)}, f32[8,8,256]{2,1,0:T(8,128)}, bf16[4,528,512]{2,1,0:T(8,128)(2,1)}) custom-call(bf16[2048,256]{1,0:T(8,128)(2,1)} %refs_7_.1, bf16[2048,256]{1,0:T(8,128)(2,1)} %refs_4_.1, f32[8,256]{1,0:T(8,128)} %select_maximum_fusion.refs_2_, bf16[528,512]{1,0:T(8,128)(2,1)} %copy-done.11), custom_call_target="tpu_custom_call" | custom-call | flops 1000000 | bytes 21651456 | tf_op jit(solution)/shard_map/begin/pallas_call | solution.py:1102
  118.9 6.2 all-gather.7.cloned.1.call-done.weight.refs_3_
  125.1 26.3 %project.1 = (bf16[2048,2048]{1,0:T(8,128)(2,1)}, f32[2048,1]{1,0:T(8,128)}, f32[2048,256]{1,0:T(8,128)}, f32[2048,256]{1,0:T(8,128)}, f32[2048,512]{1,0:T(8,128...) custom-call(s32[2]{0:T(128)} %pad_add_fusion.ids, bf16[8,2048,256]{2,1,0:T(8,128)(2,1)} %get-tuple-element.68.blocks, ...), custom_call_target="tpu_custom_call" | custom-call | flops 12918456320 | bytes 35766272 | tf_op jit(solution)/shard_map/project/pallas_call | solution.py:491
  151.5 1.6 collective-permute-start.1
  153.2 2.2 collective-permute-start.2
  157.1 32.0 %mixer_forward.1 = (bf16[2,1024,512]{2,1,0:T(8,128)(2,1)S(1)}, bf16[2,2,1024,128]{3,2,1,0:T(8,128)(2,1)S(1)}, bf16[2,1024,512]{2,1,0:T(8,128)(2,1)}, f32[8,2,2,128,256]{4,3,2,1,0:T(8,128)}) custom-call(f32[2,1024,256]{2,1,0:T(8,128)} %bitcast.85, f32[2,1024,256]{2,1,0:T(8,128)} %bitcast.88, f32[2,1024,512]{2,1,0:T(8,128)} %bitcast.82, ...), custom_call_target="tpu_custom_call" | custom-call | tf_op jit(solution)/shard_map/mixer_forward/pallas_call | solution.py:332
  190.0 1.3 copy-done.7
  191.4 16.6 %all-gather.11.cloned.1.call-done = bf16[2048,512]{1,0:T(8,128)(2,1)} async-done(((bf16[512,512]{1,0:T(8,128)(2,1)}), bf16[2048,512]{1,0:T(8,128)(2,1)}) %all-gather.11.cloned.1.call-update) | async-done | bytes 2097168 | tf_op jit(solution)/shard_map/all_gather | solution.py:466
  207.9 84.0 %exchange.3 = (f32[2048,256]{1,0:T(8,128)}, bf16[8,2048,256]{2,1,0:T(8,128)(2,1)}) custom-call(bf16[2048,512]{1,0:T(8,128)(2,1)} %bitcast.80, bf16[4,512,512]{2,1,0:T(8,128)(2,1)} %bitcast.138, bf16[2048,256]{1,0:T(8,128)(2,1)} %refs_7_.1, f32[1,256]{1,0:T(1,128)} %bitcast.130), custom_call_target="tpu_custom_call" | custom-call | flops 4294967296 | bytes 15729664 | tf_op jit(solution)/shard_map/exchange/pallas_call | solution.py:1032
  291.9 1.4 copy.68
  293.3 1.4 copy.69
  294.7 1.4 copy.70
  296.1 2.0 pad_maximum_fusion.wu.refs_3_
  298.2 26.4 %ffn.1 = (bf16[2048,2048]{1,0:T(8,128)(2,1)}, bf16[2048,2048]{1,0:T(8,128)(2,1)}, f32[2048,704]{1,0:T(8,128)}, f32[2048,704]{1,0:T(8,128)}, bf16[2048,704]{1,0:T(8,128)(2,1)}, /*index=5*/f32[2048,1]{1,0:T(8,128)}) custom-call(s32[2]{0:T(128)} %pad_add_fusion.ids, bf16[8,2048,256]{2,1,0:T(8,128)(2,1)} %get-tuple-element.77.xs, ...), custom_call_target="tpu_custom_call" | custom-call | flops 11811160064 | bytes 53755904 | tf_op jit(solution)/shard_map/ffn/pallas_call | solution.py:491
  324.6 10.7 %convolution_convert_fusion.1 = bf16[704,2048]{1,0:T(8,128)(2,1)} fusion(bf16[2048,704]{1,0:T(8,128)(2,1)} %get-tuple-element.82.refs_2_, bf16[2048,2048]{1,0:T(8,128)(2,1)} %get-tuple-element.80.tr), kind=kOutput, calls=%fused_computation.2 | convolution fusion | flops 5907021824 | bytes 14155776 | tf_op jit(solution)/shard_map/dot_general | solution.py:1116
  335.3 6.6 all-gather.13.cloned.1.call-done
  341.9 18.3 %ffn_back.1 = (bf16[2048,704]{1,0:T(8,128)(2,1)}, bf16[2048,704]{1,0:T(8,128)(2,1)}, f32[2048,1]{1,0:T(8,128)}) custom-call(s32[2]{0:T(128)} %pad_add_fusion.ids, bf16[2048,2048]{1,0:T(8,128)(2,1)} %get-tuple-element.80.tr, f32[2048,704]{1,0:T(8,128)} %get-tuple-element.83.gates, f32[2048,704]{1,0:T(8,128)} %get-tuple-element.84.ups, ...), custom_call_target="tpu_custom_call" | custom-call | flops 5905580032 | bytes 28590080 | tf_op jit(solution)/shard_map/ffn_back/pallas_call | solution.py:491
  360.2 1.6 reduce
  361.9 1.2 collective-permute-done.3
  363.0 10.7 %convolution_convert_fusion.2 = bf16[2048,704]{0,1:T(8,128)(2,1)} fusion(bf16[2048,2048]{1,0:T(8,128)(2,1)} %get-tuple-element.91, bf16[2048,704]{1,0:T(8,128)(2,1)} %get-tuple-element.92.refs_1_), kind=kOutput, calls=%fused_computation.3 | convolution fusion | flops 5907021824 | bytes 14155776 | tf_op jit(solution)/shard_map/dot_general | solution.py:1116
  373.8 10.7 %convolution_convert_fusion.3 = bf16[2048,704]{0,1:T(8,128)(2,1)} fusion(bf16[2048,2048]{1,0:T(8,128)(2,1)} %get-tuple-element.91, bf16[2048,704]{1,0:T(8,128)(2,1)} %get-tuple-element.86.refs_0_), kind=kOutput, calls=%fused_computation.4 | convolution fusion | flops 5907021824 | bytes 14155776 | tf_op jit(solution)/shard_map/dot_general | solution.py:1116
  385.4 1.5 collective-permute-start.4
  386.9 2.2 collective-permute-done.4
  389.1 1.5 collective-permute-start.5
  390.6 2.2 collective-permute-done.5
  394.2 88.5 %exchange.4 = (f32[2048,256]{1,0:T(8,128)}, f32[8,1,256]{2,1,0:T(1,128)}, bf16[8,2048,256]{2,1,0:T(8,128)(2,1)}) custom-call(bf16[2048,704]{1,0:T(8,128)(2,1)} %get-tuple-element.86.refs_0_, bf16[2048,704]{1,0:T(8,128)(2,1)} %get-tuple-element.92.refs_1_, bf16[2048,704]{1,0:T(8,128)(2,1)} %all-gather.9.cloned.1.call-done.wg.refs_2_, ...), custom_call_target="tpu_custom_call" | custom-call | flops 11811160064 | bytes 25183232 | tf_op jit(solution)/shard_map/exchange/pallas_call | solution.py:1032
  482.8 13.5 %back_gate.1 = (bf16[2048,2048]{1,0:T(8,128)(2,1)}, f32[2048,512]{1,0:T(8,128)}) custom-call(s32[2]{0:T(128)} %pad_add_fusion.ids, bf16[8,2048,256]{2,1,0:T(8,128)(2,1)} %get-tuple-element.94.ms, bf16[4,512,512]{2,1,0:T(8,128)(2,1)} %bitcast.139), custom_call_target="tpu_custom_call" | custom-call | flops 4294967296 | bytes 23068672 | tf_op jit(solution)/shard_map/back_gate/pallas_call | solution.py:491
  496.3 9.1 %convolution_convert_fusion.4 = bf16[512,2048]{1,0:T(8,128)(2,1)} fusion(bf16[2048,512]{1,0:T(8,128)(2,1)S(1)} %bitcast.81, bf16[2048,2048]{1,0:T(8,128)(2,1)} %get-tuple-element.96), kind=kOutput, calls=%fused_computation.6 | convolution fusion | flops 4296015872 | bytes 12582912 | tf_op jit(solution)/shard_map/dot_general | solution.py:1116
  505.4 45.5 %mixer_backward.1 = (bf16[2,1024,1536]{2,1,0:T(8,128)(2,1)}, f32[2,1024,5]{2,1,0:T(8,128)}, f32[4,256]{1,0:T(4,128)}, f32[4,256]{1,0:T(4,128)}, f32[4,512]{1,0:T(4,128)}, /*index=5*/f32[1,512]{1,0:T(1,128)}) custom-call(f32[2,1024,512]{2,1,0:T(8,128)} %bitcast.94, f32[2,1024,256]{2,1,0:T(8,128)} %bitcast.86, f32[2,1024,256]{2,1,0:T(8,128)} %bitcast.89, ...), custom_call_target="tpu_custom_call" | custom-call | tf_op jit(solution)/shard_map/mixer_backward/pallas_call | solution.py:370
  550.9 19.8 %convolution_convert_fusion = bf16[2048,1536]{1,0:T(8,128)(2,1)} fusion(bf16[2048,2048]{1,0:T(8,128)(2,1)} %get-tuple-element.110, bf16[2048,1536]{1,0:T(8,128)(2,1)} %bitcast.136), kind=kOutput, calls=%fused_computation.1 | convolution fusion | flops 12888047616 | bytes 20971520 | tf_op jit(solution)/shard_map/dot_general | solution.py:1116
  570.7 1.2 copy-done.15
  574.9 2.4 collective-permute-done.7
  578.4 4.6 convolution_bitcast_fusion
  585.9 94.3 %exchange.5 = (f32[2048,256]{1,0:T(8,128)}, f32[8,1,256]{2,1,0:T(1,128)}, bf16[2048,256]{1,0:T(8,128)(2,1)}, f32[104,128]{1,0:T(8,128)}, f32[8,256]{1,0:T(8,128)}) custom-call(bf16[2048,1536]{1,0:T(8,128)(2,1)} %bitcast.137, bf16[2048,4]{1,0:T(8,128)(2,1)} %bitcast.93, bf16[2048,704]{1,0:T(8,128)(2,1)} %get-tuple-element.82.refs_2_, ...), custom_call_target="tpu_custom_call" | custom-call | flops 18824036352 | bytes 26969088 | tf_op jit(solution)/shard_map/exchange/pallas_call | solution.py:1032
  681.8 1.2 slice.153
  685.5 1.3 slice.117
  686.8 1.2 slice_bitcast_fusion.1
  688.0 1.3 slice_bitcast_fusion
  689.9 2.4 convert_element_type.105
  692.3 2.4 convert_element_type.107
  694.7 1.3 convert_element_type.106
  696.0 2.2 convert_element_type.104
  698.3 6.3 reduce-scatter.6.cloned.1.call-done
  704.6 2.8 slice_convert_fusion
  707.4 2.1 slice_convert_fusion.2
  710.5 1.3 copy.84
  (157 shorter events, 24.1 us)
Async XLA Ops:
  7.2 3.3 copy-start.16
  7.2 5.1 copy-start.19
  7.2 5.5 copy-start.29
  7.2 5.5 copy-start.30
  7.2 6.1 copy-start.20
  7.2 117.8 %all-gather.7.cloned.1.call-start = ((), (), s32[]{:S(2)}) async-start(), calls=%async_computation.5 | async-start | bytes 5242880 | tf_op jit(solution)/shard_map/all_gather | solution.py:466
  9.6 3.8 copy-start.26
  9.6 3.8 copy-start.27
  9.7 198.3 %all-gather.11.cloned.1.call-start = ((), (), s32[]{:S(2)}) async-start(), calls=%async_computation.12 | async-start | bytes 2621440 | tf_op jit(solution)/shard_map/all_gather | solution.py:466
  10.4 107.5 %copy-start.31 = (f32[2]{0:T(128)S(1)}, f32[2]{0:T(128)}, u32[]{:S(2)}) copy-start(f32[2]{0:T(128)} %param.30) | copy-start | bytes 28
  10.4 287.7 %all-gather.9.cloned.1.call-start = ((), (), s32[]{:S(2)}) async-start(), calls=%async_computation.6 | async-start | bytes 3932160 | tf_op jit(solution)/shard_map/all_gather | solution.py:466
  11.7 330.3 %all-gather.13.cloned.1.call-start = ((), (), s32[]{:S(2)}) async-start(), calls=%async_computation.13 | async-start | bytes 3604480 | tf_op jit(solution)/shard_map/all_gather | solution.py:466
  12.2 493.1 %reduce-scatter.8.cloned.1.call-start = ((), (), s32[]{:S(2)}) async-start(), calls=%async_computation.8 | async-start | bytes 3604480 | tf_op jit(solution)/shard_map/reduce_scatter | solution.py:469
  125.1 26.4 %copy-start.17 = (bf16[512,704]{0,1:T(8,128)(2,1)S(1)}, bf16[512,704]{0,1:T(8,128)(2,1)}, u32[]{:S(2)}) copy-start(bf16[512,704]{0,1:T(8,128)(2,1)} %param.38) | copy-start | bytes 2162692
  125.1 32.0 %copy-start.3 = (f32[4,512]{1,0:T(4,128)S(1)}, f32[4,512]{1,0:T(4,128)}, u32[]{:S(2)}) copy-start(f32[4,512]{1,0:T(4,128)} %wv.3) | copy-start | bytes 24580
  125.1 32.0 %copy-start.4 = (f32[4,256]{1,0:T(4,128)S(1)}, f32[4,256]{1,0:T(4,128)}, u32[]{:S(2)}) copy-start(f32[4,256]{1,0:T(4,128)} %wq.3) | copy-start | bytes 12292
  125.1 32.0 %copy-start.5 = (f32[4,256]{1,0:T(4,128)S(1)}, f32[4,256]{1,0:T(4,128)}, u32[]{:S(2)}) copy-start(f32[4,256]{1,0:T(4,128)} %wk.3) | copy-start | bytes 12292
  125.1 32.0 %copy-start.6 = (f32[512]{0:T(512)S(1)}, f32[512]{0:T(512)}, u32[]{:S(2)}) copy-start(f32[512]{0:T(512)} %param.34) | copy-start | bytes 6148
  151.4 140.5 %collective-permute-start = (bf16[512,704]{0,1:T(8,128)(2,1)S(1)}, bf16[512,704]{0,1:T(8,128)(2,1)}, u32[]{:S(2)}, u32[]{:S(2)}) collective-permute-start(bf16[512,704]{0,1:T(8,128)(2,1)S(1)} %copy-done.17), channel_id=1, source_target_pairs={{0,8},{8,16},{16,24},{24,0},{1,9},{9,17},{17,25},{25,1},{2,10},{10... | collective-permute-start | bytes 2162696 | tf_op jit(solution)/shard_map/ppermute | solution.py:460
  151.5 141.8 %collective-permute-start.1 = (bf16[512,704]{0,1:T(8,128)(2,1)S(1)}, bf16[512,704]{0,1:T(8,128)(2,1)}, u32[]{:S(2)}, u32[]{:S(2)}) collective-permute-start(bf16[512,704]{0,1:T(8,128)(2,1)S(1)} %copy-done.17), channel_id=1, source_target_pairs={{0,16},{8,24},{16,0},{24,8},{1,17},{9,25},{17,1},{25,9},{2,18},{10... | collective-permute-start | bytes 2162696 | tf_op jit(solution)/shard_map/ppermute | solution.py:460
  153.2 141.6 %collective-permute-start.2 = (bf16[512,704]{0,1:T(8,128)(2,1)S(1)}, bf16[512,704]{0,1:T(8,128)(2,1)}, u32[]{:S(2)}, u32[]{:S(2)}) collective-permute-start(bf16[512,704]{0,1:T(8,128)(2,1)S(1)} %copy-done.17), channel_id=1, source_target_pairs={{0,24},{8,0},{16,8},{24,16},{1,25},{9,1},{17,9},{25,17},{2,26},{10... | collective-permute-start | bytes 2162696 | tf_op jit(solution)/shard_map/ppermute | solution.py:460
  156.7 32.4 %copy-start.1 = (f32[2,16,1024]{2,1,0:T(8,128)}, f32[2,16,1024]{2,1,0:T(8,128)S(1)}, u32[]{:S(2)}) copy-start(f32[2,16,1024]{2,1,0:T(8,128)S(1)} %concatenate.48.rows) | copy-start | bytes 393220
  157.0 32.0 %copy-start = (f32[2,1024,16]{2,1,0:T(8,128)}, f32[2,1024,16]{2,1,0:T(8,128)S(1)}, u32[]{:S(2)}) copy-start(f32[2,1024,16]{2,1,0:T(8,128)S(1)} %copy.65.cols) | copy-start | bytes 393220
  190.0 1.3 copy-start.7
  361.8 1.2 collective-permute-start.3
  373.8 316.1 %reduce-scatter.12.cloned.1.call-start = ((), (), s32[]{:S(2)}) async-start(), calls=%async_computation.10 | async-start | bytes 3604480 | tf_op jit(solution)/shard_map/reduce_scatter | solution.py:469
  384.6 8.6 %copy-start.10 = (f32[2048,1]{1,0:T(8,128)S(1)}, f32[2048,1]{1,0:T(8,128)}, u32[]{:S(2)}) copy-start(f32[2048,1]{1,0:T(8,128)} %get-tuple-element.85.scale) | copy-start | bytes 24580
  384.6 307.7 %reduce-scatter.14.cloned.1.call-start = ((), (), s32[]{:S(2)}) async-start(), calls=%async_computation.11 | async-start | bytes 3604480 | tf_op jit(solution)/shard_map/reduce_scatter | solution.py:469
  385.4 310.7 %reduce-scatter.10.cloned.1.call-start = ((), (), s32[]{:S(2)}) async-start(), calls=%async_computation.9 | async-start | bytes 2621440 | tf_op jit(solution)/shard_map/reduce_scatter | solution.py:469
  385.4 3.7 collective-permute-start.4
  389.1 3.7 collective-permute-start.5
  482.8 13.5 %copy-start.8 = (bf16[2,1024,512]{2,1,0:T(8,128)(2,1)S(1)}, bf16[2,1024,512]{2,1,0:T(8,128)(2,1)}, u32[]{:S(2)}) copy-start(bf16[2,1024,512]{2,1,0:T(8,128)(2,1)} %copy-done.7) | copy-start | bytes 6291460
  505.4 199.2 %reduce-scatter.6.cloned.1.call-start = ((), (), s32[]{:S(2)}) async-start(), calls=%async_computation.7 | async-start | bytes 7864320 | tf_op jit(solution)/shard_map/reduce_scatter | solution.py:469
  570.7 1.2 copy-start.15
  570.7 1.6 copy-start.21
  572.5 1.2 collective-permute-start.6
  573.7 3.7 collective-permute-start.7
  574.9 8.0 %copy-start.9 = (bf16[4,2048]{0,1:T(8,128)(2,1)}, bf16[4,2048]{0,1:T(8,128)(2,1)S(1)}, u32[]{:S(2)}) copy-start(bf16[4,2048]{0,1:T(8,128)(2,1)S(1)} %copy.74) | copy-start | bytes 49156
  577.4 5.6 copy-start.23
  577.4 5.6 copy-start.25
  577.4 5.6 copy-start.24
  577.4 5.7 copy-start.22
  577.4 5.7 copy-start.28
  577.4 6.8 copy-start.13
  577.4 6.4 collective-permute-start.8
  680.2 14.5 %copy-start.18 = (bf16[512,704]{0,1:T(8,128)(2,1)S(1)}, bf16[512,704]{0,1:T(8,128)(2,1)}, u32[]{:S(2)}) copy-start(bf16[512,704]{0,1:T(8,128)(2,1)} %reduce-scatter.8.cloned.1.call-done) | copy-start | bytes 2162692
  696.0 13.5 %copy-start.14 = (bf16[2048,256]{1,0:T(8,128)(2,1)S(1)}, bf16[2048,256]{1,0:T(8,128)(2,1)}, u32[]{:S(2)}) copy-start(bf16[2048,256]{1,0:T(8,128)(2,1)} %get-tuple-element.159) | copy-start | bytes 3145732
  698.3 12.2 %copy-start.12 = (f32[2048,256]{1,0:T(8,128)S(1)}, f32[2048,256]{1,0:T(8,128)}, u32[]{:S(2)}) copy-start(f32[2048,256]{1,0:T(8,128)} %get-tuple-element.160) | copy-start | bytes 6291460
  (2 other events, 1.8 us)
Sparse Core Ops, SparseCore 0:
  10.2 114.8 all-gather.6
  126.6 81.2 all-gather.10
  210.1 71.9 all-gather.8
  283.5 58.3 all-gather.12
  373.9 54.8 reduce-scatter.7
  431.0 56.0 reduce-scatter.11
  489.4 56.0 reduce-scatter.13
  547.7 43.7 reduce-scatter.9
  593.9 110.6 reduce-scatter.5
